TPU v7x, 32 devices: a whole 2x2x4 slice. The times are simulated.
32 devices in a mesh: groups: 2 (over y), site: 4 (over z), sample: 4 (over x, core).
Axes of the slice: x: 2, y: 2, z: 4, core: 2. Of those that a mesh axis runs over, the one named last changes fastest.
Arguments:
- site_tensor: bfloat16 [8, 2048, 2, 2048], P(('groups', 'site'), None, None, 'sample'), parts along dimension 0, may hold values from -0.25 to 0.25
- fronts_in: bfloat16 [3072, 2048], P(('groups', 'sample')), parts along dimension 0
- outcomes: int32 [8, 1536], P(('groups', 'site'), 'sample'), parts along dimension 0, may hold values from 0 to 1
- charges: int32 [10, 16], P('groups'), parts along dimension 0, may hold values from 0 to 3
Outputs:
- fronts_out: bfloat16 [8, 1536, 2048], P(('groups', 'site'), 'sample'), parts along dimension 0
- log_steps: float32 [8, 1536], P(('groups', 'site'), 'sample'), parts along dimension 0
There are 2 independent parts, one for each index of `groups`. A program takes and returns all parts, laid end to end along the dimension named above; each array names one. Nothing has to cross between parts.
All inputs are finite; a program needn't handle non-finite values.
Results may differ from a plain program's by a relative error of at most 0.012.
Values may be sent and summed in bfloat16 or wider, within the bound.
No kernel may reach another device: no remote copies, remote signals or barrier semaphores. Data moves between devices by JAX's collectives and lax.ppermute only.
A program may use at most 128 MiB of HBM per device.

v0:
```python
import jax
import jax.numpy as jnp
from jax import lax
from jax.sharding import PartitionSpec as P

BLOCK = 128
CHARGES = 4


epsilon = 1e-06


def shifted(array, axis, by):
    count = lax.axis_size(axis)
    pairs = [(i, i + by) for i in range(count) if 0 <= i + by < count]
    return lax.ppermute(array, axis, pairs)


def block_mask(left_charge, right_charge):
    phases = jnp.arange(2, dtype=jnp.int32)
    return (
        right_charge[None, None, :]
        == (left_charge[:, None, None] + phases[None, :, None]) % CHARGES
    )


def per_device(site_tensor, fronts_in, outcomes, charges):
    owner_idx = lax.axis_index("site")
    site_count = lax.axis_size("site")
    left_charge = lax.dynamic_index_in_dim(charges, owner_idx, 0, keepdims=False)
    right_charge = lax.dynamic_index_in_dim(charges, owner_idx + 1, 0, keepdims=False)
    micro_count = 8
    sections = micro_count + site_count - 1
    row_count = fronts_in.shape[0]
    gathered = lax.all_gather(site_tensor, "sample", axis=3, tiled=True)[0]
    bond_width = gathered.shape[0]
    blocks = bond_width // BLOCK
    allowed = block_mask(left_charge, right_charge).astype(gathered.dtype)
    masked = (
        gathered.reshape(blocks, BLOCK, 2, blocks, BLOCK) * allowed[:, None, :, :, None]
    ).reshape(bond_width, 2 * bond_width)
    micro_rows = row_count // micro_count
    picks_all = outcomes[0]

    def advance(front_rows, picks):
        products = jnp.dot(front_rows, masked, preferred_element_type=jnp.float32).reshape(
            micro_rows, 2, bond_width
        )
        chosen = jnp.where(picks[:, None] == 1, products[:, 1], products[:, 0])
        row_norm = jnp.sqrt(jnp.mean(chosen * chosen, axis=1) + epsilon)
        return ((chosen / row_norm[:, None]).astype(jnp.bfloat16), jnp.log(row_norm))

    def skipped(front_rows, picks):
        return (front_rows, jnp.zeros((micro_rows,), jnp.float32))

    def section(section_idx, loop_state):
        received, out_fronts, out_logs = loop_state
        micro_idx = section_idx - owner_idx
        active = (micro_idx >= 0) & (micro_idx < micro_count)
        row_start = jnp.clip(micro_idx, 0, micro_count - 1) * micro_rows
        first_rows = lax.dynamic_slice_in_dim(fronts_in, row_start, micro_rows, 0)
        incoming = jnp.where(owner_idx == 0, first_rows, received)
        picks = lax.dynamic_slice_in_dim(picks_all, row_start, micro_rows, 0)
        new_front, log_norm = lax.cond(active, advance, skipped, incoming, picks)
        old_front = lax.dynamic_slice_in_dim(out_fronts, row_start, micro_rows, 0)
        old_logs = lax.dynamic_slice_in_dim(out_logs, row_start, micro_rows, 0)
        out_fronts = lax.dynamic_update_slice_in_dim(
            out_fronts, jnp.where(active, new_front, old_front), row_start, 0
        )
        out_logs = lax.dynamic_update_slice_in_dim(
            out_logs, jnp.where(active, log_norm, old_logs), row_start, 0
        )
        passed = shifted(new_front, "site", 1)
        return (passed, out_fronts, out_logs)

    initial = (
        jnp.zeros((micro_rows, bond_width), jnp.bfloat16),
        jnp.zeros((row_count, bond_width), jnp.bfloat16),
        jnp.zeros((row_count,), jnp.float32),
    )
    final_state = lax.fori_loop(0, sections, section, initial)
    return (final_state[1][None], final_state[2][None])


def solution(mesh):
    in_specs = (
        P(("groups", "site"), None, None, "sample"),
        P(("groups", "sample"), None),
        P(("groups", "site"), "sample"),
        P("groups", None),
    )
    out_specs = (P(("groups", "site"), "sample", None), P(("groups", "site"), "sample"))
    return jax.shard_map(
        per_device, mesh=mesh, in_specs=in_specs, out_specs=out_specs, check_vma=False
    )
```

profile of v0, /device:TPU:24, one launch (start us, length us, event | category | flops | bytes accessed | tf_op | source)
XLA Modules:
  0.0 360.7 jit_solution(17284264981978438301)
XLA Ops:
  8.9 6.1 %mul.22 = bf16[16,128,2,16,128]{4,3,2,1,0:T(8,128)(2,1)} broadcast(bf16[16,2,16]{2,1,0:T(2,128)(2,1)S(1)} %compare_convert_fusion), dimensions={0,2,3} | broadcast | bytes 16778240 | tf_op jit(solution)/shard_map/mul | solution.py:40
  15.0 26.2 %mul.23 = bf16[2048,4096]{1,0:T(8,128)(2,1)} reshape(bf16[16,128,2,16,128]{4,3,2,1,0:T(8,128)(2,1)} %mul.22) | data formatting | bytes 33554432 | tf_op jit(solution)/shard_map/mul | solution.py:40
  41.1 77.5 %all-gather.2.cloned.1.call-done = bf16[1,2048,2,2048]{3,2,1,0:T(2,128)(2,1)} async-done(((bf16[1,2048,2,512]{3,2,1,0:T(2,128)(2,1)}), bf16[1,2048,2,2048]{3,2,1,0:T(2,128)(2,1)}) %all-gather.2.cloned.1.call-update) | async-done | bytes 16777232 | tf_op jit(solution)/shard_map/all_gather | solution.py:35
  118.7 13.1 %copy.10 = bf16[256,8,2,2048]{3,1,2,0:T(8,128)(2,1)S(1)} copy(bf16[256,8,2,2048]{3,2,1,0:T(2,128)(2,1)} %bitcast.29) | data formatting | bytes 33554432
  131.8 9.3 %mul.24 = bf16[2048,4096]{1,0:T(8,128)(2,1)} multiply(bf16[2048,4096]{1,0:T(8,128)(2,1)S(1)} %bitcast.28, bf16[2048,4096]{1,0:T(8,128)(2,1)S(1)} %copy-done) | non-fusion elementwise | flops 8388608 | bytes 50331648 | tf_op jit(solution)/shard_map/mul | solution.py:40
  141.3 211.4 %while.18 = (s32[]{:T(128)}, bf16[48,2048]{1,0:T(8,128)(2,1)S(1)}, bf16[384,2048]{1,0:T(8,128)(2,1)S(1)}, f32[384]{0:T(512)S(1)}, s32[]{:T(128)}, /*index=5*/pre...) while((s32[]{:T(128)}, bf16[48,2048]{1,0:T(8,128)(2,1)S(1)}, ...), condition=%wide.region_4.5_spmd, body=%wide.region_0.4_spmd.sunk | while | flops 806092992 | bytes 24644720 | solution.py:81
  141.4 1.0 dynamic-slice_select_fusion.2
  142.4 1.3 collective-permute-start
  143.9 7.4 %collective-permute-done = bf16[48,2048]{1,0:T(8,128)(2,1)S(1)} collective-permute-done((bf16[48,2048]{1,0:T(8,128)(2,1)S(1)}, bf16[48,2048]{1,0:T(8,128)(2,1)S(1)}, u32[]{:S(2)}, u32[]{:S(2)}) %collective-permute-start) | collective-permute-done | bytes 196640 | tf_op jit(solution)/shard_map/while/body/eval_jaxpr/ppermute | solution.py:16
  151.3 1.0 dynamic-slice_select_fusion.2
  152.4 1.3 collective-permute-start
  153.9 6.6 %collective-permute-done = bf16[48,2048]{1,0:T(8,128)(2,1)S(1)} collective-permute-done((bf16[48,2048]{1,0:T(8,128)(2,1)S(1)}, bf16[48,2048]{1,0:T(8,128)(2,1)S(1)}, u32[]{:S(2)}, u32[]{:S(2)}) %collective-permute-start) | collective-permute-done | bytes 196640 | tf_op jit(solution)/shard_map/while/body/eval_jaxpr/ppermute | solution.py:16
  160.4 1.0 dynamic-slice_select_fusion.2
  161.5 1.3 collective-permute-start
  163.0 34.7 %collective-permute-done = bf16[48,2048]{1,0:T(8,128)(2,1)S(1)} collective-permute-done((bf16[48,2048]{1,0:T(8,128)(2,1)S(1)}, bf16[48,2048]{1,0:T(8,128)(2,1)S(1)}, u32[]{:S(2)}, u32[]{:S(2)}) %collective-permute-start) | collective-permute-done | bytes 196640 | tf_op jit(solution)/shard_map/while/body/eval_jaxpr/ppermute | solution.py:16
  197.7 1.0 dynamic-slice_select_fusion.2
  198.7 10.8 %conditional.2 = (bf16[48,2048]{1,0:T(8,128)(2,1)S(1)}, f32[48]{0:T(128)S(1)}) conditional(s32[]{:T(128)} %convert_element_type.22, bf16[48,2048]{1,0:T(8,128)(2,1)S(1)} %dynamic-slice_select_fusion.2, (s32[384]{0:T(512)S(1)}, s32[]{:T(128)}, bf16[48,2048]{1,0:T(8,128)(2,1)S(1)}, bf16[2048,4096]{1,0:T(8,128)(2,1)}) %tuple.53), branch_computations={%region_1.1_spmd, %region_2.3_spmd} | conditional | flops 805896320 | bytes 22676772 | solution.py:64
  198.7 8.8 %fusion.8 = f32[48,4096]{1,0:T(8,128)S(1)} fusion(bf16[48,2048]{1,0:T(8,128)(2,1)S(1)} %get-tuple-element.177, bf16[2048,4096]{1,0:T(8,128)(2,1)} %get-tuple-element.178), kind=kOutput, calls=%fused_computation.24 | convolution fusion | flops 805306368 | bytes 17760256 | tf_op jit(solution)/shard_map/while/body/eval_jaxpr/cond/branch_1_fun/dot_general | solution.py:46
  209.5 1.3 collective-permute-start
  211.1 6.0 %collective-permute-done = bf16[48,2048]{1,0:T(8,128)(2,1)S(1)} collective-permute-done((bf16[48,2048]{1,0:T(8,128)(2,1)S(1)}, bf16[48,2048]{1,0:T(8,128)(2,1)S(1)}, u32[]{:S(2)}, u32[]{:S(2)}) %collective-permute-start) | collective-permute-done | bytes 196640 | tf_op jit(solution)/shard_map/while/body/eval_jaxpr/ppermute | solution.py:16
  218.1 10.8 %conditional.2 = (bf16[48,2048]{1,0:T(8,128)(2,1)S(1)}, f32[48]{0:T(128)S(1)}) conditional(s32[]{:T(128)} %convert_element_type.22, bf16[48,2048]{1,0:T(8,128)(2,1)S(1)} %dynamic-slice_select_fusion.2, (s32[384]{0:T(512)S(1)}, s32[]{:T(128)}, bf16[48,2048]{1,0:T(8,128)(2,1)S(1)}, bf16[2048,4096]{1,0:T(8,128)(2,1)}) %tuple.53), branch_computations={%region_1.1_spmd, %region_2.3_spmd} | conditional | flops 805896320 | bytes 22676772 | solution.py:64
  218.1 8.8 %fusion.8 = f32[48,4096]{1,0:T(8,128)S(1)} fusion(bf16[48,2048]{1,0:T(8,128)(2,1)S(1)} %get-tuple-element.177, bf16[2048,4096]{1,0:T(8,128)(2,1)} %get-tuple-element.178), kind=kOutput, calls=%fused_computation.24 | convolution fusion | flops 805306368 | bytes 17760256 | tf_op jit(solution)/shard_map/while/body/eval_jaxpr/cond/branch_1_fun/dot_general | solution.py:46
  228.9 1.3 collective-permute-start
  230.4 6.0 %collective-permute-done = bf16[48,2048]{1,0:T(8,128)(2,1)S(1)} collective-permute-done((bf16[48,2048]{1,0:T(8,128)(2,1)S(1)}, bf16[48,2048]{1,0:T(8,128)(2,1)S(1)}, u32[]{:S(2)}, u32[]{:S(2)}) %collective-permute-start) | collective-permute-done | bytes 196640 | tf_op jit(solution)/shard_map/while/body/eval_jaxpr/ppermute | solution.py:16
  237.5 10.8 %conditional.2 = (bf16[48,2048]{1,0:T(8,128)(2,1)S(1)}, f32[48]{0:T(128)S(1)}) conditional(s32[]{:T(128)} %convert_element_type.22, bf16[48,2048]{1,0:T(8,128)(2,1)S(1)} %dynamic-slice_select_fusion.2, (s32[384]{0:T(512)S(1)}, s32[]{:T(128)}, bf16[48,2048]{1,0:T(8,128)(2,1)S(1)}, bf16[2048,4096]{1,0:T(8,128)(2,1)}) %tuple.53), branch_computations={%region_1.1_spmd, %region_2.3_spmd} | conditional | flops 805896320 | bytes 22676772 | solution.py:64
  237.5 8.8 %fusion.8 = f32[48,4096]{1,0:T(8,128)S(1)} fusion(bf16[48,2048]{1,0:T(8,128)(2,1)S(1)} %get-tuple-element.177, bf16[2048,4096]{1,0:T(8,128)(2,1)} %get-tuple-element.178), kind=kOutput, calls=%fused_computation.24 | convolution fusion | flops 805306368 | bytes 17760256 | tf_op jit(solution)/shard_map/while/body/eval_jaxpr/cond/branch_1_fun/dot_general | solution.py:46
  248.3 1.3 collective-permute-start
  249.8 6.0 %collective-permute-done = bf16[48,2048]{1,0:T(8,128)(2,1)S(1)} collective-permute-done((bf16[48,2048]{1,0:T(8,128)(2,1)S(1)}, bf16[48,2048]{1,0:T(8,128)(2,1)S(1)}, u32[]{:S(2)}, u32[]{:S(2)}) %collective-permute-start) | collective-permute-done | bytes 196640 | tf_op jit(solution)/shard_map/while/body/eval_jaxpr/ppermute | solution.py:16
  256.8 10.8 %conditional.2 = (bf16[48,2048]{1,0:T(8,128)(2,1)S(1)}, f32[48]{0:T(128)S(1)}) conditional(s32[]{:T(128)} %convert_element_type.22, bf16[48,2048]{1,0:T(8,128)(2,1)S(1)} %dynamic-slice_select_fusion.2, (s32[384]{0:T(512)S(1)}, s32[]{:T(128)}, bf16[48,2048]{1,0:T(8,128)(2,1)S(1)}, bf16[2048,4096]{1,0:T(8,128)(2,1)}) %tuple.53), branch_computations={%region_1.1_spmd, %region_2.3_spmd} | conditional | flops 805896320 | bytes 22676772 | solution.py:64
  256.8 8.8 %fusion.8 = f32[48,4096]{1,0:T(8,128)S(1)} fusion(bf16[48,2048]{1,0:T(8,128)(2,1)S(1)} %get-tuple-element.177, bf16[2048,4096]{1,0:T(8,128)(2,1)} %get-tuple-element.178), kind=kOutput, calls=%fused_computation.24 | convolution fusion | flops 805306368 | bytes 17760256 | tf_op jit(solution)/shard_map/while/body/eval_jaxpr/cond/branch_1_fun/dot_general | solution.py:46
  267.7 1.3 collective-permute-start
  269.2 6.0 %collective-permute-done = bf16[48,2048]{1,0:T(8,128)(2,1)S(1)} collective-permute-done((bf16[48,2048]{1,0:T(8,128)(2,1)S(1)}, bf16[48,2048]{1,0:T(8,128)(2,1)S(1)}, u32[]{:S(2)}, u32[]{:S(2)}) %collective-permute-start) | collective-permute-done | bytes 196640 | tf_op jit(solution)/shard_map/while/body/eval_jaxpr/ppermute | solution.py:16
  276.2 10.8 %conditional.2 = (bf16[48,2048]{1,0:T(8,128)(2,1)S(1)}, f32[48]{0:T(128)S(1)}) conditional(s32[]{:T(128)} %convert_element_type.22, bf16[48,2048]{1,0:T(8,128)(2,1)S(1)} %dynamic-slice_select_fusion.2, (s32[384]{0:T(512)S(1)}, s32[]{:T(128)}, bf16[48,2048]{1,0:T(8,128)(2,1)S(1)}, bf16[2048,4096]{1,0:T(8,128)(2,1)}) %tuple.53), branch_computations={%region_1.1_spmd, %region_2.3_spmd} | conditional | flops 805896320 | bytes 22676772 | solution.py:64
  276.2 8.8 %fusion.8 = f32[48,4096]{1,0:T(8,128)S(1)} fusion(bf16[48,2048]{1,0:T(8,128)(2,1)S(1)} %get-tuple-element.177, bf16[2048,4096]{1,0:T(8,128)(2,1)} %get-tuple-element.178), kind=kOutput, calls=%fused_computation.24 | convolution fusion | flops 805306368 | bytes 17760256 | tf_op jit(solution)/shard_map/while/body/eval_jaxpr/cond/branch_1_fun/dot_general | solution.py:46
  287.0 1.3 collective-permute-start
  288.6 6.0 %collective-permute-done = bf16[48,2048]{1,0:T(8,128)(2,1)S(1)} collective-permute-done((bf16[48,2048]{1,0:T(8,128)(2,1)S(1)}, bf16[48,2048]{1,0:T(8,128)(2,1)S(1)}, u32[]{:S(2)}, u32[]{:S(2)}) %collective-permute-start) | collective-permute-done | bytes 196640 | tf_op jit(solution)/shard_map/while/body/eval_jaxpr/ppermute | solution.py:16
  295.6 10.8 %conditional.2 = (bf16[48,2048]{1,0:T(8,128)(2,1)S(1)}, f32[48]{0:T(128)S(1)}) conditional(s32[]{:T(128)} %convert_element_type.22, bf16[48,2048]{1,0:T(8,128)(2,1)S(1)} %dynamic-slice_select_fusion.2, (s32[384]{0:T(512)S(1)}, s32[]{:T(128)}, bf16[48,2048]{1,0:T(8,128)(2,1)S(1)}, bf16[2048,4096]{1,0:T(8,128)(2,1)}) %tuple.53), branch_computations={%region_1.1_spmd, %region_2.3_spmd} | conditional | flops 805896320 | bytes 22676772 | solution.py:64
  295.6 8.8 %fusion.8 = f32[48,4096]{1,0:T(8,128)S(1)} fusion(bf16[48,2048]{1,0:T(8,128)(2,1)S(1)} %get-tuple-element.177, bf16[2048,4096]{1,0:T(8,128)(2,1)} %get-tuple-element.178), kind=kOutput, calls=%fused_computation.24 | convolution fusion | flops 805306368 | bytes 17760256 | tf_op jit(solution)/shard_map/while/body/eval_jaxpr/cond/branch_1_fun/dot_general | solution.py:46
  306.4 1.3 collective-permute-start
  307.9 6.0 %collective-permute-done = bf16[48,2048]{1,0:T(8,128)(2,1)S(1)} collective-permute-done((bf16[48,2048]{1,0:T(8,128)(2,1)S(1)}, bf16[48,2048]{1,0:T(8,128)(2,1)S(1)}, u32[]{:S(2)}, u32[]{:S(2)}) %collective-permute-start) | collective-permute-done | bytes 196640 | tf_op jit(solution)/shard_map/while/body/eval_jaxpr/ppermute | solution.py:16
  315.0 10.8 %conditional.2 = (bf16[48,2048]{1,0:T(8,128)(2,1)S(1)}, f32[48]{0:T(128)S(1)}) conditional(s32[]{:T(128)} %convert_element_type.22, bf16[48,2048]{1,0:T(8,128)(2,1)S(1)} %dynamic-slice_select_fusion.2, (s32[384]{0:T(512)S(1)}, s32[]{:T(128)}, bf16[48,2048]{1,0:T(8,128)(2,1)S(1)}, bf16[2048,4096]{1,0:T(8,128)(2,1)}) %tuple.53), branch_computations={%region_1.1_spmd, %region_2.3_spmd} | conditional | flops 805896320 | bytes 22676772 | solution.py:64
  315.0 8.8 %fusion.8 = f32[48,4096]{1,0:T(8,128)S(1)} fusion(bf16[48,2048]{1,0:T(8,128)(2,1)S(1)} %get-tuple-element.177, bf16[2048,4096]{1,0:T(8,128)(2,1)} %get-tuple-element.178), kind=kOutput, calls=%fused_computation.24 | convolution fusion | flops 805306368 | bytes 17760256 | tf_op jit(solution)/shard_map/while/body/eval_jaxpr/cond/branch_1_fun/dot_general | solution.py:46
  325.8 1.3 collective-permute-start
  327.3 6.0 %collective-permute-done = bf16[48,2048]{1,0:T(8,128)(2,1)S(1)} collective-permute-done((bf16[48,2048]{1,0:T(8,128)(2,1)S(1)}, bf16[48,2048]{1,0:T(8,128)(2,1)S(1)}, u32[]{:S(2)}, u32[]{:S(2)}) %collective-permute-start) | collective-permute-done | bytes 196640 | tf_op jit(solution)/shard_map/while/body/eval_jaxpr/ppermute | solution.py:16
  334.3 10.8 %conditional.2 = (bf16[48,2048]{1,0:T(8,128)(2,1)S(1)}, f32[48]{0:T(128)S(1)}) conditional(s32[]{:T(128)} %convert_element_type.22, bf16[48,2048]{1,0:T(8,128)(2,1)S(1)} %dynamic-slice_select_fusion.2, (s32[384]{0:T(512)S(1)}, s32[]{:T(128)}, bf16[48,2048]{1,0:T(8,128)(2,1)S(1)}, bf16[2048,4096]{1,0:T(8,128)(2,1)}) %tuple.53), branch_computations={%region_1.1_spmd, %region_2.3_spmd} | conditional | flops 805896320 | bytes 22676772 | solution.py:64
  334.3 8.8 %fusion.8 = f32[48,4096]{1,0:T(8,128)S(1)} fusion(bf16[48,2048]{1,0:T(8,128)(2,1)S(1)} %get-tuple-element.177, bf16[2048,4096]{1,0:T(8,128)(2,1)} %get-tuple-element.178), kind=kOutput, calls=%fused_computation.24 | convolution fusion | flops 805306368 | bytes 17760256 | tf_op jit(solution)/shard_map/while/body/eval_jaxpr/cond/branch_1_fun/dot_general | solution.py:46
  345.2 1.3 collective-permute-start
  346.7 6.0 %collective-permute-done = bf16[48,2048]{1,0:T(8,128)(2,1)S(1)} collective-permute-done((bf16[48,2048]{1,0:T(8,128)(2,1)S(1)}, bf16[48,2048]{1,0:T(8,128)(2,1)S(1)}, u32[]{:S(2)}, u32[]{:S(2)}) %collective-permute-start) | collective-permute-done | bytes 196640 | tf_op jit(solution)/shard_map/while/body/eval_jaxpr/ppermute | solution.py:16
  (99 shorter events, 28.4 us)
Async XLA Ops:
  7.2 111.5 %all-gather.2.cloned.1.call-start = ((), (), s32[]{:S(2)}) async-start(), calls=%async_computation | async-start | bytes 20971520 | tf_op jit(solution)/shard_map/all_gather | solution.py:35
  14.9 26.2 %copy-start.2 = (s32[1,384]{1,0:T(1,128)S(1)}, s32[1,384]{1,0:T(1,128)}, u32[]{:S(2)}) copy-start(s32[1,384]{1,0:T(1,128)} %param.10) | copy-start | bytes 4612
  118.7 13.2 %copy-start = (bf16[2048,4096]{1,0:T(8,128)(2,1)S(1)}, bf16[2048,4096]{1,0:T(8,128)(2,1)}, u32[]{:S(2)}) copy-start(bf16[2048,4096]{1,0:T(8,128)(2,1)} %mul.23) | copy-start | bytes 50331652
  142.4 9.0 %collective-permute-start = (bf16[48,2048]{1,0:T(8,128)(2,1)S(1)}, bf16[48,2048]{1,0:T(8,128)(2,1)S(1)}, u32[]{:S(2)}, u32[]{:S(2)}) collective-permute-start(bf16[48,2048]{1,0:T(8,128)(2,1)S(1)} %get-tuple-element.278), channel_id=1, source_target_pairs={{0,4},{4,8},{8,12},{1,5},{5,9},{9,13},{2,6},{6,10},{10,14},{3,7},{... | collective-permute-start | bytes 589832 | tf_op jit(solution)/shard_map/while/body/eval_jaxpr/ppermute | solution.py:16
  152.4 8.1 %collective-permute-start = (bf16[48,2048]{1,0:T(8,128)(2,1)S(1)}, bf16[48,2048]{1,0:T(8,128)(2,1)S(1)}, u32[]{:S(2)}, u32[]{:S(2)}) collective-permute-start(bf16[48,2048]{1,0:T(8,128)(2,1)S(1)} %get-tuple-element.278), channel_id=1, source_target_pairs={{0,4},{4,8},{8,12},{1,5},{5,9},{9,13},{2,6},{6,10},{10,14},{3,7},{... | collective-permute-start | bytes 589832 | tf_op jit(solution)/shard_map/while/body/eval_jaxpr/ppermute | solution.py:16
  161.5 36.3 %collective-permute-start = (bf16[48,2048]{1,0:T(8,128)(2,1)S(1)}, bf16[48,2048]{1,0:T(8,128)(2,1)S(1)}, u32[]{:S(2)}, u32[]{:S(2)}) collective-permute-start(bf16[48,2048]{1,0:T(8,128)(2,1)S(1)} %get-tuple-element.278), channel_id=1, source_target_pairs={{0,4},{4,8},{8,12},{1,5},{5,9},{9,13},{2,6},{6,10},{10,14},{3,7},{... | collective-permute-start | bytes 589832 | tf_op jit(solution)/shard_map/while/body/eval_jaxpr/ppermute | solution.py:16
  209.5 7.6 %collective-permute-start = (bf16[48,2048]{1,0:T(8,128)(2,1)S(1)}, bf16[48,2048]{1,0:T(8,128)(2,1)S(1)}, u32[]{:S(2)}, u32[]{:S(2)}) collective-permute-start(bf16[48,2048]{1,0:T(8,128)(2,1)S(1)} %get-tuple-element.278), channel_id=1, source_target_pairs={{0,4},{4,8},{8,12},{1,5},{5,9},{9,13},{2,6},{6,10},{10,14},{3,7},{... | collective-permute-start | bytes 589832 | tf_op jit(solution)/shard_map/while/body/eval_jaxpr/ppermute | solution.py:16
  228.9 7.6 %collective-permute-start = (bf16[48,2048]{1,0:T(8,128)(2,1)S(1)}, bf16[48,2048]{1,0:T(8,128)(2,1)S(1)}, u32[]{:S(2)}, u32[]{:S(2)}) collective-permute-start(bf16[48,2048]{1,0:T(8,128)(2,1)S(1)} %get-tuple-element.278), channel_id=1, source_target_pairs={{0,4},{4,8},{8,12},{1,5},{5,9},{9,13},{2,6},{6,10},{10,14},{3,7},{... | collective-permute-start | bytes 589832 | tf_op jit(solution)/shard_map/while/body/eval_jaxpr/ppermute | solution.py:16
  248.3 7.6 %collective-permute-start = (bf16[48,2048]{1,0:T(8,128)(2,1)S(1)}, bf16[48,2048]{1,0:T(8,128)(2,1)S(1)}, u32[]{:S(2)}, u32[]{:S(2)}) collective-permute-start(bf16[48,2048]{1,0:T(8,128)(2,1)S(1)} %get-tuple-element.278), channel_id=1, source_target_pairs={{0,4},{4,8},{8,12},{1,5},{5,9},{9,13},{2,6},{6,10},{10,14},{3,7},{... | collective-permute-start | bytes 589832 | tf_op jit(solution)/shard_map/while/body/eval_jaxpr/ppermute | solution.py:16
  267.7 7.6 %collective-permute-start = (bf16[48,2048]{1,0:T(8,128)(2,1)S(1)}, bf16[48,2048]{1,0:T(8,128)(2,1)S(1)}, u32[]{:S(2)}, u32[]{:S(2)}) collective-permute-start(bf16[48,2048]{1,0:T(8,128)(2,1)S(1)} %get-tuple-element.278), channel_id=1, source_target_pairs={{0,4},{4,8},{8,12},{1,5},{5,9},{9,13},{2,6},{6,10},{10,14},{3,7},{... | collective-permute-start | bytes 589832 | tf_op jit(solution)/shard_map/while/body/eval_jaxpr/ppermute | solution.py:16
  287.0 7.6 %collective-permute-start = (bf16[48,2048]{1,0:T(8,128)(2,1)S(1)}, bf16[48,2048]{1,0:T(8,128)(2,1)S(1)}, u32[]{:S(2)}, u32[]{:S(2)}) collective-permute-start(bf16[48,2048]{1,0:T(8,128)(2,1)S(1)} %get-tuple-element.278), channel_id=1, source_target_pairs={{0,4},{4,8},{8,12},{1,5},{5,9},{9,13},{2,6},{6,10},{10,14},{3,7},{... | collective-permute-start | bytes 589832 | tf_op jit(solution)/shard_map/while/body/eval_jaxpr/ppermute | solution.py:16
  306.4 7.6 %collective-permute-start = (bf16[48,2048]{1,0:T(8,128)(2,1)S(1)}, bf16[48,2048]{1,0:T(8,128)(2,1)S(1)}, u32[]{:S(2)}, u32[]{:S(2)}) collective-permute-start(bf16[48,2048]{1,0:T(8,128)(2,1)S(1)} %get-tuple-element.278), channel_id=1, source_target_pairs={{0,4},{4,8},{8,12},{1,5},{5,9},{9,13},{2,6},{6,10},{10,14},{3,7},{... | collective-permute-start | bytes 589832 | tf_op jit(solution)/shard_map/while/body/eval_jaxpr/ppermute | solution.py:16
  325.8 7.6 %collective-permute-start = (bf16[48,2048]{1,0:T(8,128)(2,1)S(1)}, bf16[48,2048]{1,0:T(8,128)(2,1)S(1)}, u32[]{:S(2)}, u32[]{:S(2)}) collective-permute-start(bf16[48,2048]{1,0:T(8,128)(2,1)S(1)} %get-tuple-element.278), channel_id=1, source_target_pairs={{0,4},{4,8},{8,12},{1,5},{5,9},{9,13},{2,6},{6,10},{10,14},{3,7},{... | collective-permute-start | bytes 589832 | tf_op jit(solution)/shard_map/while/body/eval_jaxpr/ppermute | solution.py:16
  345.2 7.6 %collective-permute-start = (bf16[48,2048]{1,0:T(8,128)(2,1)S(1)}, bf16[48,2048]{1,0:T(8,128)(2,1)S(1)}, u32[]{:S(2)}, u32[]{:S(2)}) collective-permute-start(bf16[48,2048]{1,0:T(8,128)(2,1)S(1)} %get-tuple-element.278), channel_id=1, source_target_pairs={{0,4},{4,8},{8,12},{1,5},{5,9},{9,13},{2,6},{6,10},{10,14},{3,7},{... | collective-permute-start | bytes 589832 | tf_op jit(solution)/shard_map/while/body/eval_jaxpr/ppermute | solution.py:16
  352.7 1.1 copy-start.1
Sparse Core Ops, SparseCore 0:
  9.5 109.1 all-gather.1
where the time goes:
time: 362 us; the launch traced here: 361 us
  waiting for transfers between devices  175 us (48%)
  matrix products  70.3 us (19%)
  local copies, waits for them, and re-layouts  57.7 us (16%)
  other arithmetic  28.4 us (8%)
  starting transfers between devices  14.3 us (4%)
  between operations  14.1 us (4%)
    ppermute x11, waiting for transfers between devices, shifted(): return lax.ppermute(array, axis, pairs)  96.9 us
    all_gather x1, waiting for transfers between devices, per_device(): gathered = lax.all_gather(site_tensor, 'sample', axis=3, tiled=True)[0]  77.5 us
    dot_general x8, matrix products, advance(): jnp.dot(front_rows, masked, preferred_element_type=jnp.float32)  70.3 us
    mul x2, local copies, waits for them, and re-layouts, per_device(): gathered.reshape(blocks, BLOCK, 2, blocks, BLOCK)  32.2 us
    ppermute x11, starting transfers between devices, shifted(): return lax.ppermute(array, axis, pairs)  14.2 us
    unnamed x7, local copies, waits for them, and re-layouts  13.7 us
    select_n x11, other arithmetic, section(): incoming = jnp.where(owner_idx == 0, first_rows, received)  10.7 us
    mul x1, other arithmetic, per_device(): gathered.reshape(blocks, BLOCK, 2, blocks, BLOCK)  9.29 us
  transfers between devices with their start and end apart: 12, of which 12 were waited for; matrix products, arithmetic and copies ran while one was open for 10% of the time, Pallas kernels for 0%

commit v1 on v0

v1 whole, which is shorter than its diff:
```python
import functools

import jax
import jax.numpy as jnp
from jax import lax
from jax.experimental import pallas as pl
from jax.experimental.pallas import tpu as pltpu
from jax.sharding import PartitionSpec as P

BLOCK = 128
CHARGES = 4
LANES = 128
EPSILON = 1e-06
MICRO = 48
DELAY = 3


VMEM = pl.BlockSpec(memory_space=pltpu.VMEM)
HBM = pl.BlockSpec(memory_space=pl.ANY)


def allowed_outcome(charge_ref, site, i, j):
    return (charge_ref[site + 1, j] - charge_ref[site, i]) & (CHARGES - 1)


def pick_kernel(blocks, charge_ref, tensor_ref, *refs):
    *out_refs, both_ref, packed_ref = refs
    width = both_ref.shape[2]
    per_shard = width // BLOCK
    site = lax.axis_index("site")
    mine = lax.axis_index("sample") * per_shard
    row = lax.broadcasted_iota(jnp.int32, (2 * BLOCK, 2 * BLOCK), 0)
    col = lax.broadcasted_iota(jnp.int32, (2 * BLOCK, 2 * BLOCK), 1)
    source = jnp.where(row < BLOCK, 2 * row, 2 * (row - BLOCK) + 1)
    select = jnp.where(col == source, 1.0, 0.0).astype(jnp.bfloat16)
    entry = jnp.int32(0)
    for i in range(blocks):
        slot = i % 2
        pairs = tensor_ref[0, i * BLOCK : (i + 1) * BLOCK, :, :]
        both_ref[slot] = jnp.dot(
            select, pairs.reshape(2 * BLOCK, width), preferred_element_type=jnp.float32
        ).astype(jnp.bfloat16)
        for j in range(per_shard):
            outcome = allowed_outcome(charge_ref, site, i, mine + j)
            start = pl.multiple_of(jnp.minimum(outcome, 1) * BLOCK, BLOCK)
            there = pl.ds(pl.multiple_of(entry * BLOCK, BLOCK), BLOCK)
            packed_ref[there, :] = both_ref[
                slot, pl.ds(start, BLOCK), j * BLOCK : (j + 1) * BLOCK
            ]
            entry += (outcome < 2).astype(jnp.int32)
    low = 0
    for out_ref in out_refs:
        high = low + out_ref.shape[0]
        out_ref[...] = packed_ref[low:high, :]
        low = high


def pick(tensor, charges, counts):
    _, bond, _, width = tensor.shape
    blocks = bond // BLOCK
    total = blocks * (width // BLOCK)
    return pl.pallas_call(
        functools.partial(pick_kernel, blocks),
        out_shape=tuple(
            jax.ShapeDtypeStruct((count * BLOCK, BLOCK), tensor.dtype) for count in counts
        ),
        grid_spec=pltpu.PrefetchScalarGridSpec(
            num_scalar_prefetch=1,
            grid=(1,),
            in_specs=[VMEM],
            out_specs=tuple(VMEM for _ in counts),
            scratch_shapes=[
                pltpu.VMEM((2, 2 * BLOCK, width), jnp.bfloat16),
                pltpu.VMEM(((total + 1) * BLOCK, BLOCK), jnp.bfloat16),
            ],
        ),
        compiler_params=pltpu.CompilerParams(vmem_limit_bytes=16 * 1024 * 1024),
        cost_estimate=pl.CostEstimate(
            flops=8 * bond * width * BLOCK, bytes_accessed=6 * bond * width, transcendentals=0
        ),
    )(charges, tensor)


def plan_kernel(blocks, per_shard, cores, charge_ref, table_ref):
    shards, _ = table_ref.shape
    chips = shards // cores
    me = lax.axis_index("sample")
    site = lax.axis_index("site")
    total = blocks * per_shard
    for d in range(shards):
        chip = lax.rem(me // cores + d // cores, chips)
        first = (chip * cores + lax.rem(me + d, cores)) * per_shard

        def one(i, entry):
            for j in range(per_shard):
                table_ref[d, entry] = i * (shards * per_shard) + first + j
                allowed = allowed_outcome(charge_ref, site, i, first + j) < 2
                entry += allowed.astype(jnp.int32)
            return entry

        count = lax.fori_loop(0, blocks, one, jnp.int32(0))
        table_ref[d, total + 1] = count


def plan(charges, blocks, per_shard, cores, shards):
    size = blocks * per_shard + 2
    return pl.pallas_call(
        functools.partial(plan_kernel, blocks, per_shard, cores),
        out_shape=jax.ShapeDtypeStruct((shards, size), jnp.int32),
        grid_spec=pltpu.PrefetchScalarGridSpec(
            num_scalar_prefetch=1,
            grid=(1,),
            in_specs=[],
            out_specs=pl.BlockSpec(memory_space=pltpu.SMEM),
        ),
        compiler_params=pltpu.CompilerParams(vmem_limit_bytes=1024 * 1024),
        cost_estimate=pl.CostEstimate(flops=100, bytes_accessed=4096, transcendentals=0),
    )(charges)


def place_blocks(table_ref, refs, out_ref, first):
    across = out_ref.shape[1] // BLOCK
    total = table_ref.shape[1] - 2
    for d, ref in enumerate(refs):
        count = table_ref[d, total + 1]

        def one(e, carry):
            spot = table_ref[d, first + e]
            rows = pl.ds(pl.multiple_of((spot // across) * BLOCK, BLOCK), BLOCK)
            cols = pl.ds(pl.multiple_of(lax.rem(spot, across) * BLOCK, BLOCK), BLOCK)
            out_ref[rows, cols] = ref[pl.ds(pl.multiple_of(e * BLOCK, BLOCK), BLOCK), :]
            return carry

        size = ref.shape[0] // BLOCK
        lax.fori_loop(0, jnp.clip(count - first, 0, size), one, 0)


def unpack_kernel(shards, rest, extras, first, fresh, table_ref, *refs):
    refs = list(refs)
    pieces, refs = refs[:shards], refs[shards:]
    more, refs = refs[:rest], refs[rest:]
    refs = refs[extras:]
    if not fresh:
        refs = refs[1:]
    out_ref, scratch = refs[0], refs[1:]
    if fresh:
        out_ref[...] = jnp.zeros(out_ref.shape, out_ref.dtype)
    place_blocks(table_ref, pieces, out_ref, first)
    if rest:
        spare_ref, sem = scratch
        last = first + pieces[0].shape[0] // BLOCK
        total = table_ref.shape[1] - 2
        need = table_ref[0, total + 1] > last
        for d in range(1, shards):
            need |= table_ref[d, total + 1] > last

        @pl.when(need)
        def _():
            for d in range(shards):
                copy = pltpu.make_async_copy(more[d], spare_ref.at[d], sem)
                copy.start()
                copy.wait()
            place_blocks(table_ref, [spare_ref.at[d] for d in range(shards)], out_ref, last)


def unpack(table, pieces, more, extras, first, weights, bond):
    shards = len(pieces)
    fresh = weights is None
    operands = [*pieces, *more, *extras]
    in_specs = [VMEM] * shards + [HBM] * (len(more) + len(extras))
    aliases = {}
    if not fresh:
        operands.append(weights)
        in_specs.append(VMEM)
        aliases = {len(operands): 0}
    scratch = []
    if more:
        scratch = [pltpu.VMEM((shards, *more[0].shape), more[0].dtype), pltpu.SemaphoreType.DMA]
    return pl.pallas_call(
        functools.partial(unpack_kernel, shards, len(more), len(extras), first, fresh),
        out_shape=pltpu.VMEM((bond, bond), pieces[0].dtype),
        grid_spec=pltpu.PrefetchScalarGridSpec(
            num_scalar_prefetch=1,
            grid=(1,),
            in_specs=in_specs,
            out_specs=VMEM,
            scratch_shapes=scratch,
        ),
        input_output_aliases=aliases,
        compiler_params=pltpu.CompilerParams(vmem_limit_bytes=24 * 1024 * 1024),
        cost_estimate=pl.CostEstimate(
            flops=0, bytes_accessed=4 * shards * pieces[0].size, transcendentals=0
        ),
    )(table, *operands)


def step_kernel(chunks, at, relay, carried, place_ref, right_ref, *refs):
    refs = list(refs)
    first_ref, picks_ref, left_ref = refs[:3]
    weights = refs[3 : 3 + chunks]
    refs = refs[3 + chunks :]
    received_ref = refs.pop(0) if relay else None
    if carried:
        old_ref, old_norm_ref = refs[:2]
        refs = refs[4:]
    sent_ref, norm_ref, fronts_ref, norms_ref, lhs_ref, acc_ref, sems = refs
    rows, bond = sent_ref.shape
    tile = min(bond, 512)

    def copies():
        where = pl.ds(pl.multiple_of(place_ref[at - 4 + 2], 8), rows)
        return (
            pltpu.make_async_copy(old_ref, fronts_ref.at[where], sems.at[0]),
            pltpu.make_async_copy(old_norm_ref, norms_ref.at[where], sems.at[1]),
        )

    if carried:

        @pl.when(place_ref[at - 4 + 1] == 1)
        def _():
            for copy in copies():
                copy.start()

    @pl.when(place_ref[at + 1] == 1)
    def _():
        here = pl.ds(pl.multiple_of(place_ref[at + 2], 8), rows)
        front = first_ref[here, :].astype(jnp.float32)
        if relay:
            front = jnp.where(
                place_ref[at + 3] == 0, front, received_ref[...].astype(jnp.float32)
            )
        charge = (left_ref[...] + picks_ref[here, :]) & (CHARGES - 1)
        for q in range(CHARGES):
            lhs_ref[q * rows : (q + 1) * rows, :] = jnp.where(charge == q, front, 0.0).astype(
                jnp.bfloat16
            )
        for n in range(bond // tile):
            cols = slice(n * tile, (n + 1) * tile)
            total = jnp.zeros((CHARGES * rows, tile), jnp.float32)
            low = 0
            for part in weights:
                high = low + part.shape[0]
                total += jnp.dot(
                    lhs_ref[:, low:high], part[:, cols], preferred_element_type=jnp.float32
                )
                low = high
            acc_ref[:, cols] = total

        def chosen(j):
            first = pl.multiple_of(right_ref[j] * rows, 8)
            return acc_ref[pl.ds(first, rows), j * BLOCK : (j + 1) * BLOCK]

        squares = jnp.zeros((rows, LANES), jnp.float32)
        for j in range(bond // BLOCK):
            squares += chosen(j) * chosen(j)
        norm = jnp.sqrt(jnp.sum(squares, axis=1, keepdims=True) / bond + EPSILON)
        norm_ref[...] = jnp.broadcast_to(norm, norm_ref.shape)
        for j in range(bond // BLOCK):
            sent_ref[:, j * BLOCK : (j + 1) * BLOCK] = (chosen(j) / norm).astype(sent_ref.dtype)

    if carried:

        @pl.when(place_ref[at - 4 + 1] == 1)
        def _():
            for copy in copies():
                copy.wait()


def advance(step, place, right, fronts_in, picks, left, weights, received, old, results):
    row_count, bond = fronts_in.shape
    rows = MICRO
    relay = received is not None
    carried = results is not None
    operands = [fronts_in, picks, left, *weights]
    in_specs = [VMEM] * len(operands)
    aliases = {}
    if relay:
        operands.append(received)
        in_specs.append(VMEM)
    if carried:
        operands += [*old, *results]
        in_specs += [VMEM, VMEM, HBM, HBM]
        aliases = {len(operands): 2, len(operands) + 1: 3}
    return pl.pallas_call(
        functools.partial(step_kernel, len(weights), 4 * step, relay, carried),
        out_shape=(
            jax.ShapeDtypeStruct((rows, bond), jnp.bfloat16),
            jax.ShapeDtypeStruct((rows, LANES), jnp.float32),
            jax.ShapeDtypeStruct((row_count, bond), jnp.bfloat16),
            jax.ShapeDtypeStruct((row_count, LANES), jnp.float32),
        ),
        grid_spec=pltpu.PrefetchScalarGridSpec(
            num_scalar_prefetch=2,
            grid=(1,),
            in_specs=in_specs,
            out_specs=(VMEM, VMEM, HBM, HBM),
            scratch_shapes=[
                pltpu.VMEM((CHARGES * rows, bond), jnp.bfloat16),
                pltpu.VMEM((CHARGES * rows, bond), jnp.float32),
                pltpu.SemaphoreType.DMA((2,)),
            ],
        ),
        input_output_aliases=aliases,
        compiler_params=pltpu.CompilerParams(vmem_limit_bytes=24 * 1024 * 1024),
        cost_estimate=pl.CostEstimate(
            flops=2 * CHARGES * rows * bond * bond,
            bytes_accessed=2 * bond * bond,
            transcendentals=0,
        ),
    )(place, right, *operands)


def finish_kernel(at, place_ref, old_ref, old_norm_ref, _, __, fronts_ref, norms_ref, sems):
    rows = old_ref.shape[0]

    @pl.when(place_ref[at + 1] == 1)
    def _():
        where = pl.ds(pl.multiple_of(place_ref[at + 2], 8), rows)
        copies = (
            pltpu.make_async_copy(old_ref, fronts_ref.at[where], sems.at[0]),
            pltpu.make_async_copy(old_norm_ref, norms_ref.at[where], sems.at[1]),
        )
        for copy in copies:
            copy.start()
        for copy in copies:
            copy.wait()


def finish(step, place, old, results):
    return pl.pallas_call(
        functools.partial(finish_kernel, 4 * step),
        out_shape=tuple(jax.ShapeDtypeStruct(r.shape, r.dtype) for r in results),
        grid_spec=pltpu.PrefetchScalarGridSpec(
            num_scalar_prefetch=1,
            grid=(1,),
            in_specs=[VMEM, VMEM, HBM, HBM],
            out_specs=(HBM, HBM),
            scratch_shapes=[pltpu.SemaphoreType.DMA((2,))],
        ),
        input_output_aliases={3: 0, 4: 1},
        compiler_params=pltpu.CompilerParams(vmem_limit_bytes=4 * 1024 * 1024),
    )(place, *old, *results)


def gather_weights(site_tensor, charges, extras):
    shards = lax.axis_size("sample")
    sites = lax.axis_size("site")
    groups = lax.axis_size("groups")
    cores = 2 if shards % 2 == 0 else 1
    chips = shards // cores
    bond = site_tensor.shape[1]
    blocks = bond // BLOCK
    per_shard = site_tensor.shape[3] // BLOCK
    total = blocks * per_shard
    size = total // 4
    counts = [size, size, size, total - 3 * size]
    cap = 3 * size
    swap = [(i, i ^ 1) for i in range(shards)]

    def across_chips(part):
        return [
            lax.ppermute(
                part,
                "sample",
                [(i, ((i // cores - hop) % chips) * cores + i % cores) for i in range(shards)],
            )
            for hop in range(1, chips)
        ]

    def across_cores(part):
        return [lax.ppermute(part, "sample", swap)] if cores == 2 else []

    own = pick(site_tensor, charges, counts)
    far = []
    for c in range(3):
        far.append(across_chips(own[c]))

    table = plan(charges, blocks, per_shard, cores, shards)
    outcome = (charges[1:, None, :] - charges[:-1, :, None]) & (CHARGES - 1)
    held = jnp.sum((outcome < 2).reshape(sites, blocks, shards, per_shard), axis=(1, 3))
    most = jnp.max(held.astype(jnp.int32)).reshape(1)
    for hop in range(1, groups):
        pairs = [(i, (i + hop) % groups) for i in range(groups)]
        most = jnp.maximum(most, lax.ppermute(jnp.max(held).astype(jnp.int32).reshape(1), "groups", pairs))

    def send_rest(part):
        parts = [part, *across_chips(part)]
        parts = [parts[:1] + across_cores(parts[0])] + [[p] + across_cores(p) for p in parts[1:]]
        return tuple(p for pair in parts for p in pair)[1:]

    def keep(part):
        return tuple(jnp.zeros_like(part) for _ in range(shards - 1))

    rest = [own[3], *lax.cond(most[0] > cap, send_rest, keep, own[3])]
    weights = None
    for c in range(3):
        parts = [own[c], *far[c]]
        if weights is not None:
            parts, weights = lax.optimization_barrier((parts, weights))
        pieces = []
        for part in parts:
            pieces += [part, *across_cores(part)]
        weights = unpack(
            table, pieces, rest if c == 2 else [], [*extras, *rest] if c == 0 else [],
            c * size, weights, bond,
        )
    return [weights]


def pipeline(site_tensor, fronts_in, outcomes, charges):
    owner = lax.axis_index("site")
    sites = lax.axis_size("site")
    left = lax.dynamic_index_in_dim(charges, owner, 0, keepdims=False)
    right = lax.dynamic_index_in_dim(charges, owner + 1, 0, keepdims=False)
    row_count, _ = fronts_in.shape
    micro_count = row_count // MICRO
    picks = outcomes[0][:, None]
    left_lanes = jnp.repeat(left, BLOCK)[None, :]
    steps = micro_count + DELAY * (sites - 1)
    micro = jnp.arange(steps, dtype=jnp.int32) - DELAY * owner
    active = (micro >= 0) & (micro < micro_count)
    micro = jnp.clip(micro, 0, micro_count - 1)
    place = jnp.stack(
        [micro, active.astype(jnp.int32), micro * MICRO, jnp.full_like(micro, owner)], axis=1
    ).astype(jnp.int32).reshape(-1)

    weights = gather_weights(site_tensor, charges, [place, picks, left_lanes, right])
    received, old, results = {}, None, None
    for step in range(steps):
        sent, norm, *results = advance(
            step, place, right, fronts_in, picks, left_lanes, weights,
            received.pop(step - DELAY, None), old, results,
        )
        old = (sent, norm)
        pairs = [
            (s, s + 1) for s in range(sites - 1) if 0 <= step - DELAY * s < micro_count
        ]
        if pairs:
            received[step] = lax.ppermute(sent, "site", pairs)
    fronts, norms = finish(steps - 1, place, old, results)
    return fronts[None], jnp.log(norms[:, 0])[None]


def solution(mesh):
    in_specs = (
        P(("groups", "site"), None, None, "sample"),
        P(("groups", "sample"), None),
        P(("groups", "site"), "sample"),
        P("groups", None),
    )
    out_specs = (P(("groups", "site"), "sample", None), P(("groups", "site"), "sample"))
    return jax.shard_map(
        pipeline, mesh=mesh, in_specs=in_specs, out_specs=out_specs, check_vma=False
    )
```

time: 362 us -> 114 us (0.31)
  waiting for transfers between devices: 175 us -> 41.7 us
  matrix products: 70.3 us -> 0 us
  local copies, waits for them, and re-layouts: 57.7 us -> 6.83 us
  Pallas kernels: 0 us -> 40.4 us
  other arithmetic: 28.4 us -> 1.21 us
  between operations: 14.1 us -> 2.31 us
  starting transfers between devices: 14.3 us -> 20.7 us
    all_gather x1 -> x0, waiting for transfers between devices: 77.5 us -> none  [per_device(): gathered = lax.all_gather(site_tensor, 'sample', axis=3, tiled=True)[0]]
    dot_general x8 -> x0, matrix products: 70.3 us -> none  [advance(): jnp.dot(front_rows, masked, preferred_element_type=jnp.float32)]
    ppermute x11 -> x24, waiting for transfers between devices: 96.9 us -> 41.7 us  [the longest x14 20 us: pipeline(): received[step] = lax.ppermute(sent, 'site', pairs)]
    pallas_call x0 -> x23, Pallas kernels: none -> 40.4 us  [the longest x17 26.6 us: advance(): pl.pallas_call(functools.partial(step_kernel, len(weights), 4 * step, rel...]
    mul x2 -> x0, local copies, waits for them, and re-layouts: 32.2 us -> none  [per_device(): gathered.reshape(blocks, BLOCK, 2, blocks, BLOCK)]
    unnamed x7 -> x12, local copies, waits for them, and re-layouts: 13.7 us -> 2.88 us
    select_n x12 -> x0, other arithmetic: 10.8 us -> none  [the longest x11 10.7 us: section(): incoming = jnp.where(owner_idx == 0, first_rows, received)]
    mul x1 -> x0, other arithmetic: 9.29 us -> none  [per_device(): gathered.reshape(blocks, BLOCK, 2, blocks, BLOCK)]
  transfers between devices with their start and end apart: 12 -> 24, of which waited for: 12 -> 14; matrix products, arithmetic and copies ran while one was open for 10% -> 4% of each run, Pallas kernels for 0% -> 28%
where the time goes in v1:
time: 114 us; the launch traced here: 113 us
  waiting for transfers between devices  41.7 us (37%)
  Pallas kernels  40.4 us (35%)
  starting transfers between devices  20.7 us (18%)
  local copies, waits for them, and re-layouts  6.83 us (6%)
  between operations  2.31 us (2%)
  other arithmetic  1.21 us (1%)
    pallas_call x17, Pallas kernels, advance(): pl.pallas_call(functools.partial(step_kernel, len(weights), 4 * step, rel...  26.6 us
    ppermute x14, waiting for transfers between devices, pipeline(): received[step] = lax.ppermute(sent, 'site', pairs)  20 us
    ppermute x3, waiting for transfers between devices, across_chips(): lax.ppermute(part, 'sample', [(i, (i // cores - hop) % chips * cores + i...  19 us
    ppermute x14, starting transfers between devices, pipeline(): received[step] = lax.ppermute(sent, 'site', pairs)  14.6 us
    pallas_call x3, Pallas kernels, unpack(): pl.pallas_call(functools.partial(unpack_kernel, shards, len(more), len(ex...  5.86 us
    ppermute x3, starting transfers between devices, across_chips(): lax.ppermute(part, 'sample', [(i, (i // cores - hop) % chips * cores + i...  3.54 us
    pallas_call x1, Pallas kernels, pick(): pl.pallas_call(functools.partial(pick_kernel, blocks), out_shape=tuple((j...  3.53 us
    pallas_call x1, Pallas kernels, plan(): pl.pallas_call(functools.partial(plan_kernel, blocks, per_shard, cores),...  3.12 us
  transfers between devices with their start and end apart: 24, of which 14 were waited for; matrix products, arithmetic and copies ran while one was open for 4% of the time, Pallas kernels for 28%

profile of v1, /device:TPU:24, one launch (start us, length us, event | category | flops | bytes accessed | tf_op | source)
XLA Modules:
  0.0 113.1 jit_solution(4625404740801428131)
XLA Ops:
  0.6 2.2 %copy-done.1 = bf16[1,2048,2,512]{3,2,1,0:T(2,128)(2,1)S(1)} copy-done((bf16[1,2048,2,512]{3,2,1,0:T(2,128)(2,1)S(1)}, bf16[1,2048,2,512]{3,2,1,0:T(2,128)(2,1)}, u32[]{:S(2)}) %copy-start.1) | copy-done | bytes 4194328
  2.8 0.7 copy-done.2
  3.5 3.5 %shard_map.60 = (bf16[2048,128]{1,0:T(8,128)(2,1)S(1)}, bf16[2048,128]{1,0:T(8,128)(2,1)S(1)}, bf16[2048,128]{1,0:T(8,128)(2,1)S(1)}, bf16[2048,128]{1,0:T(8,128)(2,1)}) custom-call(s32[5,16]{1,0:T(8,128)S(1)} %copy-done.2, bf16[1,2048,2,512]{3,2,1,0:T(2,128)(2,1)S(1)} %copy-done.1), custom_call_target="tpu_custom_call" | custom-call | flops 1073741824 | bytes 6291456 | tf_op jit(solution)/shard_map/pallas_call | solution.py:62
  7.0 1.5 %collective-permute-start.6 = (bf16[2048,128]{1,0:T(8,128)(2,1)S(1)}, bf16[2048,128]{1,0:T(8,128)(2,1)S(1)}, u32[]{:S(2)}, u32[]{:S(2)}) collective-permute-start(bf16[2048,128]{1,0:T(8,128)(2,1)S(1)} %get-tuple-element.88.refs_0_), channel_id=1, source_target_pairs={{0,2},{1,3},{2,0},{3,1},{4,6},{5,7},{6,4},{7,5},{8,10},{9,11},{10,... | collective-permute-start | bytes 1572872 | tf_op jit(solution)/shard_map/ppermute | solution.py:362
  9.1 0.7 reduce_max.8
  9.7 1.5 %collective-permute-start.8 = (s32[1]{0:T(128)}, s32[1]{0:T(128)}, u32[]{:S(2)}, u32[]{:S(2)}) collective-permute-start(s32[1]{0:T(128)} %bitcast.4), channel_id=1, source_target_pairs={{0,16},{16,0},{1,17},{17,1},{2,18},{18,2},{3,19},{19,3},{4,20},{20... | collective-permute-start | bytes 20 | tf_op jit(solution)/shard_map/ppermute | solution.py:384
  11.8 3.1 %shard_map.59.table_ref = s32[4,66]{1,0:T(4,128)S(1)} custom-call(s32[5,16]{1,0:T(8,128)S(1)} %copy-done.3), custom_call_target="tpu_custom_call" | custom-call | flops 100 | bytes 4096 | tf_op jit(solution)/shard_map/pallas_call | solution.py:107
  15.0 6.8 %collective-permute-done.6.refs_2_ = bf16[2048,128]{1,0:T(8,128)(2,1)S(1)} collective-permute-done((bf16[2048,128]{1,0:T(8,128)(2,1)S(1)}, bf16[2048,128]{1,0:T(8,128)(2,1)S(1)}, u32[]{:S(2)}, u32[]{:S(2)}) %collective-permute-start.6) | collective-permute-done | bytes 524320 | tf_op jit(solution)/shard_map/ppermute | solution.py:362
  23.6 2.7 %conditional.1 = (bf16[2048,128]{1,0:T(8,128)(2,1)}, bf16[2048,128]{1,0:T(8,128)(2,1)}, bf16[2048,128]{1,0:T(8,128)(2,1)}) conditional(s32[]{:T(128)} %bitcast.5, () %tuple.18, bf16[2048,128]{1,0:T(8,128)(2,1)} %get-tuple-element.89.refs_8_.refs_4_), branch_computations={%region_2.3_spmd, %region_3.4_spmd} | conditional | bytes 6291600 | solution.py:394
  23.6 0.9 broadcast.70
  24.5 0.9 broadcast.70.clone
  25.4 0.9 broadcast.70.clone.1
  26.3 3.3 %shard_map.61.refs_4_ = bf16[2048,2048]{1,0:T(8,128)(2,1)S(1)} custom-call(s32[4,66]{1,0:T(4,128)S(1)} %shard_map.59.table_ref, bf16[2048,128]{1,0:T(8,128)(2,1)S(1)} %get-tuple-element.88.refs_0_, bf16[2048,128]{1,0:T(8,128)(2,1)S(1)} %collective-permute-done.5.refs_1_, bf16[2048,128]{1,0:T(8,128)(2,1)S(1)} %collective-permute-done.6.refs_2_, ...), custom_call_target="tpu_custom_call" | custom-call | bytes 4194304 | tf_op jit(solution)/shard_map/pallas_call | solution.py:179
  29.7 2.3 %collective-permute-done.4.refs_2_ = bf16[2048,128]{1,0:T(8,128)(2,1)S(1)} collective-permute-done((bf16[2048,128]{1,0:T(8,128)(2,1)S(1)}, bf16[2048,128]{1,0:T(8,128)(2,1)S(1)}, u32[]{:S(2)}, u32[]{:S(2)}) %collective-permute-start.4) | collective-permute-done | bytes 524320 | tf_op jit(solution)/shard_map/ppermute | solution.py:362
  32.4 1.5 %collective-permute-start.3 = (bf16[2048,128]{1,0:T(8,128)(2,1)S(1)}, bf16[2048,128]{1,0:T(8,128)(2,1)S(1)}, u32[]{:S(2)}, u32[]{:S(2)}) collective-permute-start(bf16[2048,128]{1,0:T(8,128)(2,1)S(1)} %get-tuple-element.96.refs_0_), channel_id=1, source_target_pairs={{0,2},{1,3},{2,0},{3,1},{4,6},{5,7},{6,4},{7,5},{8,10},{9,11},{10,... | collective-permute-start | bytes 1572872 | tf_op jit(solution)/shard_map/ppermute | solution.py:362
  34.6 1.8 %shard_map.62.refs_8_ = bf16[2048,2048]{1,0:T(8,128)(2,1)S(1)} custom-call(s32[4,66]{1,0:T(4,128)S(1)} %shard_map.59.table_ref, bf16[2048,128]{1,0:T(8,128)(2,1)S(1)} %get-tuple-element.93.refs_0_, bf16[2048,128]{1,0:T(8,128)(2,1)S(1)} %collective-permute-done.9.refs_1_, ...), custom_call_target="tpu_custom_call", output_to_operand_aliasing={{}: (5, {})} | custom-call | bytes 4194304 | tf_op jit(solution)/shard_map/pallas_call | solution.py:179
  36.4 9.9 %collective-permute-done.3.refs_2_ = bf16[2048,128]{1,0:T(8,128)(2,1)S(1)} collective-permute-done((bf16[2048,128]{1,0:T(8,128)(2,1)S(1)}, bf16[2048,128]{1,0:T(8,128)(2,1)S(1)}, u32[]{:S(2)}, u32[]{:S(2)}) %collective-permute-start.3) | collective-permute-done | bytes 524320 | tf_op jit(solution)/shard_map/ppermute | solution.py:362
  46.8 1.4 %collective-permute-done.11.refs_1_ = bf16[2048,128]{1,0:T(8,128)(2,1)S(1)} collective-permute-done((bf16[2048,128]{1,0:T(8,128)(2,1)S(1)}, bf16[2048,128]{1,0:T(8,128)(2,1)S(1)}, u32[]{:S(2)}, u32[]{:S(2)}) %collective-permute-start.11) | collective-permute-done | bytes 524320 | tf_op jit(solution)/shard_map/ppermute | solution.py:371
  48.2 0.7 collective-permute-done.12.refs_3_
  48.9 0.7 shard_map.63.refs_3_
  50.3 0.7 collective-permute-start.14
  51.6 0.7 collective-permute-start.13
  52.8 0.7 collective-permute-start.17
  54.1 0.7 collective-permute-start.16
  54.8 0.8 shard_map.68
  55.6 0.7 collective-permute-start.15
  58.2 1.3 %collective-permute-start.19 = (bf16[48,2048]{1,0:T(8,128)(2,1)S(1)}, bf16[48,2048]{1,0:T(8,128)(2,1)S(1)}, u32[]{:S(2)}, u32[]{:S(2)}) collective-permute-start(bf16[48,2048]{1,0:T(8,128)(2,1)S(1)} %get-tuple-element.123.refs_5_), channel_id=1, source_target_pairs={{0,4},{4,8},{8,12},{1,5},{5,9},{9,13},{2,6},{6,10},{10,14},{3,7},{... | collective-permute-start | bytes 589832 | tf_op jit(solution)/shard_map/ppermute | solution.py:439
  60.1 1.3 %collective-permute-start.18 = (bf16[48,2048]{1,0:T(8,128)(2,1)S(1)}, bf16[48,2048]{1,0:T(8,128)(2,1)S(1)}, u32[]{:S(2)}, u32[]{:S(2)}) collective-permute-start(bf16[48,2048]{1,0:T(8,128)(2,1)S(1)} %get-tuple-element.127.refs_5_), channel_id=1, source_target_pairs={{0,4},{4,8},{8,12},{1,5},{5,9},{9,13},{2,6},{6,10},{10,14},{3,7},{... | collective-permute-start | bytes 589832 | tf_op jit(solution)/shard_map/ppermute | solution.py:439
  62.0 1.3 %collective-permute-start.23 = (bf16[48,2048]{1,0:T(8,128)(2,1)S(1)}, bf16[48,2048]{1,0:T(8,128)(2,1)S(1)}, u32[]{:S(2)}, u32[]{:S(2)}) collective-permute-start(bf16[48,2048]{1,0:T(8,128)(2,1)S(1)} %get-tuple-element.131.refs_5_), channel_id=1, source_target_pairs={{4,8},{8,12},{5,9},{9,13},{6,10},{10,14},{7,11},{11,15},{20,24},{2... | collective-permute-start | bytes 589832 | tf_op jit(solution)/shard_map/ppermute | solution.py:439
  63.3 13.7 %collective-permute-done.19.refs_4_ = bf16[48,2048]{1,0:T(8,128)(2,1)S(1)} collective-permute-done((bf16[48,2048]{1,0:T(8,128)(2,1)S(1)}, bf16[48,2048]{1,0:T(8,128)(2,1)S(1)}, u32[]{:S(2)}, u32[]{:S(2)}) %collective-permute-start.19) | collective-permute-done | bytes 196640 | tf_op jit(solution)/shard_map/ppermute | solution.py:439
  77.0 2.6 %shard_map.73 = (bf16[48,2048]{1,0:T(8,128)(2,1)S(1)}, f32[48,128]{1,0:T(8,128)S(1)}, bf16[384,2048]{1,0:T(8,128)(2,1)}, f32[384,128]{1,0:T(8,128)S(1)}) custom-call(s32[68]{0:T(128)S(1)} %reshape.58.refs_4_.place_ref, s32[16]{0:T(128)S(1)} %get-tuple-element.172.refs_7_.right_ref, ...), custom_call_target="tpu_custom_call", output_to_operand_aliasing={{2}: (9, {}), {3}: (10, {})} | custom-call | flops 1610612736 | bytes 8388608 | tf_op jit(solution)/shard_map/pallas_call | solution.py:284
  79.6 1.3 %collective-permute-start.22 = (bf16[48,2048]{1,0:T(8,128)(2,1)S(1)}, bf16[48,2048]{1,0:T(8,128)(2,1)S(1)}, u32[]{:S(2)}, u32[]{:S(2)}) collective-permute-start(bf16[48,2048]{1,0:T(8,128)(2,1)S(1)} %get-tuple-element.135.refs_5_), channel_id=1, source_target_pairs={{4,8},{8,12},{5,9},{9,13},{6,10},{10,14},{7,11},{11,15},{20,24},{2... | collective-permute-start | bytes 589832 | tf_op jit(solution)/shard_map/ppermute | solution.py:439
  80.9 0.9 collective-permute-done.18.refs_4_
  81.8 2.6 %shard_map.74 = (bf16[48,2048]{1,0:T(8,128)(2,1)S(1)}, f32[48,128]{1,0:T(8,128)S(1)}, bf16[384,2048]{1,0:T(8,128)(2,1)}, f32[384,128]{1,0:T(8,128)S(1)}) custom-call(s32[68]{0:T(128)S(1)} %reshape.58.refs_4_.place_ref, s32[16]{0:T(128)S(1)} %get-tuple-element.172.refs_7_.right_ref, ...), custom_call_target="tpu_custom_call", output_to_operand_aliasing={{2}: (9, {}), {3}: (10, {})} | custom-call | flops 1610612736 | bytes 8388608 | tf_op jit(solution)/shard_map/pallas_call | solution.py:284
  84.4 1.5 %collective-permute-start.21 = (bf16[48,2048]{1,0:T(8,128)(2,1)S(1)}, bf16[48,2048]{1,0:T(8,128)(2,1)S(1)}, u32[]{:S(2)}, u32[]{:S(2)}) collective-permute-start(bf16[48,2048]{1,0:T(8,128)(2,1)S(1)} %get-tuple-element.139.refs_5_), channel_id=1, source_target_pairs={{4,8},{8,12},{5,9},{9,13},{6,10},{10,14},{7,11},{11,15},{20,24},{2... | collective-permute-start | bytes 589832 | tf_op jit(solution)/shard_map/ppermute | solution.py:439
  86.4 2.7 %shard_map.75 = (bf16[48,2048]{1,0:T(8,128)(2,1)S(1)}, f32[48,128]{1,0:T(8,128)S(1)}, bf16[384,2048]{1,0:T(8,128)(2,1)}, f32[384,128]{1,0:T(8,128)S(1)}) custom-call(s32[68]{0:T(128)S(1)} %reshape.58.refs_4_.place_ref, s32[16]{0:T(128)S(1)} %get-tuple-element.172.refs_7_.right_ref, ...), custom_call_target="tpu_custom_call", output_to_operand_aliasing={{2}: (9, {}), {3}: (10, {})} | custom-call | flops 1610612736 | bytes 8388608 | tf_op jit(solution)/shard_map/pallas_call | solution.py:284
  89.1 1.3 %collective-permute-start.26 = (bf16[48,2048]{1,0:T(8,128)(2,1)S(1)}, bf16[48,2048]{1,0:T(8,128)(2,1)S(1)}, u32[]{:S(2)}, u32[]{:S(2)}) collective-permute-start(bf16[48,2048]{1,0:T(8,128)(2,1)S(1)} %get-tuple-element.143.refs_5_), channel_id=1, source_target_pairs={{8,12},{9,13},{10,14},{11,15},{24,28},{25,29},{26,30},{27,31}} | collective-permute-start | bytes 589832 | tf_op jit(solution)/shard_map/ppermute | solution.py:439
  91.0 2.6 %shard_map.76 = (bf16[48,2048]{1,0:T(8,128)(2,1)S(1)}, f32[48,128]{1,0:T(8,128)S(1)}, bf16[384,2048]{1,0:T(8,128)(2,1)}, f32[384,128]{1,0:T(8,128)S(1)}) custom-call(s32[68]{0:T(128)S(1)} %reshape.58.refs_4_.place_ref, s32[16]{0:T(128)S(1)} %get-tuple-element.172.refs_7_.right_ref, ...), custom_call_target="tpu_custom_call", output_to_operand_aliasing={{2}: (9, {}), {3}: (10, {})} | custom-call | flops 1610612736 | bytes 8388608 | tf_op jit(solution)/shard_map/pallas_call | solution.py:284
  93.6 1.3 %collective-permute-start.25 = (bf16[48,2048]{1,0:T(8,128)(2,1)S(1)}, bf16[48,2048]{1,0:T(8,128)(2,1)S(1)}, u32[]{:S(2)}, u32[]{:S(2)}) collective-permute-start(bf16[48,2048]{1,0:T(8,128)(2,1)S(1)} %get-tuple-element.147.refs_5_), channel_id=1, source_target_pairs={{8,12},{9,13},{10,14},{11,15},{24,28},{25,29},{26,30},{27,31}} | collective-permute-start | bytes 589832 | tf_op jit(solution)/shard_map/ppermute | solution.py:439
  94.9 1.2 %collective-permute-done.21.refs_4_ = bf16[48,2048]{1,0:T(8,128)(2,1)S(1)} collective-permute-done((bf16[48,2048]{1,0:T(8,128)(2,1)S(1)}, bf16[48,2048]{1,0:T(8,128)(2,1)S(1)}, u32[]{:S(2)}, u32[]{:S(2)}) %collective-permute-start.21) | collective-permute-done | bytes 196640 | tf_op jit(solution)/shard_map/ppermute | solution.py:439
  96.2 2.7 %shard_map.77 = (bf16[48,2048]{1,0:T(8,128)(2,1)S(1)}, f32[48,128]{1,0:T(8,128)S(1)}, bf16[384,2048]{1,0:T(8,128)(2,1)}, f32[384,128]{1,0:T(8,128)S(1)}) custom-call(s32[68]{0:T(128)S(1)} %reshape.58.refs_4_.place_ref, s32[16]{0:T(128)S(1)} %get-tuple-element.172.refs_7_.right_ref, ...), custom_call_target="tpu_custom_call", output_to_operand_aliasing={{2}: (9, {}), {3}: (10, {})} | custom-call | flops 1610612736 | bytes 8388608 | tf_op jit(solution)/shard_map/pallas_call | solution.py:284
  98.9 1.3 %collective-permute-start.24 = (bf16[48,2048]{1,0:T(8,128)(2,1)S(1)}, bf16[48,2048]{1,0:T(8,128)(2,1)S(1)}, u32[]{:S(2)}, u32[]{:S(2)}) collective-permute-start(bf16[48,2048]{1,0:T(8,128)(2,1)S(1)} %get-tuple-element.151.refs_5_), channel_id=1, source_target_pairs={{8,12},{9,13},{10,14},{11,15},{24,28},{25,29},{26,30},{27,31}} | collective-permute-start | bytes 589832 | tf_op jit(solution)/shard_map/ppermute | solution.py:439
  100.5 2.6 %shard_map.78 = (bf16[48,2048]{1,0:T(8,128)(2,1)S(1)}, f32[48,128]{1,0:T(8,128)S(1)}, bf16[384,2048]{1,0:T(8,128)(2,1)}, f32[384,128]{1,0:T(8,128)S(1)}) custom-call(s32[68]{0:T(128)S(1)} %reshape.58.refs_4_.place_ref, s32[16]{0:T(128)S(1)} %get-tuple-element.172.refs_7_.right_ref, ...), custom_call_target="tpu_custom_call", output_to_operand_aliasing={{2}: (9, {}), {3}: (10, {})} | custom-call | flops 1610612736 | bytes 8388608 | tf_op jit(solution)/shard_map/pallas_call | solution.py:284
  103.2 1.3 %collective-permute-done.25.refs_4_ = bf16[48,2048]{1,0:T(8,128)(2,1)S(1)} collective-permute-done((bf16[48,2048]{1,0:T(8,128)(2,1)S(1)}, bf16[48,2048]{1,0:T(8,128)(2,1)S(1)}, u32[]{:S(2)}, u32[]{:S(2)}) %collective-permute-start.25) | collective-permute-done | bytes 196640 | tf_op jit(solution)/shard_map/ppermute | solution.py:439
  104.5 2.6 %shard_map.79 = (bf16[48,2048]{1,0:T(8,128)(2,1)S(1)}, f32[48,128]{1,0:T(8,128)S(1)}, bf16[384,2048]{1,0:T(8,128)(2,1)}, f32[384,128]{1,0:T(8,128)S(1)}) custom-call(s32[68]{0:T(128)S(1)} %reshape.58.refs_4_.place_ref, s32[16]{0:T(128)S(1)} %get-tuple-element.172.refs_7_.right_ref, ...), custom_call_target="tpu_custom_call", output_to_operand_aliasing={{2}: (9, {}), {3}: (10, {})} | custom-call | flops 1610612736 | bytes 8388608 | tf_op jit(solution)/shard_map/pallas_call | solution.py:284
  107.2 1.3 %collective-permute-done.24.refs_4_ = bf16[48,2048]{1,0:T(8,128)(2,1)S(1)} collective-permute-done((bf16[48,2048]{1,0:T(8,128)(2,1)S(1)}, bf16[48,2048]{1,0:T(8,128)(2,1)S(1)}, u32[]{:S(2)}, u32[]{:S(2)}) %collective-permute-start.24) | collective-permute-done | bytes 196640 | tf_op jit(solution)/shard_map/ppermute | solution.py:439
  108.5 2.7 %shard_map.80 = (bf16[48,2048]{1,0:T(8,128)(2,1)S(1)}, f32[48,128]{1,0:T(8,128)S(1)}, bf16[384,2048]{1,0:T(8,128)(2,1)}, f32[384,128]{1,0:T(8,128)S(1)}) custom-call(s32[68]{0:T(128)S(1)} %reshape.58.refs_4_.place_ref, s32[16]{0:T(128)S(1)} %get-tuple-element.172.refs_7_.right_ref, ...), custom_call_target="tpu_custom_call", output_to_operand_aliasing={{2}: (9, {}), {3}: (10, {})} | custom-call | flops 1610612736 | bytes 8388608 | tf_op jit(solution)/shard_map/pallas_call | solution.py:284
  111.1 1.2 %shard_map.81 = (bf16[384,2048]{1,0:T(8,128)(2,1)}, f32[384,128]{1,0:T(8,128)S(1)}) custom-call(s32[68]{0:T(128)S(1)} %reshape.58.refs_4_.place_ref, bf16[48,2048]{1,0:T(8,128)(2,1)S(1)} %get-tuple-element.163.old_ref, f32[48,128]{1,0:T(8,128)S(1)} %get-tuple-element.164.old_norm_ref, ...), custom_call_target="tpu_custom_call", output_to_operand_aliasing={{0}: (3, {}), {1}: (4, {})} | custom-call | tf_op jit(solution)/shard_map/pallas_call | solution.py:330
  (54 shorter events, 10.9 us)
Async XLA Ops:
  0.6 2.2 %copy-start.1 = (bf16[1,2048,2,512]{3,2,1,0:T(2,128)(2,1)S(1)}, bf16[1,2048,2,512]{3,2,1,0:T(2,128)(2,1)}, u32[]{:S(2)}) copy-start(bf16[1,2048,2,512]{3,2,1,0:T(2,128)(2,1)} %tensor_ref.1) | copy-start | bytes 12582916
  2.8 0.7 copy-start.2
  3.5 8.3 %copy-start.3 = (s32[5,16]{1,0:T(8,128)S(1)}, s32[5,16]{1,0:T(8,128)}, u32[]{:S(2)}) copy-start(s32[5,16]{1,0:T(8,128)} %charge_ref.3) | copy-start | bytes 964
  3.5 18.6 %copy-start.5 = (s32[1,384]{1,0:T(1,128)S(1)}, s32[1,384]{1,0:T(1,128)}, u32[]{:S(2)}) copy-start(s32[1,384]{1,0:T(1,128)} %param.8) | copy-start | bytes 4612
  7.0 14.8 %collective-permute-start.6 = (bf16[2048,128]{1,0:T(8,128)(2,1)S(1)}, bf16[2048,128]{1,0:T(8,128)(2,1)S(1)}, u32[]{:S(2)}, u32[]{:S(2)}) collective-permute-start(bf16[2048,128]{1,0:T(8,128)(2,1)S(1)} %get-tuple-element.88.refs_0_), channel_id=1, source_target_pairs={{0,2},{1,3},{2,0},{3,1},{4,6},{5,7},{6,4},{7,5},{8,10},{9,11},{10,... | collective-permute-start | bytes 1572872 | tf_op jit(solution)/shard_map/ppermute | solution.py:362
  8.5 17.7 %collective-permute-start.5 = (bf16[2048,128]{1,0:T(8,128)(2,1)S(1)}, bf16[2048,128]{1,0:T(8,128)(2,1)S(1)}, u32[]{:S(2)}, u32[]{:S(2)}) collective-permute-start(bf16[2048,128]{1,0:T(8,128)(2,1)S(1)} %get-tuple-element.88.refs_0_), channel_id=1, source_target_pairs={{0,1},{1,0},{2,3},{3,2},{4,5},{5,4},{6,7},{7,6},{8,9},{9,8},{10,11... | collective-permute-start | bytes 1572872 | tf_op jit(solution)/shard_map/ppermute | solution.py:371
  9.7 12.6 %collective-permute-start.8 = (s32[1]{0:T(128)}, s32[1]{0:T(128)}, u32[]{:S(2)}, u32[]{:S(2)}) collective-permute-start(s32[1]{0:T(128)} %bitcast.4), channel_id=1, source_target_pairs={{0,16},{16,0},{1,17},{17,1},{2,18},{18,2},{3,19},{19,3},{4,20},{20... | collective-permute-start | bytes 20 | tf_op jit(solution)/shard_map/ppermute | solution.py:384
  11.3 20.7 %collective-permute-start.4 = (bf16[2048,128]{1,0:T(8,128)(2,1)S(1)}, bf16[2048,128]{1,0:T(8,128)(2,1)S(1)}, u32[]{:S(2)}, u32[]{:S(2)}) collective-permute-start(bf16[2048,128]{1,0:T(8,128)(2,1)S(1)} %get-tuple-element.93.refs_0_), channel_id=1, source_target_pairs={{0,2},{1,3},{2,0},{3,1},{4,6},{5,7},{6,4},{7,5},{8,10},{9,11},{10,... | collective-permute-start | bytes 1572872 | tf_op jit(solution)/shard_map/ppermute | solution.py:362
  21.8 4.4 %collective-permute-start.7 = (bf16[2048,128]{1,0:T(8,128)(2,1)S(1)}, bf16[2048,128]{1,0:T(8,128)(2,1)}, u32[]{:S(2)}, u32[]{:S(2)}) collective-permute-start(bf16[2048,128]{1,0:T(8,128)(2,1)S(1)} %collective-permute-done.6.refs_2_), channel_id=1, source_target_pairs={{0,1},{1,0},{2,3},{3,2},{4,5},{5,4},{6,7},{7,6},{8,9},{9,8},{10,11... | collective-permute-start | bytes 1572872 | tf_op jit(solution)/shard_map/ppermute | solution.py:371
  31.9 2.0 %collective-permute-start.10 = (bf16[2048,128]{1,0:T(8,128)(2,1)S(1)}, bf16[2048,128]{1,0:T(8,128)(2,1)S(1)}, u32[]{:S(2)}, u32[]{:S(2)}) collective-permute-start(bf16[2048,128]{1,0:T(8,128)(2,1)S(1)} %collective-permute-done.4.refs_2_), channel_id=1, source_target_pairs={{0,1},{1,0},{2,3},{3,2},{4,5},{5,4},{6,7},{7,6},{8,9},{9,8},{10,11... | collective-permute-start | bytes 1572872 | tf_op jit(solution)/shard_map/ppermute | solution.py:371
  31.9 2.7 %collective-permute-start.9 = (bf16[2048,128]{1,0:T(8,128)(2,1)S(1)}, bf16[2048,128]{1,0:T(8,128)(2,1)S(1)}, u32[]{:S(2)}, u32[]{:S(2)}) collective-permute-start(bf16[2048,128]{1,0:T(8,128)(2,1)S(1)} %get-tuple-element.93.refs_0_), channel_id=1, source_target_pairs={{0,1},{1,0},{2,3},{3,2},{4,5},{5,4},{6,7},{7,6},{8,9},{9,8},{10,11... | collective-permute-start | bytes 1572872 | tf_op jit(solution)/shard_map/ppermute | solution.py:371
  32.4 16.5 %copy-start.4 = (bf16[2048,128]{1,0:T(8,128)(2,1)S(1)}, bf16[2048,128]{1,0:T(8,128)(2,1)}, u32[]{:S(2)}) copy-start(bf16[2048,128]{1,0:T(8,128)(2,1)} %get-tuple-element.89.refs_8_.refs_4_) | copy-start | bytes 1572868
  32.4 13.8 %collective-permute-start.3 = (bf16[2048,128]{1,0:T(8,128)(2,1)S(1)}, bf16[2048,128]{1,0:T(8,128)(2,1)S(1)}, u32[]{:S(2)}, u32[]{:S(2)}) collective-permute-start(bf16[2048,128]{1,0:T(8,128)(2,1)S(1)} %get-tuple-element.96.refs_0_), channel_id=1, source_target_pairs={{0,2},{1,3},{2,0},{3,1},{4,6},{5,7},{6,4},{7,5},{8,10},{9,11},{10,... | collective-permute-start | bytes 1572872 | tf_op jit(solution)/shard_map/ppermute | solution.py:362
  36.4 13.3 %copy-start = (bf16[384,2048]{1,0:T(8,128)(2,1)S(1)}, bf16[384,2048]{1,0:T(8,128)(2,1)}, u32[]{:S(2)}) copy-start(bf16[384,2048]{1,0:T(8,128)(2,1)} %refs_0_.33) | copy-start | bytes 4718596
  46.3 1.9 %collective-permute-start.11 = (bf16[2048,128]{1,0:T(8,128)(2,1)S(1)}, bf16[2048,128]{1,0:T(8,128)(2,1)S(1)}, u32[]{:S(2)}, u32[]{:S(2)}) collective-permute-start(bf16[2048,128]{1,0:T(8,128)(2,1)S(1)} %get-tuple-element.96.refs_0_), channel_id=1, source_target_pairs={{0,1},{1,0},{2,3},{3,2},{4,5},{5,4},{6,7},{7,6},{8,9},{9,8},{10,11... | collective-permute-start | bytes 1572872 | tf_op jit(solution)/shard_map/ppermute | solution.py:371
  46.3 2.7 %collective-permute-start.12 = (bf16[2048,128]{1,0:T(8,128)(2,1)S(1)}, bf16[2048,128]{1,0:T(8,128)(2,1)S(1)}, u32[]{:S(2)}, u32[]{:S(2)}) collective-permute-start(bf16[2048,128]{1,0:T(8,128)(2,1)S(1)} %collective-permute-done.3.refs_2_), channel_id=1, source_target_pairs={{0,1},{1,0},{2,3},{3,2},{4,5},{5,4},{6,7},{7,6},{8,9},{9,8},{10,11... | collective-permute-start | bytes 1572872 | tf_op jit(solution)/shard_map/ppermute | solution.py:371
  50.3 3.2 %collective-permute-start.14 = (bf16[48,2048]{1,0:T(8,128)(2,1)S(1)}, bf16[48,2048]{1,0:T(8,128)(2,1)S(1)}, u32[]{:S(2)}, u32[]{:S(2)}) collective-permute-start(bf16[48,2048]{1,0:T(8,128)(2,1)S(1)} %get-tuple-element.99.refs_4_), channel_id=1, source_target_pairs={{0,4},{1,5},{2,6},{3,7},{16,20},{17,21},{18,22},{19,23}} | collective-permute-start | bytes 589832 | tf_op jit(solution)/shard_map/ppermute | solution.py:439
  51.6 3.2 %collective-permute-start.13 = (bf16[48,2048]{1,0:T(8,128)(2,1)S(1)}, bf16[48,2048]{1,0:T(8,128)(2,1)S(1)}, u32[]{:S(2)}, u32[]{:S(2)}) collective-permute-start(bf16[48,2048]{1,0:T(8,128)(2,1)S(1)} %get-tuple-element.103.refs_4_), channel_id=1, source_target_pairs={{0,4},{1,5},{2,6},{3,7},{16,20},{17,21},{18,22},{19,23}} | collective-permute-start | bytes 589832 | tf_op jit(solution)/shard_map/ppermute | solution.py:439
  52.8 3.4 %collective-permute-start.17 = (bf16[48,2048]{1,0:T(8,128)(2,1)S(1)}, bf16[48,2048]{1,0:T(8,128)(2,1)S(1)}, u32[]{:S(2)}, u32[]{:S(2)}) collective-permute-start(bf16[48,2048]{1,0:T(8,128)(2,1)S(1)} %get-tuple-element.107.refs_5_), channel_id=1, source_target_pairs={{0,4},{1,5},{2,6},{3,7},{16,20},{17,21},{18,22},{19,23}} | collective-permute-start | bytes 589832 | tf_op jit(solution)/shard_map/ppermute | solution.py:439
  54.1 3.4 %collective-permute-start.16 = (bf16[48,2048]{1,0:T(8,128)(2,1)S(1)}, bf16[48,2048]{1,0:T(8,128)(2,1)S(1)}, u32[]{:S(2)}, u32[]{:S(2)}) collective-permute-start(bf16[48,2048]{1,0:T(8,128)(2,1)S(1)} %get-tuple-element.111.refs_5_), channel_id=1, source_target_pairs={{0,4},{4,8},{1,5},{5,9},{2,6},{6,10},{3,7},{7,11},{16,20},{20,24},... | collective-permute-start | bytes 589832 | tf_op jit(solution)/shard_map/ppermute | solution.py:439
  55.6 3.9 %collective-permute-start.15 = (bf16[48,2048]{1,0:T(8,128)(2,1)S(1)}, bf16[48,2048]{1,0:T(8,128)(2,1)S(1)}, u32[]{:S(2)}, u32[]{:S(2)}) collective-permute-start(bf16[48,2048]{1,0:T(8,128)(2,1)S(1)} %get-tuple-element.115.refs_5_), channel_id=1, source_target_pairs={{0,4},{4,8},{1,5},{5,9},{2,6},{6,10},{3,7},{7,11},{16,20},{20,24},... | collective-permute-start | bytes 589832 | tf_op jit(solution)/shard_map/ppermute | solution.py:439
  56.9 4.5 %collective-permute-start.20 = (bf16[48,2048]{1,0:T(8,128)(2,1)S(1)}, bf16[48,2048]{1,0:T(8,128)(2,1)S(1)}, u32[]{:S(2)}, u32[]{:S(2)}) collective-permute-start(bf16[48,2048]{1,0:T(8,128)(2,1)S(1)} %get-tuple-element.119.refs_5_), channel_id=1, source_target_pairs={{0,4},{4,8},{1,5},{5,9},{2,6},{6,10},{3,7},{7,11},{16,20},{20,24},... | collective-permute-start | bytes 589832 | tf_op jit(solution)/shard_map/ppermute | solution.py:439
  58.2 18.8 %collective-permute-start.19 = (bf16[48,2048]{1,0:T(8,128)(2,1)S(1)}, bf16[48,2048]{1,0:T(8,128)(2,1)S(1)}, u32[]{:S(2)}, u32[]{:S(2)}) collective-permute-start(bf16[48,2048]{1,0:T(8,128)(2,1)S(1)} %get-tuple-element.123.refs_5_), channel_id=1, source_target_pairs={{0,4},{4,8},{8,12},{1,5},{5,9},{9,13},{2,6},{6,10},{10,14},{3,7},{... | collective-permute-start | bytes 589832 | tf_op jit(solution)/shard_map/ppermute | solution.py:439
  60.1 21.7 %collective-permute-start.18 = (bf16[48,2048]{1,0:T(8,128)(2,1)S(1)}, bf16[48,2048]{1,0:T(8,128)(2,1)S(1)}, u32[]{:S(2)}, u32[]{:S(2)}) collective-permute-start(bf16[48,2048]{1,0:T(8,128)(2,1)S(1)} %get-tuple-element.127.refs_5_), channel_id=1, source_target_pairs={{0,4},{4,8},{8,12},{1,5},{5,9},{9,13},{2,6},{6,10},{10,14},{3,7},{... | collective-permute-start | bytes 589832 | tf_op jit(solution)/shard_map/ppermute | solution.py:439
  62.0 24.4 %collective-permute-start.23 = (bf16[48,2048]{1,0:T(8,128)(2,1)S(1)}, bf16[48,2048]{1,0:T(8,128)(2,1)S(1)}, u32[]{:S(2)}, u32[]{:S(2)}) collective-permute-start(bf16[48,2048]{1,0:T(8,128)(2,1)S(1)} %get-tuple-element.131.refs_5_), channel_id=1, source_target_pairs={{4,8},{8,12},{5,9},{9,13},{6,10},{10,14},{7,11},{11,15},{20,24},{2... | collective-permute-start | bytes 589832 | tf_op jit(solution)/shard_map/ppermute | solution.py:439
  79.6 11.4 %collective-permute-start.22 = (bf16[48,2048]{1,0:T(8,128)(2,1)S(1)}, bf16[48,2048]{1,0:T(8,128)(2,1)S(1)}, u32[]{:S(2)}, u32[]{:S(2)}) collective-permute-start(bf16[48,2048]{1,0:T(8,128)(2,1)S(1)} %get-tuple-element.135.refs_5_), channel_id=1, source_target_pairs={{4,8},{8,12},{5,9},{9,13},{6,10},{10,14},{7,11},{11,15},{20,24},{2... | collective-permute-start | bytes 589832 | tf_op jit(solution)/shard_map/ppermute | solution.py:439
  84.4 11.8 %collective-permute-start.21 = (bf16[48,2048]{1,0:T(8,128)(2,1)S(1)}, bf16[48,2048]{1,0:T(8,128)(2,1)S(1)}, u32[]{:S(2)}, u32[]{:S(2)}) collective-permute-start(bf16[48,2048]{1,0:T(8,128)(2,1)S(1)} %get-tuple-element.139.refs_5_), channel_id=1, source_target_pairs={{4,8},{8,12},{5,9},{9,13},{6,10},{10,14},{7,11},{11,15},{20,24},{2... | collective-permute-start | bytes 589832 | tf_op jit(solution)/shard_map/ppermute | solution.py:439
  89.1 11.5 %collective-permute-start.26 = (bf16[48,2048]{1,0:T(8,128)(2,1)S(1)}, bf16[48,2048]{1,0:T(8,128)(2,1)S(1)}, u32[]{:S(2)}, u32[]{:S(2)}) collective-permute-start(bf16[48,2048]{1,0:T(8,128)(2,1)S(1)} %get-tuple-element.143.refs_5_), channel_id=1, source_target_pairs={{8,12},{9,13},{10,14},{11,15},{24,28},{25,29},{26,30},{27,31}} | collective-permute-start | bytes 589832 | tf_op jit(solution)/shard_map/ppermute | solution.py:439
  93.6 10.9 %collective-permute-start.25 = (bf16[48,2048]{1,0:T(8,128)(2,1)S(1)}, bf16[48,2048]{1,0:T(8,128)(2,1)S(1)}, u32[]{:S(2)}, u32[]{:S(2)}) collective-permute-start(bf16[48,2048]{1,0:T(8,128)(2,1)S(1)} %get-tuple-element.147.refs_5_), channel_id=1, source_target_pairs={{8,12},{9,13},{10,14},{11,15},{24,28},{25,29},{26,30},{27,31}} | collective-permute-start | bytes 589832 | tf_op jit(solution)/shard_map/ppermute | solution.py:439
  98.9 9.6 %collective-permute-start.24 = (bf16[48,2048]{1,0:T(8,128)(2,1)S(1)}, bf16[48,2048]{1,0:T(8,128)(2,1)S(1)}, u32[]{:S(2)}, u32[]{:S(2)}) collective-permute-start(bf16[48,2048]{1,0:T(8,128)(2,1)S(1)} %get-tuple-element.151.refs_5_), channel_id=1, source_target_pairs={{8,12},{9,13},{10,14},{11,15},{24,28},{25,29},{26,30},{27,31}} | collective-permute-start | bytes 589832 | tf_op jit(solution)/shard_map/ppermute | solution.py:439

commit v2 on v1

v2 whole, which is shorter than its diff:
```python
import functools

import jax
import jax.numpy as jnp
from jax import lax
from jax.experimental import pallas as pl
from jax.experimental.pallas import tpu as pltpu
from jax.sharding import PartitionSpec as P

BLOCK = 128
CHARGES = 4
LANES = 128
EPSILON = 1e-06
MICRO = 48
DELAY = 3


VMEM = pl.BlockSpec(memory_space=pltpu.VMEM)
HBM = pl.BlockSpec(memory_space=pl.ANY)


def allowed_outcome(charge_ref, site, i, j):
    return (charge_ref[site + 1, j] - charge_ref[site, i]) & (CHARGES - 1)


def pick_kernel(blocks, starts, charge_ref, tensor_ref, packed_ref, *refs):
    *out_refs, both_ref = refs
    width = tensor_ref.shape[3]
    per_shard = width // BLOCK
    site = lax.axis_index("site")
    mine = lax.axis_index("sample") * per_shard
    row = lax.broadcasted_iota(jnp.int32, (2 * BLOCK, 2 * BLOCK), 0)
    col = lax.broadcasted_iota(jnp.int32, (2 * BLOCK, 2 * BLOCK), 1)
    source = jnp.where(row < BLOCK, 2 * row, 2 * (row - BLOCK) + 1)
    select = jnp.where(col == source, 1.0, 0.0).astype(jnp.bfloat16)
    both_ref[...] = select
    entry = jnp.int32(0)
    for i in range(blocks):
        pairs = tensor_ref[0, i * BLOCK : (i + 1) * BLOCK, :, :].reshape(2 * BLOCK, width)
        for j in range(per_shard):
            outcome = allowed_outcome(charge_ref, site, i, mine + j)
            start = pl.multiple_of(jnp.minimum(outcome, 1) * BLOCK, BLOCK)
            there = pl.ds(pl.multiple_of(entry * BLOCK, BLOCK), BLOCK)
            packed_ref[there, :] = jnp.dot(
                both_ref[pl.ds(start, BLOCK), :],
                pairs[:, j * BLOCK : (j + 1) * BLOCK],
                preferred_element_type=jnp.float32,
            ).astype(jnp.bfloat16)
            entry += (outcome < 2).astype(jnp.int32)
    for start, out_ref in zip(starts, out_refs):
        low = start * BLOCK
        out_ref[...] = packed_ref[low : low + out_ref.shape[0], :]


def pick(tensor, charges, spans):
    _, bond, _, width = tensor.shape
    blocks = bond // BLOCK
    total = blocks * (width // BLOCK)
    return pl.pallas_call(
        functools.partial(pick_kernel, blocks, [low for low, _ in spans]),
        out_shape=tuple(
            pltpu.VMEM((count * BLOCK, BLOCK), tensor.dtype)
            for count in (total + 1, *[high - low for low, high in spans])
        ),
        grid_spec=pltpu.PrefetchScalarGridSpec(
            num_scalar_prefetch=1,
            grid=(1,),
            in_specs=[VMEM],
            out_specs=(VMEM,) * (1 + len(spans)),
            scratch_shapes=[pltpu.VMEM((2 * BLOCK, 2 * BLOCK), jnp.bfloat16)],
        ),
        compiler_params=pltpu.CompilerParams(vmem_limit_bytes=16 * 1024 * 1024),
        cost_estimate=pl.CostEstimate(
            flops=8 * bond * width * BLOCK, bytes_accessed=6 * bond * width, transcendentals=0
        ),
    )(charges, tensor)


def plan_kernel(blocks, per_shard, cores, charge_ref, table_ref):
    shards, _ = table_ref.shape
    chips = shards // cores
    me = lax.axis_index("sample")
    site = lax.axis_index("site")
    total = blocks * per_shard
    for d in range(shards):
        chip = lax.rem(me // cores + d // cores, chips)
        first = (chip * cores + lax.rem(me + d, cores)) * per_shard

        def one(i, entry):
            for j in range(per_shard):
                table_ref[d, entry] = i * (shards * per_shard) + first + j
                allowed = allowed_outcome(charge_ref, site, i, first + j) < 2
                entry += allowed.astype(jnp.int32)
            return entry

        count = lax.fori_loop(0, blocks, one, jnp.int32(0))
        table_ref[d, total + 1] = count


def plan(charges, blocks, per_shard, cores, shards):
    size = blocks * per_shard + 2
    return pl.pallas_call(
        functools.partial(plan_kernel, blocks, per_shard, cores),
        out_shape=jax.ShapeDtypeStruct((shards, size), jnp.int32),
        grid_spec=pltpu.PrefetchScalarGridSpec(
            num_scalar_prefetch=1,
            grid=(1,),
            in_specs=[],
            out_specs=pl.BlockSpec(memory_space=pltpu.SMEM),
        ),
        compiler_params=pltpu.CompilerParams(vmem_limit_bytes=1024 * 1024),
        cost_estimate=pl.CostEstimate(flops=100, bytes_accessed=4096, transcendentals=0),
    )(charges)


def place_blocks(table_ref, d, first, ref, out_ref):
    across = out_ref.shape[1] // BLOCK
    total = table_ref.shape[1] - 2
    size = min(ref.shape[0] // BLOCK, total - first)

    def one(e, carry):
        spot = table_ref[d, first + e]
        rows = pl.ds(pl.multiple_of((spot // across) * BLOCK, BLOCK), BLOCK)
        cols = pl.ds(pl.multiple_of(lax.rem(spot, across) * BLOCK, BLOCK), BLOCK)
        out_ref[rows, cols] = ref[pl.ds(pl.multiple_of(e * BLOCK, BLOCK), BLOCK), :]
        return carry

    lax.fori_loop(0, jnp.clip(table_ref[d, total + 1] - first, 0, size), one, 0)


def unpack_kernel(pieces, extras, fresh, table_ref, *refs):
    refs = list(refs)
    held, refs = refs[: len(pieces)], refs[len(pieces) + extras + (0 if fresh else 1) :]
    out_ref, scratch = refs[0], refs[1:]
    first_site = lax.axis_index("site") == 0
    if fresh:
        out_ref[...] = jnp.zeros(out_ref.shape, out_ref.dtype)
    for ref, (d, first, kind) in zip(held, pieces):
        place = functools.partial(place_blocks, table_ref, d, first, out_ref=out_ref)
        if kind == "always":
            place(ref)
        elif kind == "rest":

            @pl.when(table_ref[d, table_ref.shape[1] - 1] > first)
            def _(ref=ref, place=place):
                spare_ref, sem = scratch
                copy = pltpu.make_async_copy(ref, spare_ref, sem)
                copy.start()
                copy.wait()
                place(spare_ref)

        else:

            @pl.when(first_site if kind == "first" else ~first_site)
            def _(ref=ref, place=place):
                place(ref)


def unpack(table, pieces, extras, weights, bond):
    fresh = weights is None
    operands = [piece[0] for piece in pieces] + list(extras)
    in_specs = [HBM if piece[3] == "rest" else VMEM for piece in pieces] + [HBM] * len(extras)
    aliases = {}
    if not fresh:
        operands.append(weights)
        in_specs.append(VMEM)
        aliases = {len(operands): 0}
    rest = [piece[0] for piece in pieces if piece[3] == "rest"]
    scratch = [pltpu.VMEM(rest[0].shape, rest[0].dtype), pltpu.SemaphoreType.DMA] if rest else []
    dtype = pieces[0][0].dtype
    return pl.pallas_call(
        functools.partial(unpack_kernel, [piece[1:] for piece in pieces], len(extras), fresh),
        out_shape=pltpu.VMEM((bond, bond), dtype),
        grid_spec=pltpu.PrefetchScalarGridSpec(
            num_scalar_prefetch=1,
            grid=(1,),
            in_specs=in_specs,
            out_specs=VMEM,
            scratch_shapes=scratch,
        ),
        input_output_aliases=aliases,
        compiler_params=pltpu.CompilerParams(vmem_limit_bytes=24 * 1024 * 1024),
        cost_estimate=pl.CostEstimate(
            flops=0,
            bytes_accessed=4 * sum(piece[0].size for piece in pieces if piece[3] != "rest"),
            transcendentals=0,
        ),
    )(table, *operands)


def blank(shape, dtype, count):
    return pl.pallas_call(
        lambda *refs: None,
        out_shape=(jax.ShapeDtypeStruct(shape, dtype),) * count,
        out_specs=(HBM,) * count,
        compiler_params=pltpu.CompilerParams(vmem_limit_bytes=1024 * 1024),
    )()


def step_kernel(chunks, at, relay, carried, ends, place_ref, right_ref, *refs):
    refs = list(refs)
    first_ref, picks_ref, left_ref = refs[:3]
    weights = refs[3 : 3 + chunks]
    refs = refs[3 + chunks :]
    received_ref = refs.pop(0) if relay else None
    if carried:
        old_ref, old_norm_ref = refs[:2]
        refs = refs[4:]
    sent_ref, norm_ref, fronts_ref, norms_ref, lhs_ref, acc_ref, sems = refs
    rows, bond = sent_ref.shape
    tile = min(bond, 512)

    def copies(back, front_ref, row_norm_ref):
        where = pl.ds(pl.multiple_of(place_ref[at - 4 * back + 2], 8), rows)
        return (
            pltpu.make_async_copy(front_ref, fronts_ref.at[where], sems.at[0]),
            pltpu.make_async_copy(row_norm_ref, norms_ref.at[where], sems.at[1]),
        )

    if carried:

        @pl.when(place_ref[at - 4 + 1] == 1)
        def _():
            for copy in copies(1, old_ref, old_norm_ref):
                copy.start()

    @pl.when(place_ref[at + 1] == 1)
    def _():
        here = pl.ds(pl.multiple_of(place_ref[at + 2], 8), rows)
        front = first_ref[here, :].astype(jnp.float32)
        if relay:
            front = jnp.where(
                place_ref[at + 3] == 0, front, received_ref[...].astype(jnp.float32)
            )
        charge = (left_ref[...] + picks_ref[here, :]) & (CHARGES - 1)
        for q in range(CHARGES):
            lhs_ref[q * rows : (q + 1) * rows, :] = jnp.where(charge == q, front, 0.0).astype(
                jnp.bfloat16
            )
        for n in range(bond // tile):
            cols = slice(n * tile, (n + 1) * tile)
            total = jnp.zeros((CHARGES * rows, tile), jnp.float32)
            low = 0
            for part in weights:
                high = low + part.shape[0]
                total += jnp.dot(
                    lhs_ref[:, low:high], part[:, cols], preferred_element_type=jnp.float32
                )
                low = high
            acc_ref[:, cols] = total

        def chosen(j):
            first = pl.multiple_of(right_ref[j] * rows, 8)
            return acc_ref[pl.ds(first, rows), j * BLOCK : (j + 1) * BLOCK]

        squares = jnp.zeros((rows, LANES), jnp.float32)
        for j in range(bond // BLOCK):
            squares += chosen(j) * chosen(j)
        norm = jnp.sqrt(jnp.sum(squares, axis=1, keepdims=True) / bond + EPSILON)
        norm_ref[...] = jnp.broadcast_to(norm, norm_ref.shape)
        for j in range(bond // BLOCK):
            sent_ref[:, j * BLOCK : (j + 1) * BLOCK] = (chosen(j) / norm).astype(sent_ref.dtype)

    if carried:

        @pl.when(place_ref[at - 4 + 1] == 1)
        def _():
            for copy in copies(1, old_ref, old_norm_ref):
                copy.wait()

    if ends:

        @pl.when(place_ref[at + 1] == 1)
        def _():
            for copy in copies(0, sent_ref, norm_ref):
                copy.start()
            for copy in copies(0, sent_ref, norm_ref):
                copy.wait()


def advance(step, ends, place, right, fronts_in, picks, left, weights, received, old, results):
    row_count, bond = fronts_in.shape
    rows = MICRO
    relay = received is not None
    carried = results is not None
    operands = [fronts_in, picks, left, *weights]
    in_specs = [VMEM] * len(operands)
    aliases = {}
    if relay:
        operands.append(received)
        in_specs.append(VMEM)
    if carried:
        operands += [*old, *results]
        in_specs += [VMEM, VMEM, HBM, HBM]
        aliases = {len(operands): 2, len(operands) + 1: 3}
    return pl.pallas_call(
        functools.partial(step_kernel, len(weights), 4 * step, relay, carried, ends),
        out_shape=(
            jax.ShapeDtypeStruct((rows, bond), jnp.bfloat16),
            jax.ShapeDtypeStruct((rows, LANES), jnp.float32),
            jax.ShapeDtypeStruct((row_count, bond), jnp.bfloat16),
            jax.ShapeDtypeStruct((row_count, LANES), jnp.float32),
        ),
        grid_spec=pltpu.PrefetchScalarGridSpec(
            num_scalar_prefetch=2,
            grid=(1,),
            in_specs=in_specs,
            out_specs=(VMEM, VMEM, HBM, HBM),
            scratch_shapes=[
                pltpu.VMEM((CHARGES * rows, bond), jnp.bfloat16),
                pltpu.VMEM((CHARGES * rows, bond), jnp.float32),
                pltpu.SemaphoreType.DMA((2,)),
            ],
        ),
        input_output_aliases=aliases,
        compiler_params=pltpu.CompilerParams(vmem_limit_bytes=24 * 1024 * 1024),
        cost_estimate=pl.CostEstimate(
            flops=2 * CHARGES * rows * bond * bond,
            bytes_accessed=2 * bond * bond,
            transcendentals=0,
        ),
    )(place, right, *operands)


def gather_weights(site_tensor, charges, extras):
    shards = lax.axis_size("sample")
    sites = lax.axis_size("site")
    groups = lax.axis_size("groups")
    cores = 2 if shards % 2 == 0 else 1
    chips = shards // cores
    bond = site_tensor.shape[1]
    blocks = bond // BLOCK
    per_shard = site_tensor.shape[3] // BLOCK
    total = blocks * per_shard
    unit = total // 16
    early, turn, cap = 6 * unit, 8 * unit, 12 * unit
    if sites == 1:
        turn = early
    spans = [(0, early), (early, turn), (turn, cap), (early, cap)]

    def to(hop, i):
        return ((i // cores - hop) % chips) * cores + i % cores

    def move(part, pairs):
        flat = [(s * shards + i, t * shards + j) for (s, i), (t, j) in pairs]
        return lax.ppermute(part, ("site", "sample"), flat)

    everyone = [(s, i) for s in range(sites) for i in range(shards)]

    def across_chips(part, up, among):
        return [
            move(part, [((s, i), (s + up, to(hop, i))) for s, i in everyone if s in among])
            for hop in range(1, chips)
        ]

    def across_cores(part):
        return lax.ppermute(part, "sample", [(i, i ^ 1) for i in range(shards)])

    def with_cores(parts, first, kind):
        pieces = []
        for hop, part in enumerate(parts, 1):
            pieces.append((part, hop * cores, first, kind))
            if cores == 2:
                pieces.append((across_cores(part), hop * cores + 1, first, kind))
        return pieces

    packed, head, detour, tail, late = pick(site_tensor, charges, spans)
    one, others = range(1), range(1, sites)
    head = across_chips(head, 0, range(sites))
    tail = across_chips(tail, 0, one)
    away = across_chips(detour, 1, one)
    late = across_chips(late, 0, others)

    table = plan(charges, blocks, per_shard, cores, shards)
    outcome = (charges[1:, None, :] - charges[:-1, :, None]) & (CHARGES - 1)
    held = jnp.sum((outcome < 2).reshape(sites, blocks, shards, per_shard), axis=(1, 3))
    mine = jnp.max(held.astype(jnp.int32)).reshape(1)
    most = mine
    for hop in range(1, groups):
        pairs = [(i, (i + hop) % groups) for i in range(groups)]
        most = jnp.maximum(most, lax.ppermute(mine, "groups", pairs))

    rest_shape = ((total - cap) * BLOCK, BLOCK)

    def send_rest(blocks):
        parts = across_chips(blocks[cap * BLOCK : total * BLOCK], 0, range(sites))
        return tuple(piece[0] for piece in with_cores(parts, cap, "rest"))

    def keep(blocks):
        return tuple(blank(rest_shape, blocks.dtype, (chips - 1) * cores))

    rest = lax.cond(most[0] > cap, send_rest, keep, packed) if chips > 1 else ()
    rest = [(part, cores + k, cap, "rest") for k, part in enumerate(rest)]

    local = [(packed, 0, 0, "always")]
    if cores == 2:
        local.append((across_cores(packed), 1, 0, "always"))
    weights = unpack(table, local, [*extras, *[piece[0] for piece in rest]], None, bond)

    home = [move(part, [((1, i), (0, i)) for i in range(shards)]) for part in away]
    (head, home), weights = lax.optimization_barrier(((head, home), weights))
    pieces = with_cores(head, 0, "always")
    pieces += with_cores(home, early, "first")
    weights = unpack(table, pieces, [], weights, bond)
    tail, weights = lax.optimization_barrier((tail, weights))
    pieces = with_cores(tail, turn, "first")
    weights = unpack(table, pieces + rest, [], weights, bond)

    def exchange(after):
        parts, after = lax.optimization_barrier((late, after))
        return with_cores(parts, early, "others")

    def complete(weights, pieces, after):
        return unpack(table, pieces, [after], weights, bond)

    return weights, exchange, complete


def pipeline(site_tensor, fronts_in, outcomes, charges):
    owner = lax.axis_index("site")
    sites = lax.axis_size("site")
    left = lax.dynamic_index_in_dim(charges, owner, 0, keepdims=False)
    right = lax.dynamic_index_in_dim(charges, owner + 1, 0, keepdims=False)
    row_count, _ = fronts_in.shape
    micro_count = row_count // MICRO
    picks = outcomes[0][:, None]
    left_lanes = jnp.repeat(left, BLOCK)[None, :]
    steps = micro_count + DELAY * (sites - 1)
    micro = jnp.arange(steps, dtype=jnp.int32) - DELAY * owner
    active = (micro >= 0) & (micro < micro_count)
    micro = jnp.clip(micro, 0, micro_count - 1)
    place = jnp.stack(
        [micro, active.astype(jnp.int32), micro * MICRO, jnp.full_like(micro, owner)], axis=1
    ).astype(jnp.int32).reshape(-1)

    weights, exchange, complete = gather_weights(site_tensor, charges, [place, picks, left_lanes, right])
    received, old, results = {}, None, None
    for step in range(steps):
        if step == DELAY - 1:
            late = exchange(old[0])
        if step == DELAY:
            weights = complete(weights, late, old[0])
        sent, norm, *results = advance(
            step, step == steps - 1, place, right, fronts_in, picks, left_lanes, [weights],
            received.pop(step - DELAY, None), old, results,
        )
        old = (sent, norm)
        pairs = [
            (s, s + 1) for s in range(sites - 1) if 0 <= step - DELAY * s < micro_count
        ]
        if pairs:
            received[step] = lax.ppermute(sent, "site", pairs)
    fronts, norms = results
    return fronts[None], jnp.log(norms[:, 0])[None]


def solution(mesh):
    in_specs = (
        P(("groups", "site"), None, None, "sample"),
        P(("groups", "sample"), None),
        P(("groups", "site"), "sample"),
        P("groups", None),
    )
    out_specs = (P(("groups", "site"), "sample", None), P(("groups", "site"), "sample"))
    return jax.shard_map(
        pipeline, mesh=mesh, in_specs=in_specs, out_specs=out_specs, check_vma=False
    )
```

time: 114 us -> 126 us (1.11)
  waiting for transfers between devices: 41.7 us -> 49.9 us
  starting transfers between devices: 20.7 us -> 24.9 us
    ppermute x14, waiting for transfers between devices: 20 us -> 25.9 us  [pipeline(): received[step] = lax.ppermute(sent, 'site', pairs)]
    ppermute x10 -> x11, starting transfers between devices: 6.08 us -> 10.3 us  [the longest x5 7.9 us: move(): return lax.ppermute(part, ('site', 'sample'), flat)]
    another operation x3 -> x0, local copies, waits for them, and re-layouts: 2.65 us -> none
    ppermute x10 -> x11, waiting for transfers between devices: 21.8 us -> 24 us  [the longest x5 22.7 us: move(): return lax.ppermute(part, ('site', 'sample'), flat)]
    unnamed x12 -> x22, local copies, waits for them, and re-layouts: 2.88 us -> 4.58 us
    pallas_call x17, Pallas kernels: 26.6 us -> 28 us  [advance(): pl.pallas_call(functools.partial(step_kernel, len(weights), 4 * step, rel...]
    pallas_call x5 -> x6, Pallas kernels: 10.6 us -> 10 us  [the longest x4 6.95 us: unpack(): pl.pallas_call(functools.partial(unpack_kernel, [piece[1:] for piece in p...]
  transfers between devices with their start and end apart: 24 -> 25, of which waited for: 14 -> 11; matrix products, arithmetic and copies ran while one was open for 4% -> 1% of each run, Pallas kernels for 28% -> 27%
where the time goes in v2:
time: 126 us; the launch traced here: 125 us
  waiting for transfers between devices  49.9 us (40%)
  Pallas kernels  41.1 us (33%)
  starting transfers between devices  24.9 us (20%)
  local copies, waits for them, and re-layouts  5.87 us (5%)
  between operations  2.34 us (2%)
    pallas_call x17, Pallas kernels, advance(): pl.pallas_call(functools.partial(step_kernel, len(weights), 4 * step, rel...  28 us
    ppermute x14, waiting for transfers between devices, pipeline(): received[step] = lax.ppermute(sent, 'site', pairs)  25.9 us
    ppermute x5, waiting for transfers between devices, move(): return lax.ppermute(part, ('site', 'sample'), flat)  22.7 us
    ppermute x14, starting transfers between devices, pipeline(): received[step] = lax.ppermute(sent, 'site', pairs)  14.6 us
    ppermute x5, starting transfers between devices, move(): return lax.ppermute(part, ('site', 'sample'), flat)  7.9 us
    pallas_call x4, Pallas kernels, unpack(): pl.pallas_call(functools.partial(unpack_kernel, [piece[1:] for piece in p...  6.95 us
    unnamed x22, local copies, waits for them, and re-layouts  4.58 us
    pallas_call x1, Pallas kernels, plan(): pl.pallas_call(functools.partial(plan_kernel, blocks, per_shard, cores),...  3.12 us
  transfers between devices with their start and end apart: 25, of which 11 were waited for; matrix products, arithmetic and copies ran while one was open for 1% of the time, Pallas kernels for 27%

profile of v2, /device:TPU:24, one launch (start us, length us, event | category | flops | bytes accessed | tf_op | source)
XLA Modules:
  0.0 125.3 jit_solution(14560506202396276687)
XLA Ops:
  0.6 2.2 %copy-done.1 = bf16[1,2048,2,512]{3,2,1,0:T(2,128)(2,1)S(1)} copy-done((bf16[1,2048,2,512]{3,2,1,0:T(2,128)(2,1)S(1)}, bf16[1,2048,2,512]{3,2,1,0:T(2,128)(2,1)}, u32[]{:S(2)}) %copy-start.1) | copy-done | bytes 4194328
  2.8 0.7 copy-done.2
  3.5 3.1 %shard_map.60 = (bf16[8320,128]{1,0:T(8,128)(2,1)S(1)}, bf16[3072,128]{1,0:T(8,128)(2,1)}, bf16[1024,128]{1,0:T(8,128)(2,1)S(1)}, bf16[2048,128]{1,0:T(8,128)(2,1)S(1)}, bf16[3072,128]{1,0:T(8,128)(2,1)S(1)}) custom-call(s32[5,16]{1,0:T(8,128)S(1)} %copy-done.2, bf16[1,2048,2,512]{3,2,1,0:T(2,128)(2,1)S(1)} %copy-done.1), custom_call_target="tpu_custom_call" | custom-call | flops 1073741824 | bytes 6291456 | tf_op jit(solution)/shard_map/pallas_call | solution.py:59
  6.6 0.9 copy-done.4
  7.5 0.8 copy-done.6
  8.3 1.4 %collective-permute-start.5 = (bf16[1024,128]{1,0:T(8,128)(2,1)S(1)}, bf16[1024,128]{1,0:T(8,128)(2,1)}, u32[]{:S(2)}, u32[]{:S(2)}) collective-permute-start(bf16[1024,128]{1,0:T(8,128)(2,1)S(1)} %get-tuple-element.85), channel_id=1, source_target_pairs={{0,6},{1,7},{2,4},{3,5},{16,22},{17,23},{18,20},{19,21}} | collective-permute-start | bytes 786440 | tf_op jit(solution)/shard_map/ppermute | solution.py:346
  9.6 1.5 %collective-permute-start.4 = (bf16[3072,128]{1,0:T(8,128)(2,1)}, bf16[3072,128]{1,0:T(8,128)(2,1)S(1)}, u32[]{:S(2)}, u32[]{:S(2)}) collective-permute-start(bf16[3072,128]{1,0:T(8,128)(2,1)} %get-tuple-element.84), channel_id=1, source_target_pairs={{0,2},{1,3},{2,0},{3,1},{4,6},{5,7},{6,4},{7,5},{8,10},{9,11},{10,... | collective-permute-start | bytes 2359304 | tf_op jit(solution)/shard_map/ppermute | solution.py:346
  11.7 0.7 reduce_max.9
  12.3 1.5 %collective-permute-start.8 = (s32[1]{0:T(128)}, s32[1]{0:T(128)}, u32[]{:S(2)}, u32[]{:S(2)}) collective-permute-start(s32[1]{0:T(128)} %bitcast.4), channel_id=1, source_target_pairs={{0,16},{16,0},{1,17},{17,1},{2,18},{18,2},{3,19},{19,3},{4,20},{20... | collective-permute-start | bytes 20 | tf_op jit(solution)/shard_map/ppermute | solution.py:381
  13.9 3.1 %shard_map.59.table_ref = s32[4,66]{1,0:T(4,128)S(1)} custom-call(s32[5,16]{1,0:T(8,128)S(1)} %copy-done.3), custom_call_target="tpu_custom_call" | custom-call | flops 100 | bytes 4096 | tf_op jit(solution)/shard_map/pallas_call | solution.py:102
  17.1 0.7 collective-permute-start.6
  19.5 3.9 %shard_map.61.refs_4_ = bf16[2048,2048]{1,0:T(8,128)(2,1)S(1)} custom-call(s32[4,66]{1,0:T(4,128)S(1)} %shard_map.59.table_ref, bf16[8320,128]{1,0:T(8,128)(2,1)S(1)} %get-tuple-element.86.refs_0_, bf16[8320,128]{1,0:T(8,128)(2,1)} %collective-permute-done.7.refs_1_, s32[68]{0:T(128)S(1)} %reshape.57.refs_2_.place_ref, s32[384,1]{1,0:T(8,128)S(1)} %copy.96.refs_3_.refs_1_, ...), custom_call_target="tpu_custom_call" | custom-call | bytes 8519680 | tf_op jit(solution)/shard_map/pallas_call | solution.py:171
  23.4 6.4 %collective-permute-done.4.refs_0_ = bf16[3072,128]{1,0:T(8,128)(2,1)S(1)} collective-permute-done((bf16[3072,128]{1,0:T(8,128)(2,1)}, bf16[3072,128]{1,0:T(8,128)(2,1)S(1)}, u32[]{:S(2)}, u32[]{:S(2)}) %collective-permute-start.4) | collective-permute-done | bytes 786464 | tf_op jit(solution)/shard_map/ppermute | solution.py:346
  29.8 0.8 collective-permute-start.3
  31.2 1.2 collective-permute-done.10.refs_3_
  32.5 1.5 %shard_map.62.refs_4_ = bf16[2048,2048]{1,0:T(8,128)(2,1)S(1)} custom-call(s32[4,66]{1,0:T(4,128)S(1)} %shard_map.59.table_ref, bf16[3072,128]{1,0:T(8,128)(2,1)S(1)} %collective-permute-done.4.refs_0_, bf16[3072,128]{1,0:T(8,128)(2,1)S(1)} %collective-permute-done.9.refs_1_, ...), custom_call_target="tpu_custom_call", output_to_operand_aliasing={{}: (5, {})} | custom-call | bytes 4194304 | tf_op jit(solution)/shard_map/pallas_call | solution.py:171
  34.4 3.5 %collective-permute-start.2 = (bf16[3072,128]{1,0:T(8,128)(2,1)S(1)}, bf16[3072,128]{1,0:T(8,128)(2,1)S(1)}, u32[]{:S(2)}, u32[]{:S(2)}) collective-permute-start(bf16[3072,128]{1,0:T(8,128)(2,1)S(1)} %copy-done.5), channel_id=1, source_target_pairs={{4,6},{5,7},{6,4},{7,5},{8,10},{9,11},{10,8},{11,9},{12,14},{13,15... | collective-permute-start | bytes 2359304 | tf_op jit(solution)/shard_map/ppermute | solution.py:346
  39.7 16.3 %collective-permute-done.2.refs_0_ = bf16[3072,128]{1,0:T(8,128)(2,1)S(1)} collective-permute-done((bf16[3072,128]{1,0:T(8,128)(2,1)S(1)}, bf16[3072,128]{1,0:T(8,128)(2,1)S(1)}, u32[]{:S(2)}, u32[]{:S(2)}) %collective-permute-start.2) | collective-permute-done | bytes 786464 | tf_op jit(solution)/shard_map/ppermute | solution.py:346
  56.0 0.7 collective-permute-start.14
  56.7 0.7 collective-permute-start.13
  58.0 0.7 collective-permute-start.17
  58.7 0.9 shard_map.67.refs_3_
  60.2 0.7 collective-permute-start.16
  60.9 0.8 shard_map.69
  61.7 0.7 collective-permute-start.15
  63.0 0.7 collective-permute-start.20
  64.3 1.3 %collective-permute-start.19 = (bf16[48,2048]{1,0:T(8,128)(2,1)S(1)}, bf16[48,2048]{1,0:T(8,128)(2,1)S(1)}, u32[]{:S(2)}, u32[]{:S(2)}) collective-permute-start(bf16[48,2048]{1,0:T(8,128)(2,1)S(1)} %get-tuple-element.119.refs_5_), channel_id=1, source_target_pairs={{0,4},{4,8},{8,12},{1,5},{5,9},{9,13},{2,6},{6,10},{10,14},{3,7},{... | collective-permute-start | bytes 589832 | tf_op jit(solution)/shard_map/ppermute | solution.py:452
  66.2 1.3 %collective-permute-start.18 = (bf16[48,2048]{1,0:T(8,128)(2,1)S(1)}, bf16[48,2048]{1,0:T(8,128)(2,1)S(1)}, u32[]{:S(2)}, u32[]{:S(2)}) collective-permute-start(bf16[48,2048]{1,0:T(8,128)(2,1)S(1)} %get-tuple-element.123.refs_5_), channel_id=1, source_target_pairs={{0,4},{4,8},{8,12},{1,5},{5,9},{9,13},{2,6},{6,10},{10,14},{3,7},{... | collective-permute-start | bytes 589832 | tf_op jit(solution)/shard_map/ppermute | solution.py:452
  68.1 1.3 %collective-permute-start.23 = (bf16[48,2048]{1,0:T(8,128)(2,1)S(1)}, bf16[48,2048]{1,0:T(8,128)(2,1)S(1)}, u32[]{:S(2)}, u32[]{:S(2)}) collective-permute-start(bf16[48,2048]{1,0:T(8,128)(2,1)S(1)} %get-tuple-element.127.refs_5_), channel_id=1, source_target_pairs={{4,8},{8,12},{5,9},{9,13},{6,10},{10,14},{7,11},{11,15},{20,24},{2... | collective-permute-start | bytes 589832 | tf_op jit(solution)/shard_map/ppermute | solution.py:452
  69.4 19.8 %collective-permute-done.19.refs_4_ = bf16[48,2048]{1,0:T(8,128)(2,1)S(1)} collective-permute-done((bf16[48,2048]{1,0:T(8,128)(2,1)S(1)}, bf16[48,2048]{1,0:T(8,128)(2,1)S(1)}, u32[]{:S(2)}, u32[]{:S(2)}) %collective-permute-start.19) | collective-permute-done | bytes 196640 | tf_op jit(solution)/shard_map/ppermute | solution.py:452
  89.2 2.6 %shard_map.74 = (bf16[48,2048]{1,0:T(8,128)(2,1)S(1)}, f32[48,128]{1,0:T(8,128)S(1)}, bf16[384,2048]{1,0:T(8,128)(2,1)}, f32[384,128]{1,0:T(8,128)S(1)}) custom-call(s32[68]{0:T(128)S(1)} %reshape.57.refs_2_.place_ref, s32[16]{0:T(128)S(1)} %get-tuple-element.164.refs_5_.right_ref, ...), custom_call_target="tpu_custom_call", output_to_operand_aliasing={{2}: (9, {}), {3}: (10, {})} | custom-call | flops 1610612736 | bytes 8388608 | tf_op jit(solution)/shard_map/pallas_call | solution.py:296
  91.8 1.3 %collective-permute-start.22 = (bf16[48,2048]{1,0:T(8,128)(2,1)S(1)}, bf16[48,2048]{1,0:T(8,128)(2,1)S(1)}, u32[]{:S(2)}, u32[]{:S(2)}) collective-permute-start(bf16[48,2048]{1,0:T(8,128)(2,1)S(1)} %get-tuple-element.131.refs_5_), channel_id=1, source_target_pairs={{4,8},{8,12},{5,9},{9,13},{6,10},{10,14},{7,11},{11,15},{20,24},{2... | collective-permute-start | bytes 589832 | tf_op jit(solution)/shard_map/ppermute | solution.py:452
  93.1 0.9 collective-permute-done.18.refs_4_
  94.0 2.7 %shard_map.75 = (bf16[48,2048]{1,0:T(8,128)(2,1)S(1)}, f32[48,128]{1,0:T(8,128)S(1)}, bf16[384,2048]{1,0:T(8,128)(2,1)}, f32[384,128]{1,0:T(8,128)S(1)}) custom-call(s32[68]{0:T(128)S(1)} %reshape.57.refs_2_.place_ref, s32[16]{0:T(128)S(1)} %get-tuple-element.164.refs_5_.right_ref, ...), custom_call_target="tpu_custom_call", output_to_operand_aliasing={{2}: (9, {}), {3}: (10, {})} | custom-call | flops 1610612736 | bytes 8388608 | tf_op jit(solution)/shard_map/pallas_call | solution.py:296
  96.6 1.5 %collective-permute-start.21 = (bf16[48,2048]{1,0:T(8,128)(2,1)S(1)}, bf16[48,2048]{1,0:T(8,128)(2,1)S(1)}, u32[]{:S(2)}, u32[]{:S(2)}) collective-permute-start(bf16[48,2048]{1,0:T(8,128)(2,1)S(1)} %get-tuple-element.135.refs_5_), channel_id=1, source_target_pairs={{4,8},{8,12},{5,9},{9,13},{6,10},{10,14},{7,11},{11,15},{20,24},{2... | collective-permute-start | bytes 589832 | tf_op jit(solution)/shard_map/ppermute | solution.py:452
  98.6 2.6 %shard_map.76 = (bf16[48,2048]{1,0:T(8,128)(2,1)S(1)}, f32[48,128]{1,0:T(8,128)S(1)}, bf16[384,2048]{1,0:T(8,128)(2,1)}, f32[384,128]{1,0:T(8,128)S(1)}) custom-call(s32[68]{0:T(128)S(1)} %reshape.57.refs_2_.place_ref, s32[16]{0:T(128)S(1)} %get-tuple-element.164.refs_5_.right_ref, ...), custom_call_target="tpu_custom_call", output_to_operand_aliasing={{2}: (9, {}), {3}: (10, {})} | custom-call | flops 1610612736 | bytes 8388608 | tf_op jit(solution)/shard_map/pallas_call | solution.py:296
  101.2 1.3 %collective-permute-start.26 = (bf16[48,2048]{1,0:T(8,128)(2,1)S(1)}, bf16[48,2048]{1,0:T(8,128)(2,1)S(1)}, u32[]{:S(2)}, u32[]{:S(2)}) collective-permute-start(bf16[48,2048]{1,0:T(8,128)(2,1)S(1)} %get-tuple-element.139.refs_5_), channel_id=1, source_target_pairs={{8,12},{9,13},{10,14},{11,15},{24,28},{25,29},{26,30},{27,31}} | collective-permute-start | bytes 589832 | tf_op jit(solution)/shard_map/ppermute | solution.py:452
  102.5 0.6 collective-permute-done.22.refs_4_
  103.2 2.6 %shard_map.77 = (bf16[48,2048]{1,0:T(8,128)(2,1)S(1)}, f32[48,128]{1,0:T(8,128)S(1)}, bf16[384,2048]{1,0:T(8,128)(2,1)}, f32[384,128]{1,0:T(8,128)S(1)}) custom-call(s32[68]{0:T(128)S(1)} %reshape.57.refs_2_.place_ref, s32[16]{0:T(128)S(1)} %get-tuple-element.164.refs_5_.right_ref, ...), custom_call_target="tpu_custom_call", output_to_operand_aliasing={{2}: (9, {}), {3}: (10, {})} | custom-call | flops 1610612736 | bytes 8388608 | tf_op jit(solution)/shard_map/pallas_call | solution.py:296
  105.8 1.3 %collective-permute-start.25 = (bf16[48,2048]{1,0:T(8,128)(2,1)S(1)}, bf16[48,2048]{1,0:T(8,128)(2,1)S(1)}, u32[]{:S(2)}, u32[]{:S(2)}) collective-permute-start(bf16[48,2048]{1,0:T(8,128)(2,1)S(1)} %get-tuple-element.143.refs_5_), channel_id=1, source_target_pairs={{8,12},{9,13},{10,14},{11,15},{24,28},{25,29},{26,30},{27,31}} | collective-permute-start | bytes 589832 | tf_op jit(solution)/shard_map/ppermute | solution.py:452
  107.1 1.0 collective-permute-done.21.refs_4_
  108.2 2.7 %shard_map.78 = (bf16[48,2048]{1,0:T(8,128)(2,1)S(1)}, f32[48,128]{1,0:T(8,128)S(1)}, bf16[384,2048]{1,0:T(8,128)(2,1)}, f32[384,128]{1,0:T(8,128)S(1)}) custom-call(s32[68]{0:T(128)S(1)} %reshape.57.refs_2_.place_ref, s32[16]{0:T(128)S(1)} %get-tuple-element.164.refs_5_.right_ref, ...), custom_call_target="tpu_custom_call", output_to_operand_aliasing={{2}: (9, {}), {3}: (10, {})} | custom-call | flops 1610612736 | bytes 8388608 | tf_op jit(solution)/shard_map/pallas_call | solution.py:296
  110.8 1.3 %collective-permute-start.24 = (bf16[48,2048]{1,0:T(8,128)(2,1)S(1)}, bf16[48,2048]{1,0:T(8,128)(2,1)S(1)}, u32[]{:S(2)}, u32[]{:S(2)}) collective-permute-start(bf16[48,2048]{1,0:T(8,128)(2,1)S(1)} %get-tuple-element.147.refs_5_), channel_id=1, source_target_pairs={{8,12},{9,13},{10,14},{11,15},{24,28},{25,29},{26,30},{27,31}} | collective-permute-start | bytes 589832 | tf_op jit(solution)/shard_map/ppermute | solution.py:452
  112.6 2.7 %shard_map.79 = (bf16[48,2048]{1,0:T(8,128)(2,1)S(1)}, f32[48,128]{1,0:T(8,128)S(1)}, bf16[384,2048]{1,0:T(8,128)(2,1)}, f32[384,128]{1,0:T(8,128)S(1)}) custom-call(s32[68]{0:T(128)S(1)} %reshape.57.refs_2_.place_ref, s32[16]{0:T(128)S(1)} %get-tuple-element.164.refs_5_.right_ref, ...), custom_call_target="tpu_custom_call", output_to_operand_aliasing={{2}: (9, {}), {3}: (10, {})} | custom-call | flops 1610612736 | bytes 8388608 | tf_op jit(solution)/shard_map/pallas_call | solution.py:296
  115.2 1.3 %collective-permute-done.25.refs_4_ = bf16[48,2048]{1,0:T(8,128)(2,1)S(1)} collective-permute-done((bf16[48,2048]{1,0:T(8,128)(2,1)S(1)}, bf16[48,2048]{1,0:T(8,128)(2,1)S(1)}, u32[]{:S(2)}, u32[]{:S(2)}) %collective-permute-start.25) | collective-permute-done | bytes 196640 | tf_op jit(solution)/shard_map/ppermute | solution.py:452
  116.5 2.6 %shard_map.80 = (bf16[48,2048]{1,0:T(8,128)(2,1)S(1)}, f32[48,128]{1,0:T(8,128)S(1)}, bf16[384,2048]{1,0:T(8,128)(2,1)}, f32[384,128]{1,0:T(8,128)S(1)}) custom-call(s32[68]{0:T(128)S(1)} %reshape.57.refs_2_.place_ref, s32[16]{0:T(128)S(1)} %get-tuple-element.164.refs_5_.right_ref, ...), custom_call_target="tpu_custom_call", output_to_operand_aliasing={{2}: (9, {}), {3}: (10, {})} | custom-call | flops 1610612736 | bytes 8388608 | tf_op jit(solution)/shard_map/pallas_call | solution.py:296
  119.2 1.4 %collective-permute-done.24.refs_4_ = bf16[48,2048]{1,0:T(8,128)(2,1)S(1)} collective-permute-done((bf16[48,2048]{1,0:T(8,128)(2,1)S(1)}, bf16[48,2048]{1,0:T(8,128)(2,1)S(1)}, u32[]{:S(2)}, u32[]{:S(2)}) %collective-permute-start.24) | collective-permute-done | bytes 196640 | tf_op jit(solution)/shard_map/ppermute | solution.py:452
  120.6 4.0 %shard_map.81 = (bf16[48,2048]{1,0:T(8,128)(2,1)}, f32[48,128]{1,0:T(8,128)}, bf16[384,2048]{1,0:T(8,128)(2,1)}, f32[384,128]{1,0:T(8,128)S(1)}) custom-call(s32[68]{0:T(128)S(1)} %reshape.57.refs_2_.place_ref, s32[16]{0:T(128)S(1)} %get-tuple-element.164.refs_5_.right_ref, ...), custom_call_target="tpu_custom_call", output_to_operand_aliasing={{2}: (9, {}), {3}: (10, {})} | custom-call | flops 1610612736 | bytes 8388608 | tf_op jit(solution)/shard_map/pallas_call | solution.py:296
  (64 shorter events, 9.0 us)
Async XLA Ops:
  0.6 2.2 %copy-start.1 = (bf16[1,2048,2,512]{3,2,1,0:T(2,128)(2,1)S(1)}, bf16[1,2048,2,512]{3,2,1,0:T(2,128)(2,1)}, u32[]{:S(2)}) copy-start(bf16[1,2048,2,512]{3,2,1,0:T(2,128)(2,1)} %tensor_ref.1) | copy-start | bytes 12582916
  2.8 0.7 copy-start.2
  3.5 10.3 %copy-start.3 = (s32[5,16]{1,0:T(8,128)S(1)}, s32[5,16]{1,0:T(8,128)}, u32[]{:S(2)}) copy-start(s32[5,16]{1,0:T(8,128)} %charge_ref.3) | copy-start | bytes 964
  3.5 14.5 %copy-start.12 = (s32[1,384]{1,0:T(1,128)S(1)}, s32[1,384]{1,0:T(1,128)}, u32[]{:S(2)}) copy-start(s32[1,384]{1,0:T(1,128)} %param.8) | copy-start | bytes 4612
  6.6 0.9 copy-start.4
  7.5 0.8 copy-start.6
  8.3 11.2 %collective-permute-start.7 = (bf16[8320,128]{1,0:T(8,128)(2,1)S(1)}, bf16[8320,128]{1,0:T(8,128)(2,1)}, u32[]{:S(2)}, u32[]{:S(2)}) collective-permute-start(bf16[8320,128]{1,0:T(8,128)(2,1)S(1)} %get-tuple-element.86.refs_0_), channel_id=1, source_target_pairs={{0,1},{1,0},{2,3},{3,2},{4,5},{5,4},{6,7},{7,6},{8,9},{9,8},{10,11... | collective-permute-start | bytes 6389768 | tf_op jit(solution)/shard_map/ppermute | solution.py:357
  8.3 8.8 %collective-permute-start.5 = (bf16[1024,128]{1,0:T(8,128)(2,1)S(1)}, bf16[1024,128]{1,0:T(8,128)(2,1)}, u32[]{:S(2)}, u32[]{:S(2)}) collective-permute-start(bf16[1024,128]{1,0:T(8,128)(2,1)S(1)} %get-tuple-element.85), channel_id=1, source_target_pairs={{0,6},{1,7},{2,4},{3,5},{16,22},{17,23},{18,20},{19,21}} | collective-permute-start | bytes 786440 | tf_op jit(solution)/shard_map/ppermute | solution.py:346
  9.6 20.2 %collective-permute-start.4 = (bf16[3072,128]{1,0:T(8,128)(2,1)}, bf16[3072,128]{1,0:T(8,128)(2,1)S(1)}, u32[]{:S(2)}, u32[]{:S(2)}) collective-permute-start(bf16[3072,128]{1,0:T(8,128)(2,1)} %get-tuple-element.84), channel_id=1, source_target_pairs={{0,2},{1,3},{2,0},{3,1},{4,6},{5,7},{6,4},{7,5},{8,10},{9,11},{10,... | collective-permute-start | bytes 2359304 | tf_op jit(solution)/shard_map/ppermute | solution.py:346
  12.3 5.9 %collective-permute-start.8 = (s32[1]{0:T(128)}, s32[1]{0:T(128)}, u32[]{:S(2)}, u32[]{:S(2)}) collective-permute-start(s32[1]{0:T(128)} %bitcast.4), channel_id=1, source_target_pairs={{0,16},{16,0},{1,17},{17,1},{2,18},{18,2},{3,19},{19,3},{4,20},{20... | collective-permute-start | bytes 20 | tf_op jit(solution)/shard_map/ppermute | solution.py:381
  17.1 6.3 %collective-permute-start.6 = (bf16[1024,128]{1,0:T(8,128)(2,1)}, bf16[1024,128]{1,0:T(8,128)(2,1)S(1)}, u32[]{:S(2)}, u32[]{:S(2)}) collective-permute-start(bf16[1024,128]{1,0:T(8,128)(2,1)} %collective-permute-done.5), channel_id=1, source_target_pairs={{4,0},{5,1},{6,2},{7,3},{20,16},{21,17},{22,18},{23,19}} | collective-permute-start | bytes 786440 | tf_op jit(solution)/shard_map/ppermute | solution.py:346
  19.5 10.3 %copy-start.7 = (bf16[2048,128]{1,0:T(8,128)(2,1)S(1)}, bf16[2048,128]{1,0:T(8,128)(2,1)}, u32[]{:S(2)}) copy-start(bf16[2048,128]{1,0:T(8,128)(2,1)} %copy-done.6) | copy-start | bytes 1572868
  29.8 2.7 %collective-permute-start.9 = (bf16[3072,128]{1,0:T(8,128)(2,1)S(1)}, bf16[3072,128]{1,0:T(8,128)(2,1)S(1)}, u32[]{:S(2)}, u32[]{:S(2)}) collective-permute-start(bf16[3072,128]{1,0:T(8,128)(2,1)S(1)} %collective-permute-done.4.refs_0_), channel_id=1, source_target_pairs={{0,1},{1,0},{2,3},{3,2},{4,5},{5,4},{6,7},{7,6},{8,9},{9,8},{10,11... | collective-permute-start | bytes 2359304 | tf_op jit(solution)/shard_map/ppermute | solution.py:357
  29.8 4.5 %copy-start.5 = (bf16[3072,128]{1,0:T(8,128)(2,1)S(1)}, bf16[3072,128]{1,0:T(8,128)(2,1)}, u32[]{:S(2)}) copy-start(bf16[3072,128]{1,0:T(8,128)(2,1)} %copy-done.4) | copy-start | bytes 2359300
  29.8 8.1 %copy-start.9 = (bf16[2048,128]{1,0:T(8,128)(2,1)S(1)}, bf16[2048,128]{1,0:T(8,128)(2,1)}, u32[]{:S(2)}) copy-start(bf16[2048,128]{1,0:T(8,128)(2,1)} %get-tuple-element.87.refs_6_.refs_2_) | copy-start | bytes 1572868
  29.8 8.1 %copy-start.11 = (bf16[2048,128]{1,0:T(8,128)(2,1)S(1)}, bf16[2048,128]{1,0:T(8,128)(2,1)}, u32[]{:S(2)}) copy-start(bf16[2048,128]{1,0:T(8,128)(2,1)} %get-tuple-element.88.refs_7_.refs_3_) | copy-start | bytes 1572868
  29.8 4.1 %collective-permute-start.3 = (bf16[2048,128]{1,0:T(8,128)(2,1)S(1)}, bf16[2048,128]{1,0:T(8,128)(2,1)S(1)}, u32[]{:S(2)}, u32[]{:S(2)}) collective-permute-start(bf16[2048,128]{1,0:T(8,128)(2,1)S(1)} %copy-done.7), channel_id=1, source_target_pairs={{0,2},{1,3},{2,0},{3,1},{16,18},{17,19},{18,16},{19,17}} | collective-permute-start | bytes 1572872 | tf_op jit(solution)/shard_map/ppermute | solution.py:346
  30.7 1.8 %collective-permute-start.10 = (bf16[1024,128]{1,0:T(8,128)(2,1)S(1)}, bf16[1024,128]{1,0:T(8,128)(2,1)S(1)}, u32[]{:S(2)}, u32[]{:S(2)}) collective-permute-start(bf16[1024,128]{1,0:T(8,128)(2,1)S(1)} %collective-permute-done.6.refs_2_), channel_id=1, source_target_pairs={{0,1},{1,0},{2,3},{3,2},{4,5},{5,4},{6,7},{7,6},{8,9},{9,8},{10,11... | collective-permute-start | bytes 786440 | tf_op jit(solution)/shard_map/ppermute | solution.py:357
  34.0 3.9 %collective-permute-start.11 = (bf16[2048,128]{1,0:T(8,128)(2,1)S(1)}, bf16[2048,128]{1,0:T(8,128)(2,1)S(1)}, u32[]{:S(2)}, u32[]{:S(2)}) collective-permute-start(bf16[2048,128]{1,0:T(8,128)(2,1)S(1)} %collective-permute-done.3.refs_0_), channel_id=1, source_target_pairs={{0,1},{1,0},{2,3},{3,2},{4,5},{5,4},{6,7},{7,6},{8,9},{9,8},{10,11... | collective-permute-start | bytes 1572872 | tf_op jit(solution)/shard_map/ppermute | solution.py:357
  34.4 4.2 %copy-start = (bf16[384,2048]{1,0:T(8,128)(2,1)S(1)}, bf16[384,2048]{1,0:T(8,128)(2,1)}, u32[]{:S(2)}) copy-start(bf16[384,2048]{1,0:T(8,128)(2,1)} %refs_0_.33) | copy-start | bytes 4718596
  34.4 21.7 %collective-permute-start.2 = (bf16[3072,128]{1,0:T(8,128)(2,1)S(1)}, bf16[3072,128]{1,0:T(8,128)(2,1)S(1)}, u32[]{:S(2)}, u32[]{:S(2)}) collective-permute-start(bf16[3072,128]{1,0:T(8,128)(2,1)S(1)} %copy-done.5), channel_id=1, source_target_pairs={{4,6},{5,7},{6,4},{7,5},{8,10},{9,11},{10,8},{11,9},{12,14},{13,15... | collective-permute-start | bytes 2359304 | tf_op jit(solution)/shard_map/ppermute | solution.py:346
  56.0 2.6 %collective-permute-start.12 = (bf16[3072,128]{1,0:T(8,128)(2,1)S(1)}, bf16[3072,128]{1,0:T(8,128)(2,1)S(1)}, u32[]{:S(2)}, u32[]{:S(2)}) collective-permute-start(bf16[3072,128]{1,0:T(8,128)(2,1)S(1)} %collective-permute-done.2.refs_0_), channel_id=1, source_target_pairs={{0,1},{1,0},{2,3},{3,2},{4,5},{5,4},{6,7},{7,6},{8,9},{9,8},{10,11... | collective-permute-start | bytes 2359304 | tf_op jit(solution)/shard_map/ppermute | solution.py:357
  56.0 3.6 %collective-permute-start.14 = (bf16[48,2048]{1,0:T(8,128)(2,1)S(1)}, bf16[48,2048]{1,0:T(8,128)(2,1)S(1)}, u32[]{:S(2)}, u32[]{:S(2)}) collective-permute-start(bf16[48,2048]{1,0:T(8,128)(2,1)S(1)} %get-tuple-element.94.refs_4_), channel_id=1, source_target_pairs={{0,4},{1,5},{2,6},{3,7},{16,20},{17,21},{18,22},{19,23}} | collective-permute-start | bytes 589832 | tf_op jit(solution)/shard_map/ppermute | solution.py:452
  56.7 4.2 %collective-permute-start.13 = (bf16[48,2048]{1,0:T(8,128)(2,1)S(1)}, bf16[48,2048]{1,0:T(8,128)(2,1)S(1)}, u32[]{:S(2)}, u32[]{:S(2)}) collective-permute-start(bf16[48,2048]{1,0:T(8,128)(2,1)S(1)} %get-tuple-element.98.refs_4_), channel_id=1, source_target_pairs={{0,4},{1,5},{2,6},{3,7},{16,20},{17,21},{18,22},{19,23}} | collective-permute-start | bytes 589832 | tf_op jit(solution)/shard_map/ppermute | solution.py:452
  58.0 4.4 %collective-permute-start.17 = (bf16[48,2048]{1,0:T(8,128)(2,1)S(1)}, bf16[48,2048]{1,0:T(8,128)(2,1)S(1)}, u32[]{:S(2)}, u32[]{:S(2)}) collective-permute-start(bf16[48,2048]{1,0:T(8,128)(2,1)S(1)} %get-tuple-element.103.refs_2_.refs_5_), channel_id=1, source_target_pairs={{0,4},{1,5},{2,6},{3,7},{16,20},{17,21},{18,22},{19,23}} | collective-permute-start | bytes 589832 | tf_op jit(solution)/shard_map/ppermute | solution.py:452
  60.2 3.4 %collective-permute-start.16 = (bf16[48,2048]{1,0:T(8,128)(2,1)S(1)}, bf16[48,2048]{1,0:T(8,128)(2,1)S(1)}, u32[]{:S(2)}, u32[]{:S(2)}) collective-permute-start(bf16[48,2048]{1,0:T(8,128)(2,1)S(1)} %get-tuple-element.107.refs_5_), channel_id=1, source_target_pairs={{0,4},{4,8},{1,5},{5,9},{2,6},{6,10},{3,7},{7,11},{16,20},{20,24},... | collective-permute-start | bytes 589832 | tf_op jit(solution)/shard_map/ppermute | solution.py:452
  61.7 3.9 %collective-permute-start.15 = (bf16[48,2048]{1,0:T(8,128)(2,1)S(1)}, bf16[48,2048]{1,0:T(8,128)(2,1)S(1)}, u32[]{:S(2)}, u32[]{:S(2)}) collective-permute-start(bf16[48,2048]{1,0:T(8,128)(2,1)S(1)} %get-tuple-element.111.refs_5_), channel_id=1, source_target_pairs={{0,4},{4,8},{1,5},{5,9},{2,6},{6,10},{3,7},{7,11},{16,20},{20,24},... | collective-permute-start | bytes 589832 | tf_op jit(solution)/shard_map/ppermute | solution.py:452
  63.0 4.5 %collective-permute-start.20 = (bf16[48,2048]{1,0:T(8,128)(2,1)S(1)}, bf16[48,2048]{1,0:T(8,128)(2,1)S(1)}, u32[]{:S(2)}, u32[]{:S(2)}) collective-permute-start(bf16[48,2048]{1,0:T(8,128)(2,1)S(1)} %get-tuple-element.115.refs_5_), channel_id=1, source_target_pairs={{0,4},{4,8},{1,5},{5,9},{2,6},{6,10},{3,7},{7,11},{16,20},{20,24},... | collective-permute-start | bytes 589832 | tf_op jit(solution)/shard_map/ppermute | solution.py:452
  64.3 24.9 %collective-permute-start.19 = (bf16[48,2048]{1,0:T(8,128)(2,1)S(1)}, bf16[48,2048]{1,0:T(8,128)(2,1)S(1)}, u32[]{:S(2)}, u32[]{:S(2)}) collective-permute-start(bf16[48,2048]{1,0:T(8,128)(2,1)S(1)} %get-tuple-element.119.refs_5_), channel_id=1, source_target_pairs={{0,4},{4,8},{8,12},{1,5},{5,9},{9,13},{2,6},{6,10},{10,14},{3,7},{... | collective-permute-start | bytes 589832 | tf_op jit(solution)/shard_map/ppermute | solution.py:452
  66.2 27.8 %collective-permute-start.18 = (bf16[48,2048]{1,0:T(8,128)(2,1)S(1)}, bf16[48,2048]{1,0:T(8,128)(2,1)S(1)}, u32[]{:S(2)}, u32[]{:S(2)}) collective-permute-start(bf16[48,2048]{1,0:T(8,128)(2,1)S(1)} %get-tuple-element.123.refs_5_), channel_id=1, source_target_pairs={{0,4},{4,8},{8,12},{1,5},{5,9},{9,13},{2,6},{6,10},{10,14},{3,7},{... | collective-permute-start | bytes 589832 | tf_op jit(solution)/shard_map/ppermute | solution.py:452
  68.1 30.5 %collective-permute-start.23 = (bf16[48,2048]{1,0:T(8,128)(2,1)S(1)}, bf16[48,2048]{1,0:T(8,128)(2,1)S(1)}, u32[]{:S(2)}, u32[]{:S(2)}) collective-permute-start(bf16[48,2048]{1,0:T(8,128)(2,1)S(1)} %get-tuple-element.127.refs_5_), channel_id=1, source_target_pairs={{4,8},{8,12},{5,9},{9,13},{6,10},{10,14},{7,11},{11,15},{20,24},{2... | collective-permute-start | bytes 589832 | tf_op jit(solution)/shard_map/ppermute | solution.py:452
  91.8 11.4 %collective-permute-start.22 = (bf16[48,2048]{1,0:T(8,128)(2,1)S(1)}, bf16[48,2048]{1,0:T(8,128)(2,1)S(1)}, u32[]{:S(2)}, u32[]{:S(2)}) collective-permute-start(bf16[48,2048]{1,0:T(8,128)(2,1)S(1)} %get-tuple-element.131.refs_5_), channel_id=1, source_target_pairs={{4,8},{8,12},{5,9},{9,13},{6,10},{10,14},{7,11},{11,15},{20,24},{2... | collective-permute-start | bytes 589832 | tf_op jit(solution)/shard_map/ppermute | solution.py:452
  96.6 11.5 %collective-permute-start.21 = (bf16[48,2048]{1,0:T(8,128)(2,1)S(1)}, bf16[48,2048]{1,0:T(8,128)(2,1)S(1)}, u32[]{:S(2)}, u32[]{:S(2)}) collective-permute-start(bf16[48,2048]{1,0:T(8,128)(2,1)S(1)} %get-tuple-element.135.refs_5_), channel_id=1, source_target_pairs={{4,8},{8,12},{5,9},{9,13},{6,10},{10,14},{7,11},{11,15},{20,24},{2... | collective-permute-start | bytes 589832 | tf_op jit(solution)/shard_map/ppermute | solution.py:452
  101.2 11.3 %collective-permute-start.26 = (bf16[48,2048]{1,0:T(8,128)(2,1)S(1)}, bf16[48,2048]{1,0:T(8,128)(2,1)S(1)}, u32[]{:S(2)}, u32[]{:S(2)}) collective-permute-start(bf16[48,2048]{1,0:T(8,128)(2,1)S(1)} %get-tuple-element.139.refs_5_), channel_id=1, source_target_pairs={{8,12},{9,13},{10,14},{11,15},{24,28},{25,29},{26,30},{27,31}} | collective-permute-start | bytes 589832 | tf_op jit(solution)/shard_map/ppermute | solution.py:452
  105.8 10.7 %collective-permute-start.25 = (bf16[48,2048]{1,0:T(8,128)(2,1)S(1)}, bf16[48,2048]{1,0:T(8,128)(2,1)S(1)}, u32[]{:S(2)}, u32[]{:S(2)}) collective-permute-start(bf16[48,2048]{1,0:T(8,128)(2,1)S(1)} %get-tuple-element.143.refs_5_), channel_id=1, source_target_pairs={{8,12},{9,13},{10,14},{11,15},{24,28},{25,29},{26,30},{27,31}} | collective-permute-start | bytes 589832 | tf_op jit(solution)/shard_map/ppermute | solution.py:452
  110.8 9.8 %collective-permute-start.24 = (bf16[48,2048]{1,0:T(8,128)(2,1)S(1)}, bf16[48,2048]{1,0:T(8,128)(2,1)S(1)}, u32[]{:S(2)}, u32[]{:S(2)}) collective-permute-start(bf16[48,2048]{1,0:T(8,128)(2,1)S(1)} %get-tuple-element.147.refs_5_), channel_id=1, source_target_pairs={{8,12},{9,13},{10,14},{11,15},{24,28},{25,29},{26,30},{27,31}} | collective-permute-start | bytes 589832 | tf_op jit(solution)/shard_map/ppermute | solution.py:452

commit v3 on v2

--- a/solution.py
+++ b/solution.py
@@ -10,6 +10,7 @@
 BLOCK = 128
 CHARGES = 4
 LANES = 128
+SHIFT = 12
 EPSILON = 1e-06
 MICRO = 48
 DELAY = 3
@@ -88,7 +89,7 @@
 
         def one(i, entry):
             for j in range(per_shard):
-                table_ref[d, entry] = i * (shards * per_shard) + first + j
+                table_ref[d, entry] = (i << SHIFT) + first + j
                 allowed = allowed_outcome(charge_ref, site, i, first + j) < 2
                 entry += allowed.astype(jnp.int32)
             return entry
@@ -114,14 +115,13 @@
 
 
 def place_blocks(table_ref, d, first, ref, out_ref):
-    across = out_ref.shape[1] // BLOCK
     total = table_ref.shape[1] - 2
     size = min(ref.shape[0] // BLOCK, total - first)
 
     def one(e, carry):
         spot = table_ref[d, first + e]
-        rows = pl.ds(pl.multiple_of((spot // across) * BLOCK, BLOCK), BLOCK)
-        cols = pl.ds(pl.multiple_of(lax.rem(spot, across) * BLOCK, BLOCK), BLOCK)
+        rows = pl.ds(pl.multiple_of((spot >> SHIFT) * BLOCK, BLOCK), BLOCK)
+        cols = pl.ds(pl.multiple_of((spot & ((1 << SHIFT) - 1)) * BLOCK, BLOCK), BLOCK)
         out_ref[rows, cols] = ref[pl.ds(pl.multiple_of(e * BLOCK, BLOCK), BLOCK), :]
         return carry
 
@@ -197,7 +197,7 @@
     )()
 
 
-def step_kernel(chunks, at, relay, carried, ends, place_ref, right_ref, *refs):
+def step_kernel(chunks, step, relay, carried, ends, right_ref, *refs):
     refs = list(refs)
     first_ref, picks_ref, left_ref = refs[:3]
     weights = refs[3 : 3 + chunks]
@@ -208,10 +208,17 @@
         refs = refs[4:]
     sent_ref, norm_ref, fronts_ref, norms_ref, lhs_ref, acc_ref, sems = refs
     rows, bond = sent_ref.shape
+    site = lax.axis_index("site")
+    micro = step - DELAY * site
+    micro_count = first_ref.shape[0] // rows
+
+    def active(back):
+        return (micro >= back) & (micro < micro_count + back)
+
     tile = min(bond, 512)
 
     def copies(back, front_ref, row_norm_ref):
-        where = pl.ds(pl.multiple_of(place_ref[at - 4 * back + 2], 8), rows)
+        where = pl.ds(pl.multiple_of((micro - back) * rows, 8), rows)
         return (
             pltpu.make_async_copy(front_ref, fronts_ref.at[where], sems.at[0]),
             pltpu.make_async_copy(row_norm_ref, norms_ref.at[where], sems.at[1]),
@@ -219,19 +226,17 @@
 
     if carried:
 
-        @pl.when(place_ref[at - 4 + 1] == 1)
+        @pl.when(active(1))
         def _():
             for copy in copies(1, old_ref, old_norm_ref):
                 copy.start()
 
-    @pl.when(place_ref[at + 1] == 1)
+    @pl.when(active(0))
     def _():
-        here = pl.ds(pl.multiple_of(place_ref[at + 2], 8), rows)
+        here = pl.ds(pl.multiple_of(micro * rows, 8), rows)
         front = first_ref[here, :].astype(jnp.float32)
         if relay:
-            front = jnp.where(
-                place_ref[at + 3] == 0, front, received_ref[...].astype(jnp.float32)
-            )
+            front = jnp.where(site == 0, front, received_ref[...].astype(jnp.float32))
         charge = (left_ref[...] + picks_ref[here, :]) & (CHARGES - 1)
         for q in range(CHARGES):
             lhs_ref[q * rows : (q + 1) * rows, :] = jnp.where(charge == q, front, 0.0).astype(
@@ -263,14 +268,14 @@
 
     if carried:
 
-        @pl.when(place_ref[at - 4 + 1] == 1)
+        @pl.when(active(1))
         def _():
             for copy in copies(1, old_ref, old_norm_ref):
                 copy.wait()
 
     if ends:
 
-        @pl.when(place_ref[at + 1] == 1)
+        @pl.when(active(0))
         def _():
             for copy in copies(0, sent_ref, norm_ref):
                 copy.start()
@@ -278,7 +283,7 @@
                 copy.wait()
 
 
-def advance(step, ends, place, right, fronts_in, picks, left, weights, received, old, results):
+def advance(step, ends, right, fronts_in, picks, left, weights, received, old, results):
     row_count, bond = fronts_in.shape
     rows = MICRO
     relay = received is not None
@@ -292,9 +297,9 @@
     if carried:
         operands += [*old, *results]
         in_specs += [VMEM, VMEM, HBM, HBM]
-        aliases = {len(operands): 2, len(operands) + 1: 3}
+        aliases = {len(operands) - 1: 2, len(operands): 3}
     return pl.pallas_call(
-        functools.partial(step_kernel, len(weights), 4 * step, relay, carried, ends),
+        functools.partial(step_kernel, len(weights), step, relay, carried, ends),
         out_shape=(
             jax.ShapeDtypeStruct((rows, bond), jnp.bfloat16),
             jax.ShapeDtypeStruct((rows, LANES), jnp.float32),
@@ -302,7 +307,7 @@
             jax.ShapeDtypeStruct((row_count, LANES), jnp.float32),
         ),
         grid_spec=pltpu.PrefetchScalarGridSpec(
-            num_scalar_prefetch=2,
+            num_scalar_prefetch=1,
             grid=(1,),
             in_specs=in_specs,
             out_specs=(VMEM, VMEM, HBM, HBM),
@@ -319,7 +324,7 @@
             bytes_accessed=2 * bond * bond,
             transcendentals=0,
         ),
-    )(place, right, *operands)
+    )(right, *operands)
 
 
 def gather_weights(site_tensor, charges, extras):
@@ -333,7 +338,7 @@
     per_shard = site_tensor.shape[3] // BLOCK
     total = blocks * per_shard
     unit = total // 16
-    early, turn, cap = 6 * unit, 8 * unit, 12 * unit
+    early, turn, cap = 6 * unit, 6 * unit + 3 * unit, 12 * unit
     if sites == 1:
         turn = early
     spans = [(0, early), (early, turn), (turn, cap), (early, cap)]
@@ -365,10 +370,10 @@
         return pieces
 
     packed, head, detour, tail, late = pick(site_tensor, charges, spans)
-    one, others = range(1), range(1, sites)
+    one, others, relay = range(1), range(1, sites), min(3, sites - 1)
     head = across_chips(head, 0, range(sites))
     tail = across_chips(tail, 0, one)
-    away = across_chips(detour, 1, one)
+    away = across_chips(detour, relay, one)
     late = across_chips(late, 0, others)
 
     table = plan(charges, blocks, per_shard, cores, shards)
@@ -397,13 +402,13 @@
         local.append((across_cores(packed), 1, 0, "always"))
     weights = unpack(table, local, [*extras, *[piece[0] for piece in rest]], None, bond)
 
-    home = [move(part, [((1, i), (0, i)) for i in range(shards)]) for part in away]
-    (head, home), weights = lax.optimization_barrier(((head, home), weights))
+    home = [move(part, [((relay, i), (0, i)) for i in range(shards)]) for part in away]
+    head, weights = lax.optimization_barrier((head, weights))
     pieces = with_cores(head, 0, "always")
-    pieces += with_cores(home, early, "first")
     weights = unpack(table, pieces, [], weights, bond)
-    tail, weights = lax.optimization_barrier((tail, weights))
-    pieces = with_cores(tail, turn, "first")
+    (tail, home), weights = lax.optimization_barrier(((tail, home), weights))
+    pieces = with_cores(home, early, "first")
+    pieces += with_cores(tail, turn, "first")
     weights = unpack(table, pieces + rest, [], weights, bond)
 
     def exchange(after):
@@ -426,14 +431,7 @@
     picks = outcomes[0][:, None]
     left_lanes = jnp.repeat(left, BLOCK)[None, :]
     steps = micro_count + DELAY * (sites - 1)
-    micro = jnp.arange(steps, dtype=jnp.int32) - DELAY * owner
-    active = (micro >= 0) & (micro < micro_count)
-    micro = jnp.clip(micro, 0, micro_count - 1)
-    place = jnp.stack(
-        [micro, active.astype(jnp.int32), micro * MICRO, jnp.full_like(micro, owner)], axis=1
-    ).astype(jnp.int32).reshape(-1)
-
-    weights, exchange, complete = gather_weights(site_tensor, charges, [place, picks, left_lanes, right])
+    weights, exchange, complete = gather_weights(site_tensor, charges, [picks, left_lanes, right])
     received, old, results = {}, None, None
     for step in range(steps):
         if step == DELAY - 1:
@@ -441,7 +439,7 @@
         if step == DELAY:
             weights = complete(weights, late, old[0])
         sent, norm, *results = advance(
-            step, step == steps - 1, place, right, fronts_in, picks, left_lanes, [weights],
+            step, step == steps - 1, right, fronts_in, picks, left_lanes, [weights],
             received.pop(step - DELAY, None), old, results,
         )
         old = (sent, norm)

time: 126 us -> 129 us (1.024)
  waiting for transfers between devices: 49.9 us -> 54.6 us
    ppermute x5, waiting for transfers between devices: 22.7 us -> 34.1 us  [move(): return lax.ppermute(part, ('site', 'sample'), flat)]
    ppermute x14, waiting for transfers between devices: 25.9 us -> 18.8 us  [pipeline(): received[step] = lax.ppermute(sent, 'site', pairs)]
    unnamed x22 -> x18, local copies, waits for them, and re-layouts: 4.58 us -> 4.53 us
  transfers between devices with their start and end apart: 25 -> 25, of which waited for: 11 -> 14; matrix products, arithmetic and copies ran while one was open for 1% -> 1% of each run, Pallas kernels for 27% -> 26%
where the time goes in v3:
time: 129 us
  waiting for transfers between devices  54.6 us (42%)
  Pallas kernels  40.5 us (31%)
  starting transfers between devices  24.6 us (19%)
  local copies, waits for them, and re-layouts  5.56 us (4%)
  between operations  2.4 us (2%)
    ppermute x5, waiting for transfers between devices, move(): return lax.ppermute(part, ('site', 'sample'), flat)  34.1 us
    pallas_call x17, Pallas kernels, advance(): pl.pallas_call(functools.partial(step_kernel, len(weights), step, relay,...  28.2 us
    ppermute x14, waiting for transfers between devices, pipeline(): received[step] = lax.ppermute(sent, 'site', pairs)  18.8 us
    ppermute x14, starting transfers between devices, pipeline(): received[step] = lax.ppermute(sent, 'site', pairs)  14.4 us
    ppermute x5, starting transfers between devices, move(): return lax.ppermute(part, ('site', 'sample'), flat)  8.16 us
    pallas_call x4, Pallas kernels, unpack(): pl.pallas_call(functools.partial(unpack_kernel, [piece[1:] for piece in p...  6.17 us
    unnamed x18, local copies, waits for them, and re-layouts  4.53 us
    pallas_call x1, Pallas kernels, plan(): pl.pallas_call(functools.partial(plan_kernel, blocks, per_shard, cores),...  3.12 us
  transfers between devices with their start and end apart: 25, of which 14 were waited for; matrix products, arithmetic and copies ran while one was open for 1% of the time, Pallas kernels for 26%

profile of v3, /device:TPU:24, one launch (start us, length us, event | category | flops | bytes accessed | tf_op | source)
XLA Modules:
  0.0 128.8 jit_solution(13231413489031632184)
XLA Ops:
  0.6 2.2 %copy-done.1 = bf16[1,2048,2,512]{3,2,1,0:T(2,128)(2,1)S(1)} copy-done((bf16[1,2048,2,512]{3,2,1,0:T(2,128)(2,1)S(1)}, bf16[1,2048,2,512]{3,2,1,0:T(2,128)(2,1)}, u32[]{:S(2)}) %copy-start.1) | copy-done | bytes 4194328
  2.8 0.7 copy-done.2
  3.5 3.0 %shard_map.60 = (bf16[8320,128]{1,0:T(8,128)(2,1)S(1)}, bf16[3072,128]{1,0:T(8,128)(2,1)}, bf16[1536,128]{1,0:T(8,128)(2,1)S(1)}, bf16[1536,128]{1,0:T(8,128)(2,1)S(1)}, bf16[3072,128]{1,0:T(8,128)(2,1)S(1)}) custom-call(s32[5,16]{1,0:T(8,128)S(1)} %copy-done.2, bf16[1,2048,2,512]{3,2,1,0:T(2,128)(2,1)S(1)} %copy-done.1), custom_call_target="tpu_custom_call" | custom-call | flops 1073741824 | bytes 6291456 | tf_op jit(solution)/shard_map/pallas_call | solution.py:60
  6.5 0.9 copy-done.4
  7.4 0.8 copy-done.6
  8.2 1.5 %collective-permute-start.6 = (bf16[3072,128]{1,0:T(8,128)(2,1)}, bf16[3072,128]{1,0:T(8,128)(2,1)S(1)}, u32[]{:S(2)}, u32[]{:S(2)}) collective-permute-start(bf16[3072,128]{1,0:T(8,128)(2,1)} %get-tuple-element.85), channel_id=1, source_target_pairs={{0,2},{1,3},{2,0},{3,1},{4,6},{5,7},{6,4},{7,5},{8,10},{9,11},{10,... | collective-permute-start | bytes 2359304 | tf_op jit(solution)/shard_map/ppermute | solution.py:351
  10.8 1.5 %collective-permute-start.8 = (s32[1]{0:T(128)}, s32[1]{0:T(128)}, u32[]{:S(2)}, u32[]{:S(2)}) collective-permute-start(s32[1]{0:T(128)} %bitcast.4), channel_id=1, source_target_pairs={{0,16},{16,0},{1,17},{17,1},{2,18},{18,2},{3,19},{19,3},{4,20},{20... | collective-permute-start | bytes 20 | tf_op jit(solution)/shard_map/ppermute | solution.py:386
  12.4 3.1 %shard_map.59.table_ref = s32[4,66]{1,0:T(4,128)S(1)} custom-call(s32[5,16]{1,0:T(8,128)S(1)} %copy-done.3), custom_call_target="tpu_custom_call" | custom-call | flops 100 | bytes 4096 | tf_op jit(solution)/shard_map/pallas_call | solution.py:103
  17.1 3.5 %shard_map.61.refs_2_ = bf16[2048,2048]{1,0:T(8,128)(2,1)S(1)} custom-call(s32[4,66]{1,0:T(4,128)S(1)} %shard_map.59.table_ref, bf16[8320,128]{1,0:T(8,128)(2,1)S(1)} %get-tuple-element.86.refs_0_, bf16[8320,128]{1,0:T(8,128)(2,1)} %collective-permute-done.7.refs_1_, s32[384,1]{1,0:T(8,128)S(1)} %copy.76.refs_2_.refs_1_, s32[1,2048]{1,0:T(1,128)S(1)} %bitcast.9, ...), custom_call_target="tpu_custom_call" | custom-call | bytes 8519680 | tf_op jit(solution)/shard_map/pallas_call | solution.py:171
  20.6 7.7 %collective-permute-done.6.refs_0_ = bf16[3072,128]{1,0:T(8,128)(2,1)S(1)} collective-permute-done((bf16[3072,128]{1,0:T(8,128)(2,1)}, bf16[3072,128]{1,0:T(8,128)(2,1)S(1)}, u32[]{:S(2)}, u32[]{:S(2)}) %collective-permute-start.6) | collective-permute-done | bytes 786464 | tf_op jit(solution)/shard_map/ppermute | solution.py:351
  28.3 1.3 collective-permute-start.4
  29.6 0.7 collective-permute-start.3
  30.3 14.1 %collective-permute-done.4 = bf16[1536,128]{1,0:T(8,128)(2,1)S(1)} collective-permute-done((bf16[1536,128]{1,0:T(8,128)(2,1)S(1)}, bf16[1536,128]{1,0:T(8,128)(2,1)S(1)}, u32[]{:S(2)}, u32[]{:S(2)}) %collective-permute-start.4) | collective-permute-done | bytes 393248 | tf_op jit(solution)/shard_map/ppermute | solution.py:351
  44.4 1.5 %collective-permute-start.5 = (bf16[1536,128]{1,0:T(8,128)(2,1)S(1)}, bf16[1536,128]{1,0:T(8,128)(2,1)S(1)}, u32[]{:S(2)}, u32[]{:S(2)}) collective-permute-start(bf16[1536,128]{1,0:T(8,128)(2,1)S(1)} %collective-permute-done.4), channel_id=1, source_target_pairs={{12,0},{13,1},{14,2},{15,3},{28,16},{29,17},{30,18},{31,19}} | collective-permute-start | bytes 1179656 | tf_op jit(solution)/shard_map/ppermute | solution.py:351
  46.0 3.2 %collective-permute-start.2 = (bf16[3072,128]{1,0:T(8,128)(2,1)S(1)}, bf16[3072,128]{1,0:T(8,128)(2,1)S(1)}, u32[]{:S(2)}, u32[]{:S(2)}) collective-permute-start(bf16[3072,128]{1,0:T(8,128)(2,1)S(1)} %copy-done.5), channel_id=1, source_target_pairs={{4,6},{5,7},{6,4},{7,5},{8,10},{9,11},{10,8},{11,9},{12,14},{13,15... | collective-permute-start | bytes 2359304 | tf_op jit(solution)/shard_map/ppermute | solution.py:351
  49.2 1.2 shard_map.62.refs_6_
  50.4 3.8 %collective-permute-done.5.refs_0_ = bf16[1536,128]{1,0:T(8,128)(2,1)S(1)} collective-permute-done((bf16[1536,128]{1,0:T(8,128)(2,1)S(1)}, bf16[1536,128]{1,0:T(8,128)(2,1)S(1)}, u32[]{:S(2)}, u32[]{:S(2)}) %collective-permute-start.5) | collective-permute-done | bytes 393248 | tf_op jit(solution)/shard_map/ppermute | solution.py:351
  54.7 1.2 collective-permute-done.10.refs_1_
  58.3 8.5 %collective-permute-done.2.refs_0_ = bf16[3072,128]{1,0:T(8,128)(2,1)S(1)} collective-permute-done((bf16[3072,128]{1,0:T(8,128)(2,1)S(1)}, bf16[3072,128]{1,0:T(8,128)(2,1)S(1)}, u32[]{:S(2)}, u32[]{:S(2)}) %collective-permute-start.2) | collective-permute-done | bytes 786464 | tf_op jit(solution)/shard_map/ppermute | solution.py:351
  66.8 0.7 collective-permute-start.14
  67.4 0.7 collective-permute-start.13
  68.7 0.7 collective-permute-start.17
  69.4 0.8 shard_map.67.refs_3_
  70.9 0.7 collective-permute-start.16
  71.5 0.8 shard_map.69
  72.3 0.7 collective-permute-start.15
  73.6 0.7 collective-permute-start.20
  74.9 1.3 %collective-permute-start.19 = (bf16[48,2048]{1,0:T(8,128)(2,1)S(1)}, bf16[48,2048]{1,0:T(8,128)(2,1)S(1)}, u32[]{:S(2)}, u32[]{:S(2)}) collective-permute-start(bf16[48,2048]{1,0:T(8,128)(2,1)S(1)} %get-tuple-element.119.refs_5_), channel_id=1, source_target_pairs={{0,4},{4,8},{8,12},{1,5},{5,9},{9,13},{2,6},{6,10},{10,14},{3,7},{... | collective-permute-start | bytes 589832 | tf_op jit(solution)/shard_map/ppermute | solution.py:450
  76.8 1.3 %collective-permute-start.18 = (bf16[48,2048]{1,0:T(8,128)(2,1)S(1)}, bf16[48,2048]{1,0:T(8,128)(2,1)S(1)}, u32[]{:S(2)}, u32[]{:S(2)}) collective-permute-start(bf16[48,2048]{1,0:T(8,128)(2,1)S(1)} %get-tuple-element.123.refs_5_), channel_id=1, source_target_pairs={{0,4},{4,8},{8,12},{1,5},{5,9},{9,13},{2,6},{6,10},{10,14},{3,7},{... | collective-permute-start | bytes 589832 | tf_op jit(solution)/shard_map/ppermute | solution.py:450
  78.7 1.3 %collective-permute-start.23 = (bf16[48,2048]{1,0:T(8,128)(2,1)S(1)}, bf16[48,2048]{1,0:T(8,128)(2,1)S(1)}, u32[]{:S(2)}, u32[]{:S(2)}) collective-permute-start(bf16[48,2048]{1,0:T(8,128)(2,1)S(1)} %get-tuple-element.127.refs_5_), channel_id=1, source_target_pairs={{4,8},{8,12},{5,9},{9,13},{6,10},{10,14},{7,11},{11,15},{20,24},{2... | collective-permute-start | bytes 589832 | tf_op jit(solution)/shard_map/ppermute | solution.py:450
  80.0 12.7 %collective-permute-done.19.refs_4_ = bf16[48,2048]{1,0:T(8,128)(2,1)S(1)} collective-permute-done((bf16[48,2048]{1,0:T(8,128)(2,1)S(1)}, bf16[48,2048]{1,0:T(8,128)(2,1)S(1)}, u32[]{:S(2)}, u32[]{:S(2)}) %collective-permute-start.19) | collective-permute-done | bytes 196640 | tf_op jit(solution)/shard_map/ppermute | solution.py:450
  92.8 2.6 %shard_map.74 = (bf16[48,2048]{1,0:T(8,128)(2,1)S(1)}, f32[48,128]{1,0:T(8,128)S(1)}, bf16[384,2048]{1,0:T(8,128)(2,1)}, f32[384,128]{1,0:T(8,128)S(1)}) custom-call(s32[16]{0:T(128)S(1)} %get-tuple-element.164.refs_4_.right_ref, bf16[384,2048]{1,0:T(8,128)(2,1)S(1)} %copy-done, ...), custom_call_target="tpu_custom_call", output_to_operand_aliasing={{2}: (8, {}), {3}: (9, {})} | custom-call | flops 1610612736 | bytes 8388608 | tf_op jit(solution)/shard_map/pallas_call | solution.py:301
  95.4 1.3 %collective-permute-start.22 = (bf16[48,2048]{1,0:T(8,128)(2,1)S(1)}, bf16[48,2048]{1,0:T(8,128)(2,1)S(1)}, u32[]{:S(2)}, u32[]{:S(2)}) collective-permute-start(bf16[48,2048]{1,0:T(8,128)(2,1)S(1)} %get-tuple-element.131.refs_5_), channel_id=1, source_target_pairs={{4,8},{8,12},{5,9},{9,13},{6,10},{10,14},{7,11},{11,15},{20,24},{2... | collective-permute-start | bytes 589832 | tf_op jit(solution)/shard_map/ppermute | solution.py:450
  96.7 0.9 collective-permute-done.18.refs_4_
  97.6 2.6 %shard_map.75 = (bf16[48,2048]{1,0:T(8,128)(2,1)S(1)}, f32[48,128]{1,0:T(8,128)S(1)}, bf16[384,2048]{1,0:T(8,128)(2,1)}, f32[384,128]{1,0:T(8,128)S(1)}) custom-call(s32[16]{0:T(128)S(1)} %get-tuple-element.164.refs_4_.right_ref, bf16[384,2048]{1,0:T(8,128)(2,1)S(1)} %copy-done, ...), custom_call_target="tpu_custom_call", output_to_operand_aliasing={{2}: (8, {}), {3}: (9, {})} | custom-call | flops 1610612736 | bytes 8388608 | tf_op jit(solution)/shard_map/pallas_call | solution.py:301
  100.2 1.3 %collective-permute-start.21 = (bf16[48,2048]{1,0:T(8,128)(2,1)S(1)}, bf16[48,2048]{1,0:T(8,128)(2,1)S(1)}, u32[]{:S(2)}, u32[]{:S(2)}) collective-permute-start(bf16[48,2048]{1,0:T(8,128)(2,1)S(1)} %get-tuple-element.135.refs_5_), channel_id=1, source_target_pairs={{4,8},{8,12},{5,9},{9,13},{6,10},{10,14},{7,11},{11,15},{20,24},{2... | collective-permute-start | bytes 589832 | tf_op jit(solution)/shard_map/ppermute | solution.py:450
  102.2 2.9 %shard_map.76 = (bf16[48,2048]{1,0:T(8,128)(2,1)S(1)}, f32[48,128]{1,0:T(8,128)S(1)}, bf16[384,2048]{1,0:T(8,128)(2,1)}, f32[384,128]{1,0:T(8,128)S(1)}) custom-call(s32[16]{0:T(128)S(1)} %get-tuple-element.164.refs_4_.right_ref, bf16[384,2048]{1,0:T(8,128)(2,1)S(1)} %copy-done, ...), custom_call_target="tpu_custom_call", output_to_operand_aliasing={{2}: (8, {}), {3}: (9, {})} | custom-call | flops 1610612736 | bytes 8388608 | tf_op jit(solution)/shard_map/pallas_call | solution.py:301
  105.0 1.3 %collective-permute-start.26 = (bf16[48,2048]{1,0:T(8,128)(2,1)S(1)}, bf16[48,2048]{1,0:T(8,128)(2,1)S(1)}, u32[]{:S(2)}, u32[]{:S(2)}) collective-permute-start(bf16[48,2048]{1,0:T(8,128)(2,1)S(1)} %get-tuple-element.139.refs_5_), channel_id=1, source_target_pairs={{8,12},{9,13},{10,14},{11,15},{24,28},{25,29},{26,30},{27,31}} | collective-permute-start | bytes 589832 | tf_op jit(solution)/shard_map/ppermute | solution.py:450
  106.8 2.6 %shard_map.77 = (bf16[48,2048]{1,0:T(8,128)(2,1)S(1)}, f32[48,128]{1,0:T(8,128)S(1)}, bf16[384,2048]{1,0:T(8,128)(2,1)}, f32[384,128]{1,0:T(8,128)S(1)}) custom-call(s32[16]{0:T(128)S(1)} %get-tuple-element.164.refs_4_.right_ref, bf16[384,2048]{1,0:T(8,128)(2,1)S(1)} %copy-done, ...), custom_call_target="tpu_custom_call", output_to_operand_aliasing={{2}: (8, {}), {3}: (9, {})} | custom-call | flops 1610612736 | bytes 8388608 | tf_op jit(solution)/shard_map/pallas_call | solution.py:301
  109.4 1.3 %collective-permute-start.25 = (bf16[48,2048]{1,0:T(8,128)(2,1)S(1)}, bf16[48,2048]{1,0:T(8,128)(2,1)S(1)}, u32[]{:S(2)}, u32[]{:S(2)}) collective-permute-start(bf16[48,2048]{1,0:T(8,128)(2,1)S(1)} %get-tuple-element.143.refs_5_), channel_id=1, source_target_pairs={{8,12},{9,13},{10,14},{11,15},{24,28},{25,29},{26,30},{27,31}} | collective-permute-start | bytes 589832 | tf_op jit(solution)/shard_map/ppermute | solution.py:450
  110.7 0.7 collective-permute-done.21.refs_4_
  111.4 2.6 %shard_map.78 = (bf16[48,2048]{1,0:T(8,128)(2,1)S(1)}, f32[48,128]{1,0:T(8,128)S(1)}, bf16[384,2048]{1,0:T(8,128)(2,1)}, f32[384,128]{1,0:T(8,128)S(1)}) custom-call(s32[16]{0:T(128)S(1)} %get-tuple-element.164.refs_4_.right_ref, bf16[384,2048]{1,0:T(8,128)(2,1)S(1)} %copy-done, ...), custom_call_target="tpu_custom_call", output_to_operand_aliasing={{2}: (8, {}), {3}: (9, {})} | custom-call | flops 1610612736 | bytes 8388608 | tf_op jit(solution)/shard_map/pallas_call | solution.py:301
  114.1 1.3 %collective-permute-start.24 = (bf16[48,2048]{1,0:T(8,128)(2,1)S(1)}, bf16[48,2048]{1,0:T(8,128)(2,1)S(1)}, u32[]{:S(2)}, u32[]{:S(2)}) collective-permute-start(bf16[48,2048]{1,0:T(8,128)(2,1)S(1)} %get-tuple-element.147.refs_5_), channel_id=1, source_target_pairs={{8,12},{9,13},{10,14},{11,15},{24,28},{25,29},{26,30},{27,31}} | collective-permute-start | bytes 589832 | tf_op jit(solution)/shard_map/ppermute | solution.py:450
  115.7 2.6 %shard_map.79 = (bf16[48,2048]{1,0:T(8,128)(2,1)S(1)}, f32[48,128]{1,0:T(8,128)S(1)}, bf16[384,2048]{1,0:T(8,128)(2,1)}, f32[384,128]{1,0:T(8,128)S(1)}) custom-call(s32[16]{0:T(128)S(1)} %get-tuple-element.164.refs_4_.right_ref, bf16[384,2048]{1,0:T(8,128)(2,1)S(1)} %copy-done, ...), custom_call_target="tpu_custom_call", output_to_operand_aliasing={{2}: (8, {}), {3}: (9, {})} | custom-call | flops 1610612736 | bytes 8388608 | tf_op jit(solution)/shard_map/pallas_call | solution.py:301
  118.4 1.5 %collective-permute-done.25.refs_4_ = bf16[48,2048]{1,0:T(8,128)(2,1)S(1)} collective-permute-done((bf16[48,2048]{1,0:T(8,128)(2,1)S(1)}, bf16[48,2048]{1,0:T(8,128)(2,1)S(1)}, u32[]{:S(2)}, u32[]{:S(2)}) %collective-permute-start.25) | collective-permute-done | bytes 196640 | tf_op jit(solution)/shard_map/ppermute | solution.py:450
  119.9 2.6 %shard_map.80 = (bf16[48,2048]{1,0:T(8,128)(2,1)S(1)}, f32[48,128]{1,0:T(8,128)S(1)}, bf16[384,2048]{1,0:T(8,128)(2,1)}, f32[384,128]{1,0:T(8,128)S(1)}) custom-call(s32[16]{0:T(128)S(1)} %get-tuple-element.164.refs_4_.right_ref, bf16[384,2048]{1,0:T(8,128)(2,1)S(1)} %copy-done, ...), custom_call_target="tpu_custom_call", output_to_operand_aliasing={{2}: (8, {}), {3}: (9, {})} | custom-call | flops 1610612736 | bytes 8388608 | tf_op jit(solution)/shard_map/pallas_call | solution.py:301
  122.6 1.5 %collective-permute-done.24.refs_4_ = bf16[48,2048]{1,0:T(8,128)(2,1)S(1)} collective-permute-done((bf16[48,2048]{1,0:T(8,128)(2,1)S(1)}, bf16[48,2048]{1,0:T(8,128)(2,1)S(1)}, u32[]{:S(2)}, u32[]{:S(2)}) %collective-permute-start.24) | collective-permute-done | bytes 196640 | tf_op jit(solution)/shard_map/ppermute | solution.py:450
  124.0 4.0 %shard_map.81 = (bf16[48,2048]{1,0:T(8,128)(2,1)}, f32[48,128]{1,0:T(8,128)}, bf16[384,2048]{1,0:T(8,128)(2,1)}, f32[384,128]{1,0:T(8,128)S(1)}) custom-call(s32[16]{0:T(128)S(1)} %get-tuple-element.164.refs_4_.right_ref, bf16[384,2048]{1,0:T(8,128)(2,1)S(1)} %copy-done, ...), custom_call_target="tpu_custom_call", output_to_operand_aliasing={{2}: (8, {}), {3}: (9, {})} | custom-call | flops 1610612736 | bytes 8388608 | tf_op jit(solution)/shard_map/pallas_call | solution.py:301
  (54 shorter events, 10.0 us)
Async XLA Ops:
  0.6 2.2 %copy-start.1 = (bf16[1,2048,2,512]{3,2,1,0:T(2,128)(2,1)S(1)}, bf16[1,2048,2,512]{3,2,1,0:T(2,128)(2,1)}, u32[]{:S(2)}) copy-start(bf16[1,2048,2,512]{3,2,1,0:T(2,128)(2,1)} %tensor_ref.1) | copy-start | bytes 12582916
  2.8 0.7 copy-start.2
  3.5 8.9 %copy-start.3 = (s32[5,16]{1,0:T(8,128)S(1)}, s32[5,16]{1,0:T(8,128)}, u32[]{:S(2)}) copy-start(s32[5,16]{1,0:T(8,128)} %charge_ref.3) | copy-start | bytes 964
  3.5 12.0 %copy-start.8 = (s32[1,384]{1,0:T(1,128)S(1)}, s32[1,384]{1,0:T(1,128)}, u32[]{:S(2)}) copy-start(s32[1,384]{1,0:T(1,128)} %param.8) | copy-start | bytes 4612
  6.5 0.9 copy-start.4
  7.4 0.8 copy-start.6
  8.2 8.8 %collective-permute-start.7 = (bf16[8320,128]{1,0:T(8,128)(2,1)S(1)}, bf16[8320,128]{1,0:T(8,128)(2,1)}, u32[]{:S(2)}, u32[]{:S(2)}) collective-permute-start(bf16[8320,128]{1,0:T(8,128)(2,1)S(1)} %get-tuple-element.86.refs_0_), channel_id=1, source_target_pairs={{0,1},{1,0},{2,3},{3,2},{4,5},{5,4},{6,7},{7,6},{8,9},{9,8},{10,11... | collective-permute-start | bytes 6389768 | tf_op jit(solution)/shard_map/ppermute | solution.py:362
  8.2 20.2 %collective-permute-start.6 = (bf16[3072,128]{1,0:T(8,128)(2,1)}, bf16[3072,128]{1,0:T(8,128)(2,1)S(1)}, u32[]{:S(2)}, u32[]{:S(2)}) collective-permute-start(bf16[3072,128]{1,0:T(8,128)(2,1)} %get-tuple-element.85), channel_id=1, source_target_pairs={{0,2},{1,3},{2,0},{3,1},{4,6},{5,7},{6,4},{7,5},{8,10},{9,11},{10,... | collective-permute-start | bytes 2359304 | tf_op jit(solution)/shard_map/ppermute | solution.py:351
  10.8 4.8 %collective-permute-start.8 = (s32[1]{0:T(128)}, s32[1]{0:T(128)}, u32[]{:S(2)}, u32[]{:S(2)}) collective-permute-start(s32[1]{0:T(128)} %bitcast.4), channel_id=1, source_target_pairs={{0,16},{16,0},{1,17},{17,1},{2,18},{18,2},{3,19},{19,3},{4,20},{20... | collective-permute-start | bytes 20 | tf_op jit(solution)/shard_map/ppermute | solution.py:386
  17.1 11.3 %copy-start.7 = (bf16[1536,128]{1,0:T(8,128)(2,1)S(1)}, bf16[1536,128]{1,0:T(8,128)(2,1)}, u32[]{:S(2)}) copy-start(bf16[1536,128]{1,0:T(8,128)(2,1)} %copy-done.6) | copy-start | bytes 1179652
  17.1 28.9 %copy-start.5 = (bf16[3072,128]{1,0:T(8,128)(2,1)S(1)}, bf16[3072,128]{1,0:T(8,128)(2,1)}, u32[]{:S(2)}) copy-start(bf16[3072,128]{1,0:T(8,128)(2,1)} %copy-done.4) | copy-start | bytes 2359300
  28.3 20.8 %collective-permute-start.9 = (bf16[3072,128]{1,0:T(8,128)(2,1)S(1)}, bf16[3072,128]{1,0:T(8,128)(2,1)S(1)}, u32[]{:S(2)}, u32[]{:S(2)}) collective-permute-start(bf16[3072,128]{1,0:T(8,128)(2,1)S(1)} %collective-permute-done.6.refs_0_), channel_id=1, source_target_pairs={{0,1},{1,0},{2,3},{3,2},{4,5},{5,4},{6,7},{7,6},{8,9},{9,8},{10,11... | collective-permute-start | bytes 2359304 | tf_op jit(solution)/shard_map/ppermute | solution.py:362
  28.3 16.1 %collective-permute-start.4 = (bf16[1536,128]{1,0:T(8,128)(2,1)S(1)}, bf16[1536,128]{1,0:T(8,128)(2,1)S(1)}, u32[]{:S(2)}, u32[]{:S(2)}) collective-permute-start(bf16[1536,128]{1,0:T(8,128)(2,1)S(1)} %copy-done.7), channel_id=1, source_target_pairs={{0,14},{1,15},{2,12},{3,13},{16,30},{17,31},{18,28},{19,29}} | collective-permute-start | bytes 1179656 | tf_op jit(solution)/shard_map/ppermute | solution.py:351
  29.6 20.8 %collective-permute-start.3 = (bf16[1536,128]{1,0:T(8,128)(2,1)S(1)}, bf16[1536,128]{1,0:T(8,128)(2,1)S(1)}, u32[]{:S(2)}, u32[]{:S(2)}) collective-permute-start(bf16[1536,128]{1,0:T(8,128)(2,1)S(1)} %get-tuple-element.83), channel_id=1, source_target_pairs={{0,2},{1,3},{2,0},{3,1},{16,18},{17,19},{18,16},{19,17}} | collective-permute-start | bytes 1179656 | tf_op jit(solution)/shard_map/ppermute | solution.py:351
  44.4 9.7 %collective-permute-start.5 = (bf16[1536,128]{1,0:T(8,128)(2,1)S(1)}, bf16[1536,128]{1,0:T(8,128)(2,1)S(1)}, u32[]{:S(2)}, u32[]{:S(2)}) collective-permute-start(bf16[1536,128]{1,0:T(8,128)(2,1)S(1)} %collective-permute-done.4), channel_id=1, source_target_pairs={{12,0},{13,1},{14,2},{15,3},{28,16},{29,17},{30,18},{31,19}} | collective-permute-start | bytes 1179656 | tf_op jit(solution)/shard_map/ppermute | solution.py:351
  46.0 20.8 %collective-permute-start.2 = (bf16[3072,128]{1,0:T(8,128)(2,1)S(1)}, bf16[3072,128]{1,0:T(8,128)(2,1)S(1)}, u32[]{:S(2)}, u32[]{:S(2)}) collective-permute-start(bf16[3072,128]{1,0:T(8,128)(2,1)S(1)} %copy-done.5), channel_id=1, source_target_pairs={{4,6},{5,7},{6,4},{7,5},{8,10},{9,11},{10,8},{11,9},{12,14},{13,15... | collective-permute-start | bytes 2359304 | tf_op jit(solution)/shard_map/ppermute | solution.py:351
  50.4 6.7 %copy-start = (bf16[384,2048]{1,0:T(8,128)(2,1)S(1)}, bf16[384,2048]{1,0:T(8,128)(2,1)}, u32[]{:S(2)}) copy-start(bf16[384,2048]{1,0:T(8,128)(2,1)} %refs_0_.33) | copy-start | bytes 4718596
  54.2 1.7 %collective-permute-start.10 = (bf16[1536,128]{1,0:T(8,128)(2,1)S(1)}, bf16[1536,128]{1,0:T(8,128)(2,1)S(1)}, u32[]{:S(2)}, u32[]{:S(2)}) collective-permute-start(bf16[1536,128]{1,0:T(8,128)(2,1)S(1)} %collective-permute-done.5.refs_0_), channel_id=1, source_target_pairs={{0,1},{1,0},{2,3},{3,2},{4,5},{5,4},{6,7},{7,6},{8,9},{9,8},{10,11... | collective-permute-start | bytes 1179656 | tf_op jit(solution)/shard_map/ppermute | solution.py:362
  54.2 2.3 %collective-permute-start.11 = (bf16[1536,128]{1,0:T(8,128)(2,1)S(1)}, bf16[1536,128]{1,0:T(8,128)(2,1)S(1)}, u32[]{:S(2)}, u32[]{:S(2)}) collective-permute-start(bf16[1536,128]{1,0:T(8,128)(2,1)S(1)} %collective-permute-done.3.refs_2_), channel_id=1, source_target_pairs={{0,1},{1,0},{2,3},{3,2},{4,5},{5,4},{6,7},{7,6},{8,9},{9,8},{10,11... | collective-permute-start | bytes 1179656 | tf_op jit(solution)/shard_map/ppermute | solution.py:362
  66.8 2.6 %collective-permute-start.12 = (bf16[3072,128]{1,0:T(8,128)(2,1)S(1)}, bf16[3072,128]{1,0:T(8,128)(2,1)S(1)}, u32[]{:S(2)}, u32[]{:S(2)}) collective-permute-start(bf16[3072,128]{1,0:T(8,128)(2,1)S(1)} %collective-permute-done.2.refs_0_), channel_id=1, source_target_pairs={{0,1},{1,0},{2,3},{3,2},{4,5},{5,4},{6,7},{7,6},{8,9},{9,8},{10,11... | collective-permute-start | bytes 2359304 | tf_op jit(solution)/shard_map/ppermute | solution.py:362
  66.8 3.5 %collective-permute-start.14 = (bf16[48,2048]{1,0:T(8,128)(2,1)S(1)}, bf16[48,2048]{1,0:T(8,128)(2,1)S(1)}, u32[]{:S(2)}, u32[]{:S(2)}) collective-permute-start(bf16[48,2048]{1,0:T(8,128)(2,1)S(1)} %get-tuple-element.94.refs_4_), channel_id=1, source_target_pairs={{0,4},{1,5},{2,6},{3,7},{16,20},{17,21},{18,22},{19,23}} | collective-permute-start | bytes 589832 | tf_op jit(solution)/shard_map/ppermute | solution.py:450
  67.4 4.1 %collective-permute-start.13 = (bf16[48,2048]{1,0:T(8,128)(2,1)S(1)}, bf16[48,2048]{1,0:T(8,128)(2,1)S(1)}, u32[]{:S(2)}, u32[]{:S(2)}) collective-permute-start(bf16[48,2048]{1,0:T(8,128)(2,1)S(1)} %get-tuple-element.98.refs_4_), channel_id=1, source_target_pairs={{0,4},{1,5},{2,6},{3,7},{16,20},{17,21},{18,22},{19,23}} | collective-permute-start | bytes 589832 | tf_op jit(solution)/shard_map/ppermute | solution.py:450
  68.7 4.3 %collective-permute-start.17 = (bf16[48,2048]{1,0:T(8,128)(2,1)S(1)}, bf16[48,2048]{1,0:T(8,128)(2,1)S(1)}, u32[]{:S(2)}, u32[]{:S(2)}) collective-permute-start(bf16[48,2048]{1,0:T(8,128)(2,1)S(1)} %get-tuple-element.103.refs_2_.refs_5_), channel_id=1, source_target_pairs={{0,4},{1,5},{2,6},{3,7},{16,20},{17,21},{18,22},{19,23}} | collective-permute-start | bytes 589832 | tf_op jit(solution)/shard_map/ppermute | solution.py:450
  70.9 3.4 %collective-permute-start.16 = (bf16[48,2048]{1,0:T(8,128)(2,1)S(1)}, bf16[48,2048]{1,0:T(8,128)(2,1)S(1)}, u32[]{:S(2)}, u32[]{:S(2)}) collective-permute-start(bf16[48,2048]{1,0:T(8,128)(2,1)S(1)} %get-tuple-element.107.refs_5_), channel_id=1, source_target_pairs={{0,4},{4,8},{1,5},{5,9},{2,6},{6,10},{3,7},{7,11},{16,20},{20,24},... | collective-permute-start | bytes 589832 | tf_op jit(solution)/shard_map/ppermute | solution.py:450
  72.3 3.9 %collective-permute-start.15 = (bf16[48,2048]{1,0:T(8,128)(2,1)S(1)}, bf16[48,2048]{1,0:T(8,128)(2,1)S(1)}, u32[]{:S(2)}, u32[]{:S(2)}) collective-permute-start(bf16[48,2048]{1,0:T(8,128)(2,1)S(1)} %get-tuple-element.111.refs_5_), channel_id=1, source_target_pairs={{0,4},{4,8},{1,5},{5,9},{2,6},{6,10},{3,7},{7,11},{16,20},{20,24},... | collective-permute-start | bytes 589832 | tf_op jit(solution)/shard_map/ppermute | solution.py:450
  73.6 4.5 %collective-permute-start.20 = (bf16[48,2048]{1,0:T(8,128)(2,1)S(1)}, bf16[48,2048]{1,0:T(8,128)(2,1)S(1)}, u32[]{:S(2)}, u32[]{:S(2)}) collective-permute-start(bf16[48,2048]{1,0:T(8,128)(2,1)S(1)} %get-tuple-element.115.refs_5_), channel_id=1, source_target_pairs={{0,4},{4,8},{1,5},{5,9},{2,6},{6,10},{3,7},{7,11},{16,20},{20,24},... | collective-permute-start | bytes 589832 | tf_op jit(solution)/shard_map/ppermute | solution.py:450
  74.9 17.9 %collective-permute-start.19 = (bf16[48,2048]{1,0:T(8,128)(2,1)S(1)}, bf16[48,2048]{1,0:T(8,128)(2,1)S(1)}, u32[]{:S(2)}, u32[]{:S(2)}) collective-permute-start(bf16[48,2048]{1,0:T(8,128)(2,1)S(1)} %get-tuple-element.119.refs_5_), channel_id=1, source_target_pairs={{0,4},{4,8},{8,12},{1,5},{5,9},{9,13},{2,6},{6,10},{10,14},{3,7},{... | collective-permute-start | bytes 589832 | tf_op jit(solution)/shard_map/ppermute | solution.py:450
  76.8 20.8 %collective-permute-start.18 = (bf16[48,2048]{1,0:T(8,128)(2,1)S(1)}, bf16[48,2048]{1,0:T(8,128)(2,1)S(1)}, u32[]{:S(2)}, u32[]{:S(2)}) collective-permute-start(bf16[48,2048]{1,0:T(8,128)(2,1)S(1)} %get-tuple-element.123.refs_5_), channel_id=1, source_target_pairs={{0,4},{4,8},{8,12},{1,5},{5,9},{9,13},{2,6},{6,10},{10,14},{3,7},{... | collective-permute-start | bytes 589832 | tf_op jit(solution)/shard_map/ppermute | solution.py:450
  78.7 23.5 %collective-permute-start.23 = (bf16[48,2048]{1,0:T(8,128)(2,1)S(1)}, bf16[48,2048]{1,0:T(8,128)(2,1)S(1)}, u32[]{:S(2)}, u32[]{:S(2)}) collective-permute-start(bf16[48,2048]{1,0:T(8,128)(2,1)S(1)} %get-tuple-element.127.refs_5_), channel_id=1, source_target_pairs={{4,8},{8,12},{5,9},{9,13},{6,10},{10,14},{7,11},{11,15},{20,24},{2... | collective-permute-start | bytes 589832 | tf_op jit(solution)/shard_map/ppermute | solution.py:450
  95.4 11.4 %collective-permute-start.22 = (bf16[48,2048]{1,0:T(8,128)(2,1)S(1)}, bf16[48,2048]{1,0:T(8,128)(2,1)S(1)}, u32[]{:S(2)}, u32[]{:S(2)}) collective-permute-start(bf16[48,2048]{1,0:T(8,128)(2,1)S(1)} %get-tuple-element.131.refs_5_), channel_id=1, source_target_pairs={{4,8},{8,12},{5,9},{9,13},{6,10},{10,14},{7,11},{11,15},{20,24},{2... | collective-permute-start | bytes 589832 | tf_op jit(solution)/shard_map/ppermute | solution.py:450
  100.2 11.2 %collective-permute-start.21 = (bf16[48,2048]{1,0:T(8,128)(2,1)S(1)}, bf16[48,2048]{1,0:T(8,128)(2,1)S(1)}, u32[]{:S(2)}, u32[]{:S(2)}) collective-permute-start(bf16[48,2048]{1,0:T(8,128)(2,1)S(1)} %get-tuple-element.135.refs_5_), channel_id=1, source_target_pairs={{4,8},{8,12},{5,9},{9,13},{6,10},{10,14},{7,11},{11,15},{20,24},{2... | collective-permute-start | bytes 589832 | tf_op jit(solution)/shard_map/ppermute | solution.py:450
  105.0 10.7 %collective-permute-start.26 = (bf16[48,2048]{1,0:T(8,128)(2,1)S(1)}, bf16[48,2048]{1,0:T(8,128)(2,1)S(1)}, u32[]{:S(2)}, u32[]{:S(2)}) collective-permute-start(bf16[48,2048]{1,0:T(8,128)(2,1)S(1)} %get-tuple-element.139.refs_5_), channel_id=1, source_target_pairs={{8,12},{9,13},{10,14},{11,15},{24,28},{25,29},{26,30},{27,31}} | collective-permute-start | bytes 589832 | tf_op jit(solution)/shard_map/ppermute | solution.py:450
  109.4 10.5 %collective-permute-start.25 = (bf16[48,2048]{1,0:T(8,128)(2,1)S(1)}, bf16[48,2048]{1,0:T(8,128)(2,1)S(1)}, u32[]{:S(2)}, u32[]{:S(2)}) collective-permute-start(bf16[48,2048]{1,0:T(8,128)(2,1)S(1)} %get-tuple-element.143.refs_5_), channel_id=1, source_target_pairs={{8,12},{9,13},{10,14},{11,15},{24,28},{25,29},{26,30},{27,31}} | collective-permute-start | bytes 589832 | tf_op jit(solution)/shard_map/ppermute | solution.py:450
  114.1 10.0 %collective-permute-start.24 = (bf16[48,2048]{1,0:T(8,128)(2,1)S(1)}, bf16[48,2048]{1,0:T(8,128)(2,1)S(1)}, u32[]{:S(2)}, u32[]{:S(2)}) collective-permute-start(bf16[48,2048]{1,0:T(8,128)(2,1)S(1)} %get-tuple-element.147.refs_5_), channel_id=1, source_target_pairs={{8,12},{9,13},{10,14},{11,15},{24,28},{25,29},{26,30},{27,31}} | collective-permute-start | bytes 589832 | tf_op jit(solution)/shard_map/ppermute | solution.py:450

commit v4 on v3

--- a/solution.py
+++ b/solution.py
@@ -206,7 +206,10 @@
     if carried:
         old_ref, old_norm_ref = refs[:2]
         refs = refs[4:]
-    sent_ref, norm_ref, fronts_ref, norms_ref, lhs_ref, acc_ref, sems = refs
+    if ends:
+        fronts_ref, norms_ref, sent_ref, norm_ref, lhs_ref, acc_ref, sems = refs
+    else:
+        sent_ref, norm_ref, fronts_ref, norms_ref, lhs_ref, acc_ref, sems = refs
     rows, bond = sent_ref.shape
     site = lax.axis_index("site")
     micro = step - DELAY * site
@@ -217,11 +220,18 @@
 
     tile = min(bond, 512)
 
+    def piece(n):
+        where = pl.ds(pl.multiple_of(micro * rows, 8), rows)
+        cols = slice(n * tile, (n + 1) * tile)
+        return pltpu.make_async_copy(
+            sent_ref.at[:, cols], fronts_ref.at[where, cols], sems.at[4 + n]
+        )
+
     def copies(back, front_ref, row_norm_ref):
         where = pl.ds(pl.multiple_of((micro - back) * rows, 8), rows)
         return (
-            pltpu.make_async_copy(front_ref, fronts_ref.at[where], sems.at[0]),
-            pltpu.make_async_copy(row_norm_ref, norms_ref.at[where], sems.at[1]),
+            pltpu.make_async_copy(front_ref, fronts_ref.at[where], sems.at[2 * back]),
+            pltpu.make_async_copy(row_norm_ref, norms_ref.at[where], sems.at[2 * back + 1]),
         )
 
     if carried:
@@ -263,8 +273,12 @@
             squares += chosen(j) * chosen(j)
         norm = jnp.sqrt(jnp.sum(squares, axis=1, keepdims=True) / bond + EPSILON)
         norm_ref[...] = jnp.broadcast_to(norm, norm_ref.shape)
+        if ends:
+            copies(0, sent_ref, norm_ref)[1].start()
         for j in range(bond // BLOCK):
             sent_ref[:, j * BLOCK : (j + 1) * BLOCK] = (chosen(j) / norm).astype(sent_ref.dtype)
+            if ends and (j + 1) % (tile // BLOCK) == 0:
+                piece((j + 1) * BLOCK // tile - 1).start()
 
     if carried:
 
@@ -277,10 +291,9 @@
 
         @pl.when(active(0))
         def _():
-            for copy in copies(0, sent_ref, norm_ref):
-                copy.start()
-            for copy in copies(0, sent_ref, norm_ref):
-                copy.wait()
+            copies(0, sent_ref, norm_ref)[1].wait()
+            for n in range(bond // tile):
+                piece(n).wait()
 
 
 def advance(step, ends, right, fronts_in, picks, left, weights, received, old, results):
@@ -288,6 +301,7 @@
     rows = MICRO
     relay = received is not None
     carried = results is not None
+    rounds = (pltpu.VMEM((rows, bond), jnp.bfloat16), pltpu.VMEM((rows, LANES), jnp.float32))
     operands = [fronts_in, picks, left, *weights]
     in_specs = [VMEM] * len(operands)
     aliases = {}
@@ -297,12 +311,11 @@
     if carried:
         operands += [*old, *results]
         in_specs += [VMEM, VMEM, HBM, HBM]
-        aliases = {len(operands) - 1: 2, len(operands): 3}
+        aliases = {len(operands) - 1: 0 if ends else 2, len(operands): 1 if ends else 3}
     return pl.pallas_call(
         functools.partial(step_kernel, len(weights), step, relay, carried, ends),
         out_shape=(
-            jax.ShapeDtypeStruct((rows, bond), jnp.bfloat16),
-            jax.ShapeDtypeStruct((rows, LANES), jnp.float32),
+            *(() if ends else (jax.ShapeDtypeStruct(r.shape, r.dtype) for r in rounds)),
             jax.ShapeDtypeStruct((row_count, bond), jnp.bfloat16),
             jax.ShapeDtypeStruct((row_count, LANES), jnp.float32),
         ),
@@ -310,11 +323,12 @@
             num_scalar_prefetch=1,
             grid=(1,),
             in_specs=in_specs,
-            out_specs=(VMEM, VMEM, HBM, HBM),
+            out_specs=(HBM, HBM) if ends else (VMEM, VMEM, HBM, HBM),
             scratch_shapes=[
+                *(rounds if ends else ()),
                 pltpu.VMEM((CHARGES * rows, bond), jnp.bfloat16),
                 pltpu.VMEM((CHARGES * rows, bond), jnp.float32),
-                pltpu.SemaphoreType.DMA((2,)),
+                pltpu.SemaphoreType.DMA((4 + bond // min(bond, 512),)),
             ],
         ),
         input_output_aliases=aliases,
@@ -438,17 +452,16 @@
             late = exchange(old[0])
         if step == DELAY:
             weights = complete(weights, late, old[0])
-        sent, norm, *results = advance(
+        *old, fronts, norms = advance(
             step, step == steps - 1, right, fronts_in, picks, left_lanes, [weights],
             received.pop(step - DELAY, None), old, results,
         )
-        old = (sent, norm)
+        results = (fronts, norms)
         pairs = [
             (s, s + 1) for s in range(sites - 1) if 0 <= step - DELAY * s < micro_count
         ]
         if pairs:
-            received[step] = lax.ppermute(sent, "site", pairs)
-    fronts, norms = results
+            received[step] = lax.ppermute(old[0], "site", pairs)
     return fronts[None], jnp.log(norms[:, 0])[None]
 
 

time: 129 us -> 129 us (level)
  transfers between devices with their start and end apart: 25 -> 25, of which waited for: 14 -> 14; matrix products, arithmetic and copies ran while one was open for 1% -> 1% of each run, Pallas kernels for 26% -> 27%
where the time goes in v4:
time: 129 us
  waiting for transfers between devices  54.2 us (42%)
  Pallas kernels  40.7 us (32%)
  starting transfers between devices  24.6 us (19%)
  local copies, waits for them, and re-layouts  5.56 us (4%)
  between operations  2.4 us (2%)
    ppermute x5, waiting for transfers between devices, move(): return lax.ppermute(part, ('site', 'sample'), flat)  34 us
    pallas_call x17, Pallas kernels, advance(): pl.pallas_call(functools.partial(step_kernel, len(weights), step, relay,...  28.4 us
    ppermute x14, waiting for transfers between devices, pipeline(): received[step] = lax.ppermute(old[0], 'site', pairs)  18.5 us
    ppermute x14, starting transfers between devices, pipeline(): received[step] = lax.ppermute(old[0], 'site', pairs)  14.4 us
    ppermute x5, starting transfers between devices, move(): return lax.ppermute(part, ('site', 'sample'), flat)  8.16 us
    pallas_call x4, Pallas kernels, unpack(): pl.pallas_call(functools.partial(unpack_kernel, [piece[1:] for piece in p...  6.17 us
    unnamed x18, local copies, waits for them, and re-layouts  4.53 us
    pallas_call x1, Pallas kernels, plan(): pl.pallas_call(functools.partial(plan_kernel, blocks, per_shard, cores),...  3.12 us
  transfers between devices with their start and end apart: 25, of which 14 were waited for; matrix products, arithmetic and copies ran while one was open for 1% of the time, Pallas kernels for 27%

profile of v4, /device:TPU:24, one launch (start us, length us, event | category | flops | bytes accessed | tf_op | source)
XLA Modules:
  0.0 128.6 jit_solution(4486611169212086212)
XLA Ops:
  0.6 2.2 %copy-done.1 = bf16[1,2048,2,512]{3,2,1,0:T(2,128)(2,1)S(1)} copy-done((bf16[1,2048,2,512]{3,2,1,0:T(2,128)(2,1)S(1)}, bf16[1,2048,2,512]{3,2,1,0:T(2,128)(2,1)}, u32[]{:S(2)}) %copy-start.1) | copy-done | bytes 4194328
  2.8 0.7 copy-done.2
  3.5 3.0 %shard_map.60 = (bf16[8320,128]{1,0:T(8,128)(2,1)S(1)}, bf16[3072,128]{1,0:T(8,128)(2,1)}, bf16[1536,128]{1,0:T(8,128)(2,1)S(1)}, bf16[1536,128]{1,0:T(8,128)(2,1)S(1)}, bf16[3072,128]{1,0:T(8,128)(2,1)S(1)}) custom-call(s32[5,16]{1,0:T(8,128)S(1)} %copy-done.2, bf16[1,2048,2,512]{3,2,1,0:T(2,128)(2,1)S(1)} %copy-done.1), custom_call_target="tpu_custom_call" | custom-call | flops 1073741824 | bytes 6291456 | tf_op jit(solution)/shard_map/pallas_call | solution.py:60
  6.5 0.9 copy-done.4
  7.4 0.8 copy-done.6
  8.2 1.5 %collective-permute-start.6 = (bf16[3072,128]{1,0:T(8,128)(2,1)}, bf16[3072,128]{1,0:T(8,128)(2,1)S(1)}, u32[]{:S(2)}, u32[]{:S(2)}) collective-permute-start(bf16[3072,128]{1,0:T(8,128)(2,1)} %get-tuple-element.85), channel_id=1, source_target_pairs={{0,2},{1,3},{2,0},{3,1},{4,6},{5,7},{6,4},{7,5},{8,10},{9,11},{10,... | collective-permute-start | bytes 2359304 | tf_op jit(solution)/shard_map/ppermute | solution.py:365
  10.8 1.5 %collective-permute-start.8 = (s32[1]{0:T(128)}, s32[1]{0:T(128)}, u32[]{:S(2)}, u32[]{:S(2)}) collective-permute-start(s32[1]{0:T(128)} %bitcast.4), channel_id=1, source_target_pairs={{0,16},{16,0},{1,17},{17,1},{2,18},{18,2},{3,19},{19,3},{4,20},{20... | collective-permute-start | bytes 20 | tf_op jit(solution)/shard_map/ppermute | solution.py:400
  12.4 3.1 %shard_map.59.table_ref = s32[4,66]{1,0:T(4,128)S(1)} custom-call(s32[5,16]{1,0:T(8,128)S(1)} %copy-done.3), custom_call_target="tpu_custom_call" | custom-call | flops 100 | bytes 4096 | tf_op jit(solution)/shard_map/pallas_call | solution.py:103
  17.1 3.5 %shard_map.61.refs_2_ = bf16[2048,2048]{1,0:T(8,128)(2,1)S(1)} custom-call(s32[4,66]{1,0:T(4,128)S(1)} %shard_map.59.table_ref, bf16[8320,128]{1,0:T(8,128)(2,1)S(1)} %get-tuple-element.86.refs_0_, bf16[8320,128]{1,0:T(8,128)(2,1)} %collective-permute-done.7.refs_1_, s32[384,1]{1,0:T(8,128)S(1)} %copy.76.refs_2_.refs_1_, s32[1,2048]{1,0:T(1,128)S(1)} %bitcast.9, ...), custom_call_target="tpu_custom_call" | custom-call | bytes 8519680 | tf_op jit(solution)/shard_map/pallas_call | solution.py:171
  20.6 7.7 %collective-permute-done.6.refs_0_ = bf16[3072,128]{1,0:T(8,128)(2,1)S(1)} collective-permute-done((bf16[3072,128]{1,0:T(8,128)(2,1)}, bf16[3072,128]{1,0:T(8,128)(2,1)S(1)}, u32[]{:S(2)}, u32[]{:S(2)}) %collective-permute-start.6) | collective-permute-done | bytes 786464 | tf_op jit(solution)/shard_map/ppermute | solution.py:365
  28.3 1.3 collective-permute-start.4
  29.6 0.7 collective-permute-start.3
  30.3 14.1 %collective-permute-done.4 = bf16[1536,128]{1,0:T(8,128)(2,1)S(1)} collective-permute-done((bf16[1536,128]{1,0:T(8,128)(2,1)S(1)}, bf16[1536,128]{1,0:T(8,128)(2,1)S(1)}, u32[]{:S(2)}, u32[]{:S(2)}) %collective-permute-start.4) | collective-permute-done | bytes 393248 | tf_op jit(solution)/shard_map/ppermute | solution.py:365
  44.4 1.5 %collective-permute-start.5 = (bf16[1536,128]{1,0:T(8,128)(2,1)S(1)}, bf16[1536,128]{1,0:T(8,128)(2,1)S(1)}, u32[]{:S(2)}, u32[]{:S(2)}) collective-permute-start(bf16[1536,128]{1,0:T(8,128)(2,1)S(1)} %collective-permute-done.4), channel_id=1, source_target_pairs={{12,0},{13,1},{14,2},{15,3},{28,16},{29,17},{30,18},{31,19}} | collective-permute-start | bytes 1179656 | tf_op jit(solution)/shard_map/ppermute | solution.py:365
  46.0 3.2 %collective-permute-start.2 = (bf16[3072,128]{1,0:T(8,128)(2,1)S(1)}, bf16[3072,128]{1,0:T(8,128)(2,1)S(1)}, u32[]{:S(2)}, u32[]{:S(2)}) collective-permute-start(bf16[3072,128]{1,0:T(8,128)(2,1)S(1)} %copy-done.5), channel_id=1, source_target_pairs={{4,6},{5,7},{6,4},{7,5},{8,10},{9,11},{10,8},{11,9},{12,14},{13,15... | collective-permute-start | bytes 2359304 | tf_op jit(solution)/shard_map/ppermute | solution.py:365
  49.2 1.2 shard_map.62.refs_6_
  50.4 3.8 %collective-permute-done.5.refs_0_ = bf16[1536,128]{1,0:T(8,128)(2,1)S(1)} collective-permute-done((bf16[1536,128]{1,0:T(8,128)(2,1)S(1)}, bf16[1536,128]{1,0:T(8,128)(2,1)S(1)}, u32[]{:S(2)}, u32[]{:S(2)}) %collective-permute-start.5) | collective-permute-done | bytes 393248 | tf_op jit(solution)/shard_map/ppermute | solution.py:365
  54.7 1.2 collective-permute-done.10.refs_1_
  58.4 8.4 %collective-permute-done.2.refs_0_ = bf16[3072,128]{1,0:T(8,128)(2,1)S(1)} collective-permute-done((bf16[3072,128]{1,0:T(8,128)(2,1)S(1)}, bf16[3072,128]{1,0:T(8,128)(2,1)S(1)}, u32[]{:S(2)}, u32[]{:S(2)}) %collective-permute-start.2) | collective-permute-done | bytes 786464 | tf_op jit(solution)/shard_map/ppermute | solution.py:365
  66.8 0.7 collective-permute-start.14
  67.4 0.7 collective-permute-start.13
  68.8 0.7 collective-permute-start.17
  69.5 0.8 shard_map.67.refs_3_
  71.0 0.7 collective-permute-start.16
  71.7 0.8 shard_map.69
  72.5 0.7 collective-permute-start.15
  73.8 0.7 collective-permute-start.20
  75.2 1.3 %collective-permute-start.19 = (bf16[48,2048]{1,0:T(8,128)(2,1)S(1)}, bf16[48,2048]{1,0:T(8,128)(2,1)S(1)}, u32[]{:S(2)}, u32[]{:S(2)}) collective-permute-start(bf16[48,2048]{1,0:T(8,128)(2,1)S(1)} %get-tuple-element.119.refs_5_), channel_id=1, source_target_pairs={{0,4},{4,8},{8,12},{1,5},{5,9},{9,13},{2,6},{6,10},{10,14},{3,7},{... | collective-permute-start | bytes 589832 | tf_op jit(solution)/shard_map/ppermute | solution.py:464
  77.1 1.3 %collective-permute-start.18 = (bf16[48,2048]{1,0:T(8,128)(2,1)S(1)}, bf16[48,2048]{1,0:T(8,128)(2,1)S(1)}, u32[]{:S(2)}, u32[]{:S(2)}) collective-permute-start(bf16[48,2048]{1,0:T(8,128)(2,1)S(1)} %get-tuple-element.123.refs_5_), channel_id=1, source_target_pairs={{0,4},{4,8},{8,12},{1,5},{5,9},{9,13},{2,6},{6,10},{10,14},{3,7},{... | collective-permute-start | bytes 589832 | tf_op jit(solution)/shard_map/ppermute | solution.py:464
  79.1 1.3 %collective-permute-start.23 = (bf16[48,2048]{1,0:T(8,128)(2,1)S(1)}, bf16[48,2048]{1,0:T(8,128)(2,1)S(1)}, u32[]{:S(2)}, u32[]{:S(2)}) collective-permute-start(bf16[48,2048]{1,0:T(8,128)(2,1)S(1)} %get-tuple-element.127.refs_5_), channel_id=1, source_target_pairs={{4,8},{8,12},{5,9},{9,13},{6,10},{10,14},{7,11},{11,15},{20,24},{2... | collective-permute-start | bytes 589832 | tf_op jit(solution)/shard_map/ppermute | solution.py:464
  80.4 12.6 %collective-permute-done.19.refs_4_ = bf16[48,2048]{1,0:T(8,128)(2,1)S(1)} collective-permute-done((bf16[48,2048]{1,0:T(8,128)(2,1)S(1)}, bf16[48,2048]{1,0:T(8,128)(2,1)S(1)}, u32[]{:S(2)}, u32[]{:S(2)}) %collective-permute-start.19) | collective-permute-done | bytes 196640 | tf_op jit(solution)/shard_map/ppermute | solution.py:464
  93.0 2.7 %shard_map.74 = (bf16[48,2048]{1,0:T(8,128)(2,1)S(1)}, f32[48,128]{1,0:T(8,128)S(1)}, bf16[384,2048]{1,0:T(8,128)(2,1)}, f32[384,128]{1,0:T(8,128)S(1)}) custom-call(s32[16]{0:T(128)S(1)} %get-tuple-element.164.refs_4_.right_ref, bf16[384,2048]{1,0:T(8,128)(2,1)S(1)} %copy-done, ...), custom_call_target="tpu_custom_call", output_to_operand_aliasing={{2}: (8, {}), {3}: (9, {})} | custom-call | flops 1610612736 | bytes 8388608 | tf_op jit(solution)/shard_map/pallas_call | solution.py:315
  95.7 1.3 %collective-permute-start.22 = (bf16[48,2048]{1,0:T(8,128)(2,1)S(1)}, bf16[48,2048]{1,0:T(8,128)(2,1)S(1)}, u32[]{:S(2)}, u32[]{:S(2)}) collective-permute-start(bf16[48,2048]{1,0:T(8,128)(2,1)S(1)} %get-tuple-element.131.refs_5_), channel_id=1, source_target_pairs={{4,8},{8,12},{5,9},{9,13},{6,10},{10,14},{7,11},{11,15},{20,24},{2... | collective-permute-start | bytes 589832 | tf_op jit(solution)/shard_map/ppermute | solution.py:464
  97.0 0.9 collective-permute-done.18.refs_4_
  97.8 2.7 %shard_map.75 = (bf16[48,2048]{1,0:T(8,128)(2,1)S(1)}, f32[48,128]{1,0:T(8,128)S(1)}, bf16[384,2048]{1,0:T(8,128)(2,1)}, f32[384,128]{1,0:T(8,128)S(1)}) custom-call(s32[16]{0:T(128)S(1)} %get-tuple-element.164.refs_4_.right_ref, bf16[384,2048]{1,0:T(8,128)(2,1)S(1)} %copy-done, ...), custom_call_target="tpu_custom_call", output_to_operand_aliasing={{2}: (8, {}), {3}: (9, {})} | custom-call | flops 1610612736 | bytes 8388608 | tf_op jit(solution)/shard_map/pallas_call | solution.py:315
  100.5 1.3 %collective-permute-start.21 = (bf16[48,2048]{1,0:T(8,128)(2,1)S(1)}, bf16[48,2048]{1,0:T(8,128)(2,1)S(1)}, u32[]{:S(2)}, u32[]{:S(2)}) collective-permute-start(bf16[48,2048]{1,0:T(8,128)(2,1)S(1)} %get-tuple-element.135.refs_5_), channel_id=1, source_target_pairs={{4,8},{8,12},{5,9},{9,13},{6,10},{10,14},{7,11},{11,15},{20,24},{2... | collective-permute-start | bytes 589832 | tf_op jit(solution)/shard_map/ppermute | solution.py:464
  101.8 0.7 collective-permute-done.23.refs_4_
  102.5 2.9 %shard_map.76 = (bf16[48,2048]{1,0:T(8,128)(2,1)S(1)}, f32[48,128]{1,0:T(8,128)S(1)}, bf16[384,2048]{1,0:T(8,128)(2,1)}, f32[384,128]{1,0:T(8,128)S(1)}) custom-call(s32[16]{0:T(128)S(1)} %get-tuple-element.164.refs_4_.right_ref, bf16[384,2048]{1,0:T(8,128)(2,1)S(1)} %copy-done, ...), custom_call_target="tpu_custom_call", output_to_operand_aliasing={{2}: (8, {}), {3}: (9, {})} | custom-call | flops 1610612736 | bytes 8388608 | tf_op jit(solution)/shard_map/pallas_call | solution.py:315
  105.4 1.3 %collective-permute-start.26 = (bf16[48,2048]{1,0:T(8,128)(2,1)S(1)}, bf16[48,2048]{1,0:T(8,128)(2,1)S(1)}, u32[]{:S(2)}, u32[]{:S(2)}) collective-permute-start(bf16[48,2048]{1,0:T(8,128)(2,1)S(1)} %get-tuple-element.139.refs_5_), channel_id=1, source_target_pairs={{8,12},{9,13},{10,14},{11,15},{24,28},{25,29},{26,30},{27,31}} | collective-permute-start | bytes 589832 | tf_op jit(solution)/shard_map/ppermute | solution.py:464
  107.2 2.7 %shard_map.77 = (bf16[48,2048]{1,0:T(8,128)(2,1)S(1)}, f32[48,128]{1,0:T(8,128)S(1)}, bf16[384,2048]{1,0:T(8,128)(2,1)}, f32[384,128]{1,0:T(8,128)S(1)}) custom-call(s32[16]{0:T(128)S(1)} %get-tuple-element.164.refs_4_.right_ref, bf16[384,2048]{1,0:T(8,128)(2,1)S(1)} %copy-done, ...), custom_call_target="tpu_custom_call", output_to_operand_aliasing={{2}: (8, {}), {3}: (9, {})} | custom-call | flops 1610612736 | bytes 8388608 | tf_op jit(solution)/shard_map/pallas_call | solution.py:315
  109.9 1.3 %collective-permute-start.25 = (bf16[48,2048]{1,0:T(8,128)(2,1)S(1)}, bf16[48,2048]{1,0:T(8,128)(2,1)S(1)}, u32[]{:S(2)}, u32[]{:S(2)}) collective-permute-start(bf16[48,2048]{1,0:T(8,128)(2,1)S(1)} %get-tuple-element.143.refs_5_), channel_id=1, source_target_pairs={{8,12},{9,13},{10,14},{11,15},{24,28},{25,29},{26,30},{27,31}} | collective-permute-start | bytes 589832 | tf_op jit(solution)/shard_map/ppermute | solution.py:464
  111.8 2.7 %shard_map.78 = (bf16[48,2048]{1,0:T(8,128)(2,1)S(1)}, f32[48,128]{1,0:T(8,128)S(1)}, bf16[384,2048]{1,0:T(8,128)(2,1)}, f32[384,128]{1,0:T(8,128)S(1)}) custom-call(s32[16]{0:T(128)S(1)} %get-tuple-element.164.refs_4_.right_ref, bf16[384,2048]{1,0:T(8,128)(2,1)S(1)} %copy-done, ...), custom_call_target="tpu_custom_call", output_to_operand_aliasing={{2}: (8, {}), {3}: (9, {})} | custom-call | flops 1610612736 | bytes 8388608 | tf_op jit(solution)/shard_map/pallas_call | solution.py:315
  114.5 1.3 %collective-permute-start.24 = (bf16[48,2048]{1,0:T(8,128)(2,1)S(1)}, bf16[48,2048]{1,0:T(8,128)(2,1)S(1)}, u32[]{:S(2)}, u32[]{:S(2)}) collective-permute-start(bf16[48,2048]{1,0:T(8,128)(2,1)S(1)} %get-tuple-element.147.refs_5_), channel_id=1, source_target_pairs={{8,12},{9,13},{10,14},{11,15},{24,28},{25,29},{26,30},{27,31}} | collective-permute-start | bytes 589832 | tf_op jit(solution)/shard_map/ppermute | solution.py:464
  116.2 2.7 %shard_map.79 = (bf16[48,2048]{1,0:T(8,128)(2,1)S(1)}, f32[48,128]{1,0:T(8,128)S(1)}, bf16[384,2048]{1,0:T(8,128)(2,1)}, f32[384,128]{1,0:T(8,128)S(1)}) custom-call(s32[16]{0:T(128)S(1)} %get-tuple-element.164.refs_4_.right_ref, bf16[384,2048]{1,0:T(8,128)(2,1)S(1)} %copy-done, ...), custom_call_target="tpu_custom_call", output_to_operand_aliasing={{2}: (8, {}), {3}: (9, {})} | custom-call | flops 1610612736 | bytes 8388608 | tf_op jit(solution)/shard_map/pallas_call | solution.py:315
  118.9 1.4 %collective-permute-done.25.refs_4_ = bf16[48,2048]{1,0:T(8,128)(2,1)S(1)} collective-permute-done((bf16[48,2048]{1,0:T(8,128)(2,1)S(1)}, bf16[48,2048]{1,0:T(8,128)(2,1)S(1)}, u32[]{:S(2)}, u32[]{:S(2)}) %collective-permute-start.25) | collective-permute-done | bytes 196640 | tf_op jit(solution)/shard_map/ppermute | solution.py:464
  120.4 2.7 %shard_map.80 = (bf16[48,2048]{1,0:T(8,128)(2,1)S(1)}, f32[48,128]{1,0:T(8,128)S(1)}, bf16[384,2048]{1,0:T(8,128)(2,1)}, f32[384,128]{1,0:T(8,128)S(1)}) custom-call(s32[16]{0:T(128)S(1)} %get-tuple-element.164.refs_4_.right_ref, bf16[384,2048]{1,0:T(8,128)(2,1)S(1)} %copy-done, ...), custom_call_target="tpu_custom_call", output_to_operand_aliasing={{2}: (8, {}), {3}: (9, {})} | custom-call | flops 1610612736 | bytes 8388608 | tf_op jit(solution)/shard_map/pallas_call | solution.py:315
  123.1 1.4 %collective-permute-done.24.refs_4_ = bf16[48,2048]{1,0:T(8,128)(2,1)S(1)} collective-permute-done((bf16[48,2048]{1,0:T(8,128)(2,1)S(1)}, bf16[48,2048]{1,0:T(8,128)(2,1)S(1)}, u32[]{:S(2)}, u32[]{:S(2)}) %collective-permute-start.24) | collective-permute-done | bytes 196640 | tf_op jit(solution)/shard_map/ppermute | solution.py:464
  124.5 3.4 %shard_map.81 = (bf16[384,2048]{1,0:T(8,128)(2,1)}, f32[384,128]{1,0:T(8,128)S(1)}) custom-call(s32[16]{0:T(128)S(1)} %get-tuple-element.164.refs_4_.right_ref, bf16[384,2048]{1,0:T(8,128)(2,1)S(1)} %copy-done, s32[384,1]{1,0:T(8,128)S(1)} %copy.76.refs_2_.refs_1_, s32[1,2048]{1,0:T(1,128)S(1)} %bitcast.26, ...), custom_call_target="tpu_custom_call", output_to_operand_aliasing={{0}: (8, {}), {1}: (9, {})} | custom-call | flops 1610612736 | bytes 8388608 | tf_op jit(solution)/shard_map/pallas_call | solution.py:315
  (54 shorter events, 10.5 us)
Async XLA Ops:
  0.6 2.2 %copy-start.1 = (bf16[1,2048,2,512]{3,2,1,0:T(2,128)(2,1)S(1)}, bf16[1,2048,2,512]{3,2,1,0:T(2,128)(2,1)}, u32[]{:S(2)}) copy-start(bf16[1,2048,2,512]{3,2,1,0:T(2,128)(2,1)} %tensor_ref.1) | copy-start | bytes 12582916
  2.8 0.7 copy-start.2
  3.5 8.9 %copy-start.3 = (s32[5,16]{1,0:T(8,128)S(1)}, s32[5,16]{1,0:T(8,128)}, u32[]{:S(2)}) copy-start(s32[5,16]{1,0:T(8,128)} %charge_ref.3) | copy-start | bytes 964
  3.5 12.0 %copy-start.8 = (s32[1,384]{1,0:T(1,128)S(1)}, s32[1,384]{1,0:T(1,128)}, u32[]{:S(2)}) copy-start(s32[1,384]{1,0:T(1,128)} %param.8) | copy-start | bytes 4612
  6.5 0.9 copy-start.4
  7.4 0.8 copy-start.6
  8.2 8.8 %collective-permute-start.7 = (bf16[8320,128]{1,0:T(8,128)(2,1)S(1)}, bf16[8320,128]{1,0:T(8,128)(2,1)}, u32[]{:S(2)}, u32[]{:S(2)}) collective-permute-start(bf16[8320,128]{1,0:T(8,128)(2,1)S(1)} %get-tuple-element.86.refs_0_), channel_id=1, source_target_pairs={{0,1},{1,0},{2,3},{3,2},{4,5},{5,4},{6,7},{7,6},{8,9},{9,8},{10,11... | collective-permute-start | bytes 6389768 | tf_op jit(solution)/shard_map/ppermute | solution.py:376
  8.2 20.2 %collective-permute-start.6 = (bf16[3072,128]{1,0:T(8,128)(2,1)}, bf16[3072,128]{1,0:T(8,128)(2,1)S(1)}, u32[]{:S(2)}, u32[]{:S(2)}) collective-permute-start(bf16[3072,128]{1,0:T(8,128)(2,1)} %get-tuple-element.85), channel_id=1, source_target_pairs={{0,2},{1,3},{2,0},{3,1},{4,6},{5,7},{6,4},{7,5},{8,10},{9,11},{10,... | collective-permute-start | bytes 2359304 | tf_op jit(solution)/shard_map/ppermute | solution.py:365
  10.8 4.8 %collective-permute-start.8 = (s32[1]{0:T(128)}, s32[1]{0:T(128)}, u32[]{:S(2)}, u32[]{:S(2)}) collective-permute-start(s32[1]{0:T(128)} %bitcast.4), channel_id=1, source_target_pairs={{0,16},{16,0},{1,17},{17,1},{2,18},{18,2},{3,19},{19,3},{4,20},{20... | collective-permute-start | bytes 20 | tf_op jit(solution)/shard_map/ppermute | solution.py:400
  17.1 11.3 %copy-start.7 = (bf16[1536,128]{1,0:T(8,128)(2,1)S(1)}, bf16[1536,128]{1,0:T(8,128)(2,1)}, u32[]{:S(2)}) copy-start(bf16[1536,128]{1,0:T(8,128)(2,1)} %copy-done.6) | copy-start | bytes 1179652
  17.1 28.9 %copy-start.5 = (bf16[3072,128]{1,0:T(8,128)(2,1)S(1)}, bf16[3072,128]{1,0:T(8,128)(2,1)}, u32[]{:S(2)}) copy-start(bf16[3072,128]{1,0:T(8,128)(2,1)} %copy-done.4) | copy-start | bytes 2359300
  28.3 20.8 %collective-permute-start.9 = (bf16[3072,128]{1,0:T(8,128)(2,1)S(1)}, bf16[3072,128]{1,0:T(8,128)(2,1)S(1)}, u32[]{:S(2)}, u32[]{:S(2)}) collective-permute-start(bf16[3072,128]{1,0:T(8,128)(2,1)S(1)} %collective-permute-done.6.refs_0_), channel_id=1, source_target_pairs={{0,1},{1,0},{2,3},{3,2},{4,5},{5,4},{6,7},{7,6},{8,9},{9,8},{10,11... | collective-permute-start | bytes 2359304 | tf_op jit(solution)/shard_map/ppermute | solution.py:376
  28.3 16.1 %collective-permute-start.4 = (bf16[1536,128]{1,0:T(8,128)(2,1)S(1)}, bf16[1536,128]{1,0:T(8,128)(2,1)S(1)}, u32[]{:S(2)}, u32[]{:S(2)}) collective-permute-start(bf16[1536,128]{1,0:T(8,128)(2,1)S(1)} %copy-done.7), channel_id=1, source_target_pairs={{0,14},{1,15},{2,12},{3,13},{16,30},{17,31},{18,28},{19,29}} | collective-permute-start | bytes 1179656 | tf_op jit(solution)/shard_map/ppermute | solution.py:365
  29.6 20.8 %collective-permute-start.3 = (bf16[1536,128]{1,0:T(8,128)(2,1)S(1)}, bf16[1536,128]{1,0:T(8,128)(2,1)S(1)}, u32[]{:S(2)}, u32[]{:S(2)}) collective-permute-start(bf16[1536,128]{1,0:T(8,128)(2,1)S(1)} %get-tuple-element.83), channel_id=1, source_target_pairs={{0,2},{1,3},{2,0},{3,1},{16,18},{17,19},{18,16},{19,17}} | collective-permute-start | bytes 1179656 | tf_op jit(solution)/shard_map/ppermute | solution.py:365
  44.4 9.7 %collective-permute-start.5 = (bf16[1536,128]{1,0:T(8,128)(2,1)S(1)}, bf16[1536,128]{1,0:T(8,128)(2,1)S(1)}, u32[]{:S(2)}, u32[]{:S(2)}) collective-permute-start(bf16[1536,128]{1,0:T(8,128)(2,1)S(1)} %collective-permute-done.4), channel_id=1, source_target_pairs={{12,0},{13,1},{14,2},{15,3},{28,16},{29,17},{30,18},{31,19}} | collective-permute-start | bytes 1179656 | tf_op jit(solution)/shard_map/ppermute | solution.py:365
  46.0 20.8 %collective-permute-start.2 = (bf16[3072,128]{1,0:T(8,128)(2,1)S(1)}, bf16[3072,128]{1,0:T(8,128)(2,1)S(1)}, u32[]{:S(2)}, u32[]{:S(2)}) collective-permute-start(bf16[3072,128]{1,0:T(8,128)(2,1)S(1)} %copy-done.5), channel_id=1, source_target_pairs={{4,6},{5,7},{6,4},{7,5},{8,10},{9,11},{10,8},{11,9},{12,14},{13,15... | collective-permute-start | bytes 2359304 | tf_op jit(solution)/shard_map/ppermute | solution.py:365
  50.4 6.7 %copy-start = (bf16[384,2048]{1,0:T(8,128)(2,1)S(1)}, bf16[384,2048]{1,0:T(8,128)(2,1)}, u32[]{:S(2)}) copy-start(bf16[384,2048]{1,0:T(8,128)(2,1)} %refs_0_.33) | copy-start | bytes 4718596
  54.2 1.7 %collective-permute-start.10 = (bf16[1536,128]{1,0:T(8,128)(2,1)S(1)}, bf16[1536,128]{1,0:T(8,128)(2,1)S(1)}, u32[]{:S(2)}, u32[]{:S(2)}) collective-permute-start(bf16[1536,128]{1,0:T(8,128)(2,1)S(1)} %collective-permute-done.5.refs_0_), channel_id=1, source_target_pairs={{0,1},{1,0},{2,3},{3,2},{4,5},{5,4},{6,7},{7,6},{8,9},{9,8},{10,11... | collective-permute-start | bytes 1179656 | tf_op jit(solution)/shard_map/ppermute | solution.py:376
  54.2 2.3 %collective-permute-start.11 = (bf16[1536,128]{1,0:T(8,128)(2,1)S(1)}, bf16[1536,128]{1,0:T(8,128)(2,1)S(1)}, u32[]{:S(2)}, u32[]{:S(2)}) collective-permute-start(bf16[1536,128]{1,0:T(8,128)(2,1)S(1)} %collective-permute-done.3.refs_2_), channel_id=1, source_target_pairs={{0,1},{1,0},{2,3},{3,2},{4,5},{5,4},{6,7},{7,6},{8,9},{9,8},{10,11... | collective-permute-start | bytes 1179656 | tf_op jit(solution)/shard_map/ppermute | solution.py:376
  66.8 2.7 %collective-permute-start.12 = (bf16[3072,128]{1,0:T(8,128)(2,1)S(1)}, bf16[3072,128]{1,0:T(8,128)(2,1)S(1)}, u32[]{:S(2)}, u32[]{:S(2)}) collective-permute-start(bf16[3072,128]{1,0:T(8,128)(2,1)S(1)} %collective-permute-done.2.refs_0_), channel_id=1, source_target_pairs={{0,1},{1,0},{2,3},{3,2},{4,5},{5,4},{6,7},{7,6},{8,9},{9,8},{10,11... | collective-permute-start | bytes 2359304 | tf_op jit(solution)/shard_map/ppermute | solution.py:376
  66.8 3.5 %collective-permute-start.14 = (bf16[48,2048]{1,0:T(8,128)(2,1)S(1)}, bf16[48,2048]{1,0:T(8,128)(2,1)S(1)}, u32[]{:S(2)}, u32[]{:S(2)}) collective-permute-start(bf16[48,2048]{1,0:T(8,128)(2,1)S(1)} %get-tuple-element.94.refs_4_), channel_id=1, source_target_pairs={{0,4},{1,5},{2,6},{3,7},{16,20},{17,21},{18,22},{19,23}} | collective-permute-start | bytes 589832 | tf_op jit(solution)/shard_map/ppermute | solution.py:464
  67.4 4.2 %collective-permute-start.13 = (bf16[48,2048]{1,0:T(8,128)(2,1)S(1)}, bf16[48,2048]{1,0:T(8,128)(2,1)S(1)}, u32[]{:S(2)}, u32[]{:S(2)}) collective-permute-start(bf16[48,2048]{1,0:T(8,128)(2,1)S(1)} %get-tuple-element.98.refs_4_), channel_id=1, source_target_pairs={{0,4},{1,5},{2,6},{3,7},{16,20},{17,21},{18,22},{19,23}} | collective-permute-start | bytes 589832 | tf_op jit(solution)/shard_map/ppermute | solution.py:464
  68.8 4.4 %collective-permute-start.17 = (bf16[48,2048]{1,0:T(8,128)(2,1)S(1)}, bf16[48,2048]{1,0:T(8,128)(2,1)S(1)}, u32[]{:S(2)}, u32[]{:S(2)}) collective-permute-start(bf16[48,2048]{1,0:T(8,128)(2,1)S(1)} %get-tuple-element.103.refs_2_.refs_5_), channel_id=1, source_target_pairs={{0,4},{1,5},{2,6},{3,7},{16,20},{17,21},{18,22},{19,23}} | collective-permute-start | bytes 589832 | tf_op jit(solution)/shard_map/ppermute | solution.py:464
  71.0 3.5 %collective-permute-start.16 = (bf16[48,2048]{1,0:T(8,128)(2,1)S(1)}, bf16[48,2048]{1,0:T(8,128)(2,1)S(1)}, u32[]{:S(2)}, u32[]{:S(2)}) collective-permute-start(bf16[48,2048]{1,0:T(8,128)(2,1)S(1)} %get-tuple-element.107.refs_5_), channel_id=1, source_target_pairs={{0,4},{4,8},{1,5},{5,9},{2,6},{6,10},{3,7},{7,11},{16,20},{20,24},... | collective-permute-start | bytes 589832 | tf_op jit(solution)/shard_map/ppermute | solution.py:464
  72.5 4.0 %collective-permute-start.15 = (bf16[48,2048]{1,0:T(8,128)(2,1)S(1)}, bf16[48,2048]{1,0:T(8,128)(2,1)S(1)}, u32[]{:S(2)}, u32[]{:S(2)}) collective-permute-start(bf16[48,2048]{1,0:T(8,128)(2,1)S(1)} %get-tuple-element.111.refs_5_), channel_id=1, source_target_pairs={{0,4},{4,8},{1,5},{5,9},{2,6},{6,10},{3,7},{7,11},{16,20},{20,24},... | collective-permute-start | bytes 589832 | tf_op jit(solution)/shard_map/ppermute | solution.py:464
  73.8 4.6 %collective-permute-start.20 = (bf16[48,2048]{1,0:T(8,128)(2,1)S(1)}, bf16[48,2048]{1,0:T(8,128)(2,1)S(1)}, u32[]{:S(2)}, u32[]{:S(2)}) collective-permute-start(bf16[48,2048]{1,0:T(8,128)(2,1)S(1)} %get-tuple-element.115.refs_5_), channel_id=1, source_target_pairs={{0,4},{4,8},{1,5},{5,9},{2,6},{6,10},{3,7},{7,11},{16,20},{20,24},... | collective-permute-start | bytes 589832 | tf_op jit(solution)/shard_map/ppermute | solution.py:464
  75.2 17.8 %collective-permute-start.19 = (bf16[48,2048]{1,0:T(8,128)(2,1)S(1)}, bf16[48,2048]{1,0:T(8,128)(2,1)S(1)}, u32[]{:S(2)}, u32[]{:S(2)}) collective-permute-start(bf16[48,2048]{1,0:T(8,128)(2,1)S(1)} %get-tuple-element.119.refs_5_), channel_id=1, source_target_pairs={{0,4},{4,8},{8,12},{1,5},{5,9},{9,13},{2,6},{6,10},{10,14},{3,7},{... | collective-permute-start | bytes 589832 | tf_op jit(solution)/shard_map/ppermute | solution.py:464
  77.1 20.7 %collective-permute-start.18 = (bf16[48,2048]{1,0:T(8,128)(2,1)S(1)}, bf16[48,2048]{1,0:T(8,128)(2,1)S(1)}, u32[]{:S(2)}, u32[]{:S(2)}) collective-permute-start(bf16[48,2048]{1,0:T(8,128)(2,1)S(1)} %get-tuple-element.123.refs_5_), channel_id=1, source_target_pairs={{0,4},{4,8},{8,12},{1,5},{5,9},{9,13},{2,6},{6,10},{10,14},{3,7},{... | collective-permute-start | bytes 589832 | tf_op jit(solution)/shard_map/ppermute | solution.py:464
  79.1 23.4 %collective-permute-start.23 = (bf16[48,2048]{1,0:T(8,128)(2,1)S(1)}, bf16[48,2048]{1,0:T(8,128)(2,1)S(1)}, u32[]{:S(2)}, u32[]{:S(2)}) collective-permute-start(bf16[48,2048]{1,0:T(8,128)(2,1)S(1)} %get-tuple-element.127.refs_5_), channel_id=1, source_target_pairs={{4,8},{8,12},{5,9},{9,13},{6,10},{10,14},{7,11},{11,15},{20,24},{2... | collective-permute-start | bytes 589832 | tf_op jit(solution)/shard_map/ppermute | solution.py:464
  95.7 11.5 %collective-permute-start.22 = (bf16[48,2048]{1,0:T(8,128)(2,1)S(1)}, bf16[48,2048]{1,0:T(8,128)(2,1)S(1)}, u32[]{:S(2)}, u32[]{:S(2)}) collective-permute-start(bf16[48,2048]{1,0:T(8,128)(2,1)S(1)} %get-tuple-element.131.refs_5_), channel_id=1, source_target_pairs={{4,8},{8,12},{5,9},{9,13},{6,10},{10,14},{7,11},{11,15},{20,24},{2... | collective-permute-start | bytes 589832 | tf_op jit(solution)/shard_map/ppermute | solution.py:464
  100.5 11.3 %collective-permute-start.21 = (bf16[48,2048]{1,0:T(8,128)(2,1)S(1)}, bf16[48,2048]{1,0:T(8,128)(2,1)S(1)}, u32[]{:S(2)}, u32[]{:S(2)}) collective-permute-start(bf16[48,2048]{1,0:T(8,128)(2,1)S(1)} %get-tuple-element.135.refs_5_), channel_id=1, source_target_pairs={{4,8},{8,12},{5,9},{9,13},{6,10},{10,14},{7,11},{11,15},{20,24},{2... | collective-permute-start | bytes 589832 | tf_op jit(solution)/shard_map/ppermute | solution.py:464
  105.4 10.8 %collective-permute-start.26 = (bf16[48,2048]{1,0:T(8,128)(2,1)S(1)}, bf16[48,2048]{1,0:T(8,128)(2,1)S(1)}, u32[]{:S(2)}, u32[]{:S(2)}) collective-permute-start(bf16[48,2048]{1,0:T(8,128)(2,1)S(1)} %get-tuple-element.139.refs_5_), channel_id=1, source_target_pairs={{8,12},{9,13},{10,14},{11,15},{24,28},{25,29},{26,30},{27,31}} | collective-permute-start | bytes 589832 | tf_op jit(solution)/shard_map/ppermute | solution.py:464
  109.9 10.5 %collective-permute-start.25 = (bf16[48,2048]{1,0:T(8,128)(2,1)S(1)}, bf16[48,2048]{1,0:T(8,128)(2,1)S(1)}, u32[]{:S(2)}, u32[]{:S(2)}) collective-permute-start(bf16[48,2048]{1,0:T(8,128)(2,1)S(1)} %get-tuple-element.143.refs_5_), channel_id=1, source_target_pairs={{8,12},{9,13},{10,14},{11,15},{24,28},{25,29},{26,30},{27,31}} | collective-permute-start | bytes 589832 | tf_op jit(solution)/shard_map/ppermute | solution.py:464
  114.5 10.0 %collective-permute-start.24 = (bf16[48,2048]{1,0:T(8,128)(2,1)S(1)}, bf16[48,2048]{1,0:T(8,128)(2,1)S(1)}, u32[]{:S(2)}, u32[]{:S(2)}) collective-permute-start(bf16[48,2048]{1,0:T(8,128)(2,1)S(1)} %get-tuple-element.147.refs_5_), channel_id=1, source_target_pairs={{8,12},{9,13},{10,14},{11,15},{24,28},{25,29},{26,30},{27,31}} | collective-permute-start | bytes 589832 | tf_op jit(solution)/shard_map/ppermute | solution.py:464
